TPU v7x, 256 devices: a whole 4x4x8 slice. The times are simulated.
256 devices in a mesh: row: 16 (over x, y_lo, core), col: 8 (over z), grp: 2 (over y_hi).
Axes of the slice: x: 4, y: 4 (y_hi: 2, y_lo: 2; y = y_hi * 2 + y_lo), z: 8, core: 2. Of those that a mesh axis runs over, the one named last changes fastest.
Arguments:
- patches: bfloat16 [2, 1024, 1408], P('grp', 'row', 'col'), may hold values from -6 to 6
- vis_gain: bfloat16 [1408], P('col'), may hold values from 0.25 to 1.75
- vis_bias: bfloat16 [1408], P('col'), may hold values from -3 to 3
- vis_qkv: bfloat16 [1408, 4224], P('col', 'row'), may hold values from -1 to 1
- vis_qkv_bias: bfloat16 [4224], P('row'), may hold values from -3 to 3
- vis_out: bfloat16 [1408, 1408], P('row', 'col'), may hold values from -0.15625 to 0.15625
- vis_out_bias: bfloat16 [1408], P('col'), may hold values from -3 to 3
- proj_weight: bfloat16 [4, 1408, 1408], P(None, 'col', 'row'), may hold values from -0.078125 to 0.078125
- proj_bias: bfloat16 [1408], P('row'), may hold values from -3 to 3
- text_embeds: bfloat16 [2, 4096, 1408], P('grp', 'col', 'row'), may hold values from -6 to 6
- dec_gain: bfloat16 [1408], P('row'), may hold values from 0.25 to 1.75
- dec_qkv: bfloat16 [1408, 4224], P('row', 'col'), may hold values from -1 to 1
- dec_out: bfloat16 [1408, 1408], P('col', 'row'), may hold values from -0.15625 to 0.15625
- image_tokens: int32 [2, 8], P('grp'), may hold values from 1 to 64, 256 in all within a row
- text_gaps: int32 [2, 9], P('grp'), may hold values from 1 to 1920, 3840 in all within a row
- doc_lengths: int32 [4], replicated, may hold values from 1 to 4096, 8192 in all
Outputs:
- hidden_out: bfloat16 [2, 4096, 1408], P('grp', 'col', 'row')
All inputs are finite; a program needn't handle non-finite values.
Results may differ from a plain program's by a relative error of at most 0.0045.
The roundings to bfloat16 on the way count: a program that leaves them out, or rounds other values in their place, can miss the bound.
Values may be sent and summed in bfloat16 or wider, within the bound.
No kernel may reach another device: no remote copies, remote signals or barrier semaphores. Data moves between devices by JAX's collectives and lax.ppermute only.
A program may use at most 64 MiB of HBM per device.

v0:
```python
import math

import jax
import jax.numpy as jnp
from jax import lax
from jax.sharding import PartitionSpec as P

HEADS = 16
HEAD_DIM = 88


def rows_over_col(values):
    return lax.all_gather(values, "col", axis=0, tiled=True)


def rows_over_row(values):
    return lax.all_gather(values, "row", axis=0, tiled=True)


def sums_over_col(term_fn, count):
    return lax.psum_scatter(
        term_fn(jnp.int32(0), lax.axis_size("col") * count), "col", scatter_dimension=0, tiled=True
    )


def segment_of(index_values, lengths):
    ends = jnp.cumsum(lengths, dtype=jnp.int32)
    return jnp.sum(
        (index_values[:, None] >= ends[None, :]).astype(jnp.int32), axis=1, dtype=jnp.int32
    )


def insert_map(text_rows, image_lengths, gaps):
    offsets = jnp.cumsum(image_lengths, dtype=jnp.int32) - image_lengths
    starts = jnp.cumsum(gaps, dtype=jnp.int32)[: image_lengths.shape[0]] + offsets
    inside = (text_rows[:, None] >= starts[None, :]) & (
        text_rows[:, None] < (starts + image_lengths)[None, :]
    )
    source = jnp.sum(
        jnp.where(inside, offsets[None, :] + text_rows[:, None] - starts[None, :], 0),
        axis=1,
        dtype=jnp.int32,
    )
    return (source, jnp.any(inside, axis=1))


def product_rows(left, right):

    def term(start, count):
        return jnp.dot(left, right, preferred_element_type=jnp.float32)

    return term


def empty_state(heads, rows):
    return (
        jnp.full((heads, rows), -1e30, jnp.float32),
        jnp.zeros((heads, rows), jnp.float32),
        jnp.zeros((rows, heads, HEAD_DIM), jnp.float32),
    )


def online_block(carry, query, keys, values, usable, scale):
    best, norm_sum, accum = carry
    piece_scores = (
        jnp.einsum("qhe,khe->hqk", query, keys, preferred_element_type=jnp.float32) * scale
    )
    piece_scores = jnp.where(usable, piece_scores, -1e30)
    new_best = jnp.maximum(best, jnp.max(piece_scores, axis=2))
    piece_weights = jnp.where(usable, jnp.exp(piece_scores - new_best[:, :, None]), 0.0)
    factor = jnp.exp(best - new_best)
    norm_sum = norm_sum * factor + jnp.sum(piece_weights, axis=2)
    added = jnp.einsum(
        "hqk,khe->qhe",
        piece_weights.astype(jnp.bfloat16),
        values,
        preferred_element_type=jnp.float32,
    )
    accum = accum * jnp.transpose(factor)[:, :, None] + added
    return (new_best, norm_sum, accum)


def fold_keys(carry, query, keyval, key_marks, mask_of, scale):
    count = keyval.shape[0]
    heads = query.shape[1]
    block = math.gcd(count, 512)
    blocks = count // block
    shaped = keyval.reshape(blocks, block, heads, 2, HEAD_DIM)
    marks = key_marks.reshape(blocks, block)

    def advance(state, inputs):
        piece, piece_marks = inputs
        return (
            online_block(state, query, piece[:, :, 0], piece[:, :, 1], mask_of(piece_marks), scale),
            None,
        )

    carry, unused = lax.scan(advance, carry, (shaped, marks))
    return carry


def per_device(
    patches,
    vis_gain,
    vis_bias,
    vis_qkv,
    vis_qkv_bias,
    vis_out,
    vis_out_bias,
    proj_weight,
    proj_bias,
    text_embeds,
    dec_gain,
    dec_qkv,
    dec_out,
    image_tokens,
    text_gaps,
    doc_lengths,
):
    width = HEADS * HEAD_DIM
    scale = HEAD_DIM ** (-0.5)
    col_count = lax.axis_size("col")
    row_count = lax.axis_size("row")
    image_lengths = image_tokens[0]
    gaps = text_gaps[0]
    xfull = patches[0].astype(jnp.float32)
    rows_b = xfull.shape[0]
    sum_one, sum_two = lax.psum((jnp.sum(xfull, axis=1), jnp.sum(xfull * xfull, axis=1)), "col")
    mean = sum_one[:, None] / width
    variance = sum_two[:, None] / width - mean * mean
    normed = (
        (xfull - mean) * lax.rsqrt(variance + 1e-06) * vis_gain.astype(jnp.float32)
        + vis_bias.astype(jnp.float32)
    ).astype(jnp.bfloat16)
    gathered = rows_over_row(normed)
    patch_total = gathered.shape[0]
    rows_a = patch_total // col_count
    qkv_rows = (
        sums_over_col(product_rows(gathered, vis_qkv), rows_a) + vis_qkv_bias.astype(jnp.float32)
    ).astype(jnp.bfloat16)
    heads_row = qkv_rows.shape[1] // (3 * HEAD_DIM)
    qkv_rows = qkv_rows.reshape(rows_a, heads_row, 3, HEAD_DIM)
    query = qkv_rows[:, :, 0]
    keyval = qkv_rows[:, :, 1:].reshape(rows_a, heads_row * 2 * HEAD_DIM)
    all_keyval = rows_over_col(keyval)
    first_row = lax.axis_index("col") * rows_a
    query_ids = segment_of((first_row + jnp.arange(rows_a, dtype=jnp.int32)) // 4, image_lengths)
    key_ids = segment_of(jnp.arange(patch_total, dtype=jnp.int32) // 4, image_lengths)

    def same_image(marks):
        return (query_ids[:, None] == marks[None, :])[None]

    best_vis, norm_vis, accum_vis = fold_keys(
        empty_state(heads_row, rows_a), query, all_keyval, key_ids, same_image, scale
    )
    vis_attn = (
        (accum_vis / jnp.transpose(norm_vis)[:, :, None])
        .astype(jnp.bfloat16)
        .reshape(rows_a, heads_row * HEAD_DIM)
    )
    all_attn = rows_over_col(vis_attn)
    delta = lax.psum_scatter(
        product_rows(all_attn, vis_out)(jnp.int32(0), lax.axis_size("row") * rows_b),
        "row",
        scatter_dimension=0,
        tiled=True,
    )
    resid = (xfull + delta + vis_out_bias.astype(jnp.float32)).astype(jnp.bfloat16)
    merged = resid.reshape(rows_b // 4, 4 * resid.shape[1])
    all_merged = rows_over_row(merged)
    partial_value = jnp.dot(
        all_merged,
        proj_weight.reshape(4 * proj_weight.shape[1], proj_weight.shape[2]),
        preferred_element_type=jnp.float32,
    )
    text = text_embeds[0]
    rows_text_a = text.shape[0]
    text_total = rows_text_a * col_count

    def place_term(start, count):
        source, inside = insert_map(jnp.arange(count, dtype=jnp.int32), image_lengths, gaps)
        return jnp.where(inside[:, None], jnp.take(partial_value, source, axis=0), 0.0)

    placed = sums_over_col(place_term, rows_text_a)
    own_rows = lax.axis_index("col") * rows_text_a + jnp.arange(rows_text_a, dtype=jnp.int32)
    unused, own_inside = insert_map(own_rows, image_lengths, gaps)
    dec_input = jnp.where(
        own_inside[:, None], placed + proj_bias.astype(jnp.float32), text.astype(jnp.float32)
    ).astype(jnp.bfloat16)
    xdec = dec_input.astype(jnp.float32)
    squares = lax.psum(jnp.sum(xdec * xdec, axis=1), "row")
    dec_normed = (
        xdec * lax.rsqrt(squares[:, None] / width + 1e-05) * dec_gain.astype(jnp.float32)
    ).astype(jnp.bfloat16)
    rows_text_b = text_total // row_count
    gathered_text = rows_over_col(dec_normed)
    dec_rows = lax.psum_scatter(
        product_rows(gathered_text, dec_qkv)(jnp.int32(0), lax.axis_size("row") * rows_text_b),
        "row",
        scatter_dimension=0,
        tiled=True,
    ).astype(jnp.bfloat16)
    heads_col = dec_rows.shape[1] // (3 * HEAD_DIM)
    dec_rows = dec_rows.reshape(rows_text_b, heads_col, 3, HEAD_DIM)
    dec_query = dec_rows[:, :, 0]
    dec_keyval = dec_rows[:, :, 1:].reshape(rows_text_b, heads_col * 2 * HEAD_DIM)
    half = lax.axis_index("grp")
    in_half = lax.axis_index("row") * rows_text_b + jnp.arange(rows_text_b, dtype=jnp.int32)
    query_pos = (
        in_half // rows_text_b * (2 * rows_text_b) + half * rows_text_b + in_half % rows_text_b
    )
    query_doc = segment_of(query_pos, doc_lengths)

    def causal_doc(key_pos):
        key_doc = segment_of(key_pos, doc_lengths)
        return (
            (key_doc[None, :] == query_doc[:, None]) & (key_pos[None, :] <= query_pos[:, None])
        )[None]

    start_state = empty_state(heads_col, rows_text_b)
    piece = lax.all_gather(dec_keyval, ("row", "grp"), axis=0, tiled=True)
    key_pos = jnp.arange(piece.shape[0], dtype=jnp.int32)
    best, norm_sum, accum = fold_keys(start_state, dec_query, piece, key_pos, causal_doc, scale)
    dec_attn = (
        (accum / jnp.transpose(norm_sum)[:, :, None])
        .astype(jnp.bfloat16)
        .reshape(rows_text_b, heads_col * HEAD_DIM)
    )
    all_dec_attn = rows_over_row(dec_attn)
    dec_delta = sums_over_col(product_rows(all_dec_attn, dec_out), rows_text_a)
    return (xdec + dec_delta).astype(jnp.bfloat16)[None]


def solution(mesh):
    return jax.shard_map(
        per_device,
        mesh=mesh,
        in_specs=(
            P("grp", "row", "col"),
            P("col"),
            P("col"),
            P("col", "row"),
            P("row"),
            P("row", "col"),
            P("col"),
            P(None, "col", "row"),
            P("row"),
            P("grp", "col", "row"),
            P("row"),
            P("row", "col"),
            P("col", "row"),
            P("grp", None),
            P("grp", None),
            P(),
        ),
        out_specs=P("grp", "col", "row"),
        check_vma=False,
    )
```

profile of v0, /device:TPU:1, one launch (start us, length us, event | category | flops | bytes accessed | tf_op | source)
XLA Modules:
  0.0 657.3 jit_solution(18280702815601827841)
XLA Ops:
  9.6 17.3 %all-reduce = (f32[64]{0:T(128)S(1)}, f32[64]{0:T(128)S(1)}) all-reduce(f32[64]{0:T(128)S(1)} %fusion.48, f32[64]{0:T(128)S(1)} %convert_reduce_fusion.1), channel_id=1, replica_groups=mesh['row'=16,'col'=8,'grp'=2] {'col'}, use_global_device_ids=true, to_apply=%region_8.9 | all-reduce | flops 128 | bytes 1024 | tf_op jit(solution)/shard_map/psum | solution.py:128
  27.8 25.2 %all_gather.21 = bf16[1024,176]{1,0:T(8,128)(2,1)S(1)} all-gather(bf16[64,176]{1,0:T(8,128)(2,1)S(1)} %fusion.47), channel_id=1, replica_groups=mesh['row'=16,'col'=8,'grp'=2] {'row'}, dimensions={0}, use_global_device_ids=true | all-gather | bytes 382976 | tf_op jit(solution)/shard_map/all_gather | solution.py:17
  53.0 2.3 fusion.61
  56.2 28.6 %reduce-scatter.6.cloned.1.call-done = f32[128,264]{0,1:T(8,128)} async-done(((f32[1024,264]{0,1:T(8,128)}), f32[128,264]{0,1:T(8,128)}) %reduce-scatter.6.cloned.1.call-update) | async-done | bytes 135184 | tf_op jit(solution)/shard_map/reduce_scatter | solution.py:21
  85.8 18.1 %all_gather.22 = bf16[1024,176]{0,1:T(8,128)(2,1)S(1)} all-gather(bf16[128,176]{0,1:T(8,128)(2,1)S(1)} %bitcast.195), channel_id=1, replica_groups=mesh['row'=16,'col'=8,'grp'=2] {'col'}, dimensions={0}, use_global_device_ids=true | all-gather | bytes 405504 | tf_op jit(solution)/shard_map/all_gather | solution.py:13
  104.2 1.6 while.32
  105.8 16.4 %all-gather = bf16[1024,1,88]{0,2,1:T(8,128)(2,1)S(1)} all-gather(bf16[128,1,88]{0,2,1:T(8,128)(2,1)S(1)} %divide_convert_fusion.1), channel_id=2, replica_groups=mesh['row'=16,'col'=8,'grp'=2] {'col'}, dimensions={0}, use_global_device_ids=true | all-gather | bytes 202752 | tf_op jit(solution)/shard_map/all_gather | solution.py:13
  122.2 1.3 fusion.36
  123.8 73.5 %reduce-scatter.8.cloned.1.call-done = f32[64,176]{1,0:T(8,128)} async-done(((f32[1024,176]{1,0:T(8,128)}), f32[64,176]{1,0:T(8,128)}) %reduce-scatter.8.cloned.1.call-update) | async-done | bytes 45072 | tf_op jit(solution)/shard_map/reduce_scatter | solution.py:162
  198.3 21.1 %all_gather.24 = bf16[256,704]{1,0:T(8,128)(2,1)S(1)} all-gather(bf16[16,704]{1,0:T(8,128)(2,1)S(1)} %reshape.288), channel_id=1, replica_groups=mesh['row'=16,'col'=8,'grp'=2] {'row'}, dimensions={0}, use_global_device_ids=true | all-gather | bytes 382976 | tf_op jit(solution)/shard_map/all_gather | solution.py:17
  219.6 10.8 %gather_fusion = f32[4096,88]{1,0:T(8,128)S(1)} fusion(f32[256,88]{1,0:T(8,128)S(1)} %fusion.62, s32[4096]{0:T(1024)S(1)} %broadcast_clamp_fusion), kind=kCustom, calls=%fused_computation | custom fusion | bytes 2899968 | tf_op jit(solution)/shard_map/jit(_take)/gather | solution.py:182
  230.4 1.7 copy.32
  232.2 2.6 select_select_fusion
  235.6 33.9 %reduce-scatter.10.cloned.1.call-done = f32[512,88]{0,1:T(8,128)} async-done(((f32[4096,88]{0,1:T(8,128)}), f32[512,88]{0,1:T(8,128)}) %reduce-scatter.10.cloned.1.call-update) | async-done | bytes 180240 | tf_op jit(solution)/shard_map/reduce_scatter | solution.py:21
  269.5 1.0 fusion.31
  270.5 31.1 %psum.23 = f32[512]{0:T(512)S(1)} all-reduce(f32[512]{0:T(512)S(1)} %get-tuple-element.318), channel_id=1, replica_groups=mesh['row'=16,'col'=8,'grp'=2] {'row'}, use_global_device_ids=true, to_apply=%region_19.20 | all-reduce | flops 512 | bytes 4096 | tf_op jit(solution)/shard_map/psum | solution.py:191
  301.7 19.8 %all_gather.25 = bf16[4096,88]{0,1:T(8,128)(2,1)S(1)} all-gather(bf16[512,88]{0,1:T(8,128)(2,1)S(1)} %fusion.33), channel_id=1, replica_groups=mesh['row'=16,'col'=8,'grp'=2] {'col'}, dimensions={0}, use_global_device_ids=true | all-gather | bytes 811008 | tf_op jit(solution)/shard_map/all_gather | solution.py:13
  321.5 4.6 fusion.63
  326.2 103.9 %reduce-scatter.12.cloned.1.call-done = f32[256,528]{0,1:T(8,128)} async-done(((f32[4096,528]{0,1:T(8,128)}), f32[256,528]{0,1:T(8,128)}) %reduce-scatter.12.cloned.1.call-update) | async-done | bytes 540688 | tf_op jit(solution)/shard_map/reduce_scatter | solution.py:197
  430.1 1.1 convert_element_type.103
  432.5 91.9 %all-gather.4.cloned.1.call-done = bf16[8192,352]{0,1:T(8,128)(2,1)} async-done(((bf16[256,352]{0,1:T(8,128)(2,1)}), bf16[8192,352]{0,1:T(8,128)(2,1)}) %all-gather.4.cloned.1.call-update) | async-done | bytes 5767184 | tf_op jit(solution)/shard_map/all_gather | solution.py:221
  524.4 5.3 copy.38
  529.6 5.8 copy.34
  535.4 37.7 %while.33 = (s32[]{:T(128)}, f32[2,256]{1,0:T(2,128)S(1)}, f32[2,256]{1,0:T(2,128)S(1)}, f32[256,2,88]{0,2,1:T(8,128)S(1)}, s32[16,512]{1,0:T(8,128)S(1)}, /*ind...) while((s32[]{:T(128)}, f32[2,256]{1,0:T(2,128)S(1)}, ...), condition=%wide.region_27.28_spmd.clone, body=%wide.region_23.27_spmd.clone.sunk | while | flops 95176960 | bytes 5250217 | solution.py:98
  535.7 1.0 dynamic-slice_bitcast_fusion.5
  542.8 1.0 dynamic-slice_bitcast_fusion.5
  545.2 1.0 dynamic-slice_bitcast_fusion.5
  552.2 1.0 dynamic-slice_bitcast_fusion.5
  573.9 36.3 %all-gather.6.cloned.1.call-done = bf16[4096,176]{0,1:T(8,128)(2,1)} async-done(((bf16[256,176]{0,1:T(8,128)(2,1)}), bf16[4096,176]{0,1:T(8,128)(2,1)}) %all-gather.6.cloned.1.call-update) | async-done | bytes 1441808 | tf_op jit(solution)/shard_map/all_gather | solution.py:17
  610.1 2.9 fusion.64
  613.0 35.8 %reduce-scatter.14.cloned.1.call-done = f32[512,88]{0,1:T(8,128)} async-done(((f32[4096,88]{0,1:T(8,128)}), f32[512,88]{0,1:T(8,128)}) %reduce-scatter.14.cloned.1.call-update) | async-done | bytes 180240 | tf_op jit(solution)/shard_map/reduce_scatter | solution.py:21
  648.9 1.6 fusion.40
  (277 shorter events, 44.5 us)
Async XLA Ops:
  6.5 212.8 %copy-start = (bf16[4,176,88]{2,1,0:T(8,128)(2,1)S(1)}, bf16[4,176,88]{2,1,0:T(8,128)(2,1)}, u32[]{:S(2)}) copy-start(bf16[4,176,88]{2,1,0:T(8,128)(2,1)} %param.27) | copy-start | bytes 371716
  6.5 78.2 %reduce-scatter.6.cloned.1.call-start = ((), (), s32[]{:S(2)}) async-start(), calls=%async_computation.5 | async-start | bytes 1216512 | tf_op jit(solution)/shard_map/reduce_scatter | solution.py:21
  53.0 2.4 copy-start.6
  53.0 2.4 copy-start.7
  53.0 2.7 copy-start.8
  53.0 2.8 copy-start.9
  55.3 142.0 %reduce-scatter.8.cloned.1.call-start = ((), (), s32[]{:S(2)}) async-start(), calls=%async_computation.6 | async-start | bytes 1114112 | tf_op jit(solution)/shard_map/reduce_scatter | solution.py:162
  104.2 18.1 %copy-start.4 = (bf16[88,176]{1,0:T(8,128)(2,1)S(1)}, bf16[88,176]{1,0:T(8,128)(2,1)}, u32[]{:S(2)}) copy-start(bf16[88,176]{1,0:T(8,128)(2,1)} %param.25) | copy-start | bytes 92932
  105.8 91.5 %copy-start.1 = (bf16[1,64,176]{2,1,0:T(8,128)(2,1)S(1)}, bf16[1,64,176]{2,1,0:T(8,128)(2,1)}, u32[]{:S(2)}) copy-start(bf16[1,64,176]{2,1,0:T(8,128)(2,1)} %param.20) | copy-start | bytes 67588
  123.6 145.9 %reduce-scatter.10.cloned.1.call-start = ((), (), s32[]{:S(2)}) async-start(), calls=%async_computation.7 | async-start | bytes 1622016 | tf_op jit(solution)/shard_map/reduce_scatter | solution.py:21
  234.8 0.7 copy-start.10
  234.8 0.7 copy-start.11
  234.8 34.7 %copy-start.3 = (bf16[1,512,88]{1,2,0:T(8,128)(2,1)S(1)}, bf16[1,512,88]{1,2,0:T(8,128)(2,1)}, u32[]{:S(2)}) copy-start(bf16[1,512,88]{1,2,0:T(8,128)(2,1)} %param.29) | copy-start | bytes 270340
  234.8 86.7 %copy-start.2 = (bf16[88,528]{1,0:T(8,128)(2,1)S(1)}, bf16[88,528]{1,0:T(8,128)(2,1)}, u32[]{:S(2)}) copy-start(bf16[88,528]{1,0:T(8,128)(2,1)} %param.31) | copy-start | bytes 278788
  234.8 195.2 %reduce-scatter.12.cloned.1.call-start = ((), (), s32[]{:S(2)}) async-start(), calls=%async_computation.8 | async-start | bytes 9191424 | tf_op jit(solution)/shard_map/reduce_scatter | solution.py:197
  326.1 106.0 %copy-start.12 = (s32[4]{0:T(128)S(1)}, s32[4]{0:T(128)}, u32[]{:S(2)}) copy-start(s32[4]{0:T(128)} %param.35) | copy-start | bytes 52
  326.2 198.2 %all-gather.4.cloned.1.call-start = ((), (), s32[]{:S(2)}) async-start(), calls=%async_computation.9 | async-start | bytes 5947392 | tf_op jit(solution)/shard_map/all_gather | solution.py:221
  431.9 178.3 %all-gather.6.cloned.1.call-start = ((), (), s32[]{:S(2)}) async-start(), calls=%async_computation.10 | async-start | bytes 1531904 | tf_op jit(solution)/shard_map/all_gather | solution.py:17
  535.4 74.7 %copy-start.5 = (bf16[176,88]{1,0:T(8,128)(2,1)S(1)}, bf16[176,88]{1,0:T(8,128)(2,1)}, u32[]{:S(2)}) copy-start(bf16[176,88]{1,0:T(8,128)(2,1)} %param.32) | copy-start | bytes 92932
  573.8 75.0 %reduce-scatter.14.cloned.1.call-start = ((), (), s32[]{:S(2)}) async-start(), calls=%async_computation.11 | async-start | bytes 1622016 | tf_op jit(solution)/shard_map/reduce_scatter | solution.py:21
Sparse Core Ops, SparseCore 0:
  55.4 29.2 reduce-scatter.5
  123.7 73.5 reduce-scatter.7
  235.0 34.4 reduce-scatter.9
  326.3 103.7 reduce-scatter.11
  432.0 92.3 all-gather.3
  573.9 36.1 all-gather.5
  613.2 35.6 reduce-scatter.13
where the time goes:
time: 662 us; the launch traced here: 657 us
  waiting for transfers between devices  404 us (61%)
  blocking collectives  149 us (23%)
  local copies, waits for them, and re-layouts  41.8 us (6%)
  matrix products  23.8 us (4%)
  other arithmetic  23.4 us (4%)
  between operations  13.8 us (2%)
    reduce_scatter x1, waiting for transfers between devices, per_device(): lax.psum_scatter(product_rows(gathered_text, dec_qkv)(jnp.int32(0), lax.a...  104 us
    reduce_scatter x3, waiting for transfers between devices, sums_over_col(): lax.psum_scatter(term_fn(jnp.int32(0), lax.axis_size('col') * count), 'co...  98.3 us
    all_gather x1, waiting for transfers between devices, per_device(): piece = lax.all_gather(dec_keyval, ('row', 'grp'), axis=0, tiled=True)  91.9 us
    reduce_scatter x1, waiting for transfers between devices, per_device(): lax.psum_scatter(product_rows(all_attn, vis_out)(jnp.int32(0), lax.axis_s...  73.5 us
    all_gather x3, blocking collectives, rows_over_col(): return lax.all_gather(values, 'col', axis=0, tiled=True)  54.3 us
    all_gather x2, blocking collectives, rows_over_row(): return lax.all_gather(values, 'row', axis=0, tiled=True)  46.3 us
    all_gather x1, waiting for transfers between devices, rows_over_row(): return lax.all_gather(values, 'row', axis=0, tiled=True)  36.3 us
    psum x1, blocking collectives, per_device(): squares = lax.psum(jnp.sum(xdec * xdec, axis=1), 'row')  31.1 us
  transfers between devices with their start and end apart: 7, of which 7 were waited for; matrix products, arithmetic and copies ran while one was open for 0% of the time, Pallas kernels for 0%

commit v1 on v0

v1 whole, which is shorter than its diff:
```python
import functools

import jax
import jax.numpy as jnp
from jax import lax
from jax.experimental import pallas as pl
from jax.experimental.pallas import tpu as pltpu
from jax.sharding import PartitionSpec as P

HEADS = 16
HEAD_DIM = 88
WIDTH = HEADS * HEAD_DIM
TPD = 256
LOG2E = 1.4426950408889634
NEG = -1e30
F32 = jnp.float32
BF16 = jnp.bfloat16


def spread(values, axes):
    count = lax.axis_size(axes)
    return lax.all_to_all(
        jnp.broadcast_to(values[None], (count,) + values.shape), axes, split_axis=0, concat_axis=0
    )


def exchange(values, axes):
    return lax.all_to_all(values, axes, split_axis=0, concat_axis=0)


def dot0(left, right):
    return lax.dot_general(left, right, (((0,), (0,)), ((), ())), preferred_element_type=F32)


def segment_of(index_values, lengths):
    ends = jnp.cumsum(lengths, dtype=jnp.int32)
    return jnp.sum(
        (index_values[:, None] >= ends[None, :]).astype(jnp.int32), axis=1, dtype=jnp.int32
    )


def image_starts(lengths, gaps):
    offsets = jnp.cumsum(lengths, dtype=jnp.int32) - lengths
    return jnp.cumsum(gaps, dtype=jnp.int32)[: lengths.shape[0]] + offsets, offsets


def insert_map(text_rows, lengths, gaps):
    starts, offsets = image_starts(lengths, gaps)
    inside = (text_rows[:, None] >= starts[None, :]) & (
        text_rows[:, None] < (starts + lengths)[None, :]
    )
    source = jnp.sum(
        jnp.where(inside, offsets[None, :] + text_rows[:, None] - starts[None, :], 0),
        axis=1,
        dtype=jnp.int32,
    )
    return source, jnp.any(inside, axis=1)


def rows_of_merged(merged, lengths, gaps):
    starts, offsets = image_starts(lengths, gaps)
    inside = (merged[:, None] >= offsets[None, :]) & (
        merged[:, None] < (offsets + lengths)[None, :]
    )
    return jnp.sum(
        jnp.where(inside, starts[None, :] + merged[:, None] - offsets[None, :], 0),
        axis=1,
        dtype=jnp.int32,
    )


def sequence_position(rows, half):
    return (rows // TPD) * (2 * TPD) + half * TPD + rows % TPD


def decoder_kernel(
    bounds_ref, q_ref, kv_ref, bias_ref, image_kv_ref, image_pos_ref, qpos_ref, out_ref, acc_ref
):
    rows = q_ref.shape[1]
    block = kv_ref.shape[4]
    factor = LOG2E * HEAD_DIM ** (-0.5)
    query = q_ref[...]
    low = qpos_ref[0:1, :]
    span = qpos_ref[1:2, :]
    acc_ref[...] = jnp.zeros_like(acc_ref)

    def fold(state, keys, values, key_pos):
        best, total = state
        scores = dot0(keys, query)
        offset = key_pos - low
        allowed = (offset >= 0) & (offset <= span)
        scores = jnp.where(allowed, scores, NEG)
        new_best = jnp.maximum(best, jnp.max(scores, axis=0, keepdims=True))
        weights = jnp.exp2((scores - new_best) * factor)
        keep = jnp.exp2((best - new_best) * factor)
        total = total * keep + jnp.sum(weights, axis=0, keepdims=True)
        acc_ref[...] = acc_ref[...] * keep + jnp.dot(
            values, weights.astype(BF16), preferred_element_type=F32
        )
        return new_best, total

    state = (jnp.full((1, rows), NEG, F32), jnp.zeros((1, rows), F32))
    image_keys = jnp.concatenate(
        [image_kv_ref[0], jnp.zeros((8, image_kv_ref.shape[2]), BF16)], axis=0
    )
    state = fold(state, image_keys, image_kv_ref[1], image_pos_ref[...])
    step = lax.broadcasted_iota(jnp.int32, (block, 1), 0)
    in_pair = jnp.where(step >= TPD, step + TPD, step)

    def chunk(index, state):
        for half in range(2):
            keys = jnp.concatenate([kv_ref[index, half, 0], bias_ref[index, half]], axis=0)
            base = index * (2 * block) + half * TPD
            state = fold(state, keys, kv_ref[index, half, 1], in_pair + base)
        return state

    best, total = lax.fori_loop(bounds_ref[0], bounds_ref[1], chunk, state)
    out_ref[...] = (acc_ref[...] / total).astype(BF16)


def decoder_attention(bounds, query, keyval, bias, image_keyval, image_pos, qpos):
    vmem = pl.BlockSpec(memory_space=pltpu.VMEM)
    return pl.pallas_call(
        decoder_kernel,
        out_shape=jax.ShapeDtypeStruct((HEAD_DIM, query.shape[1]), BF16),
        in_specs=[pl.BlockSpec(memory_space=pltpu.SMEM)] + [vmem] * 6,
        out_specs=vmem,
        scratch_shapes=[pltpu.VMEM((HEAD_DIM, query.shape[1]), F32)],
        compiler_params=pltpu.CompilerParams(vmem_limit_bytes=32 * 1024 * 1024),
        name="decoder_attention",
    )(bounds, query, keyval, bias, image_keyval, image_pos, qpos)


def per_device(
    patches,
    vis_gain,
    vis_bias,
    vis_qkv,
    vis_qkv_bias,
    vis_out,
    vis_out_bias,
    proj_weight,
    proj_bias,
    text_embeds,
    dec_gain,
    dec_qkv,
    dec_out,
    image_tokens,
    text_gaps,
    doc_lengths,
):
    cols = lax.axis_size("col")
    rows = lax.axis_size("row")
    row = lax.axis_index("row")
    col = lax.axis_index("col")
    half = lax.axis_index("grp")
    scale = HEAD_DIM ** (-0.5)
    lengths, gaps = image_tokens[0], text_gaps[0]
    images = lengths.shape[0]

    table = jnp.concatenate([lengths, gaps])
    other_table = lax.ppermute(table, "grp", [(0, 1), (1, 0)])
    tables = jnp.where(
        half == 0, jnp.stack([table, other_table]), jnp.stack([other_table, table])
    )
    both_lengths, both_gaps = tables[:, :images], tables[:, images:]

    feat_c = vis_out.shape[1]
    packed = jnp.concatenate(
        [
            dec_qkv,
            vis_out,
            jnp.transpose(proj_weight, (2, 0, 1)).reshape(HEAD_DIM, 4 * feat_c),
            dec_out.T,
        ],
        axis=1,
    )
    gathered_w = lax.all_gather(packed, "col", axis=0)
    qkv_w = dec_qkv.shape[1]

    rows_b = patches.shape[1]
    part = rows_b // cols
    mine = exchange(patches[0].reshape(cols, part, feat_c), "col")
    mine = jnp.transpose(mine, (1, 0, 2)).reshape(part, WIDTH)
    raw = spread(mine, "row").reshape(rows * part, WIDTH)
    vis_w = spread(
        jnp.concatenate(
            [vis_qkv, vis_gain[:, None], vis_bias[:, None], vis_out_bias[:, None]], axis=1
        ),
        "col",
    ).reshape(WIDTH, -1)
    vis_n = vis_qkv.shape[1]
    affine = vis_w[:, vis_n:].T.astype(F32)
    xfull = raw.astype(F32)
    mean = jnp.sum(xfull, axis=1, keepdims=True) / WIDTH
    variance = jnp.sum(xfull * xfull, axis=1, keepdims=True) / WIDTH - mean * mean
    normed = (
        (xfull - mean) * lax.rsqrt(variance + 1e-06) * affine[0:1] + affine[1:2]
    ).astype(BF16)
    qkv_rows = (
        jnp.dot(normed, vis_w[:, :vis_n], preferred_element_type=F32) + vis_qkv_bias.astype(F32)
    ).astype(BF16)

    text = text_embeds[0].T
    positions = text.shape[1]
    text, gathered_w = lax.optimization_barrier((text, gathered_w))
    text_all = lax.all_gather(text, "row", axis=0, tiled=True)

    heads_w = jnp.transpose(
        gathered_w[:, :, :qkv_w].reshape(cols, HEAD_DIM, 2, 3 * HEAD_DIM), (0, 2, 1, 3)
    ).reshape(rows, HEAD_DIM, 3 * HEAD_DIM)
    outs_w = jnp.transpose(
        gathered_w[:, :, qkv_w : qkv_w + feat_c].reshape(cols, HEAD_DIM, 2, HEAD_DIM), (0, 2, 1, 3)
    ).reshape(rows, HEAD_DIM, HEAD_DIM)
    gain = jnp.broadcast_to(dec_gain[None, :, None], (rows, HEAD_DIM, 1))
    row_w = exchange(jnp.concatenate([heads_w, outs_w, gain], axis=2), "row").reshape(WIDTH, -1)
    head_w = row_w[:, : 3 * HEAD_DIM]
    out_w = row_w[:, 3 * HEAD_DIM : 4 * HEAD_DIM]
    gain_all = row_w[:, 4 * HEAD_DIM :].astype(F32)
    proj_at = qkv_w + feat_c
    proj_w = jnp.transpose(
        gathered_w[:, :, proj_at : proj_at + 4 * feat_c].reshape(cols, HEAD_DIM, 4, feat_c),
        (2, 1, 0, 3),
    ).reshape(4, HEAD_DIM, WIDTH)
    dec_out_w = jnp.transpose(gathered_w[:, :, proj_at + 4 * feat_c :], (1, 0, 2)).reshape(
        HEAD_DIM, WIDTH
    )

    xtext = text_all.astype(F32)
    squares = jnp.sum(xtext * xtext, axis=0, keepdims=True)
    text_normed = (xtext * lax.rsqrt(squares / WIDTH + 1e-05) * gain_all).astype(BF16)
    text_qkv = dot0(head_w, text_normed).astype(BF16)
    own_kv = text_qkv[HEAD_DIM:]
    other_kv = lax.ppermute(own_kv, "grp", [(0, 1), (1, 0)])
    pair_kv = jnp.where(half == 0, jnp.stack([own_kv, other_kv]), jnp.stack([other_kv, own_kv]))
    all_kv = lax.all_gather(pair_kv, "col", axis=0).reshape(cols, 2, 2, HEAD_DIM, positions)

    count = rows * part
    query = qkv_rows[:, :HEAD_DIM]
    keyval = spread(qkv_rows[:, HEAD_DIM:], "col").reshape(cols * count, 2 * HEAD_DIM)
    keys, values = keyval[:, :HEAD_DIM], keyval[:, HEAD_DIM:]

    def patch_index(col_index, inner):
        return (inner // part) * rows_b + col_index * part + inner % part

    inner = jnp.arange(count, dtype=jnp.int32)
    query_ids = segment_of(patch_index(col, inner) // 4, lengths)
    every = jnp.arange(cols * count, dtype=jnp.int32)
    key_ids = segment_of(patch_index(every // count, every % count) // 4, lengths)
    allowed = query_ids[:, None] == key_ids[None, :]
    scores = (
        lax.dot_general(query, keys, (((1,), (1,)), ((), ())), preferred_element_type=F32) * scale
    )
    scores = jnp.where(allowed, scores, NEG)
    weights = jnp.where(allowed, jnp.exp(scores - jnp.max(scores, axis=1, keepdims=True)), 0.0)
    total = jnp.sum(weights, axis=1, keepdims=True)
    vis_attn = (jnp.dot(weights.astype(BF16), values, preferred_element_type=F32) / total).astype(
        BF16
    )

    def window_first(array):
        features = array.shape[1]
        return jnp.transpose(
            array.reshape(rows, part // 4, 4, features), (2, 0, 1, 3)
        ).reshape(count, features)

    own_raw = window_first(lax.dynamic_slice(raw, (0, row * HEAD_DIM), (count, HEAD_DIM)))
    own_bias = lax.dynamic_slice(affine[2], (row * HEAD_DIM,), (HEAD_DIM,))
    all_attn = spread(window_first(vis_attn).T, "row").reshape(WIDTH, count)
    resid = (own_raw.T.astype(F32) + dot0(out_w, all_attn) + own_bias[:, None]).astype(BF16)
    all_resid = spread(resid, "row").reshape(WIDTH, count)
    merged = count // 4
    projected = proj_bias.astype(F32)[:, None]
    for window in range(4):
        projected = projected + jnp.dot(
            proj_w[window],
            all_resid[:, window * merged : (window + 1) * merged],
            preferred_element_type=F32,
        )
    image_in = projected.T.astype(BF16)

    image_all = jnp.transpose(spread(image_in, "row"), (1, 0, 2)).reshape(merged, WIDTH)
    ximage = image_all.astype(F32)
    squares = jnp.sum(ximage * ximage, axis=1, keepdims=True)
    image_normed = (
        ximage * lax.rsqrt(squares / WIDTH + 1e-05) * gain_all[:, 0][None, :]
    ).astype(BF16)
    image_qkv = jnp.dot(image_normed, head_w, preferred_element_type=F32).astype(BF16)
    shared = spread(jnp.concatenate([image_qkv, image_in], axis=1), ("col", "grp"))
    shared = shared.reshape(cols, 2, merged, 4 * HEAD_DIM)

    own_rows = col * positions + jnp.arange(positions, dtype=jnp.int32)
    source, inside = insert_map(own_rows, lengths, gaps)
    pair = part // 4
    slot = (source // pair % cols) * merged + source // (pair * cols) * pair + source % pair
    chosen = (
        (slot[None, :] == jnp.arange(cols * merged, dtype=jnp.int32)[:, None]) & inside[None, :]
    ).astype(BF16)
    own_half = lax.dynamic_index_in_dim(shared, half, axis=1, keepdims=False)
    own_half = own_half.reshape(cols * merged, 4 * HEAD_DIM)
    placed_q = dot0(own_half[:, :HEAD_DIM], chosen).astype(BF16)
    placed_in = dot0(own_half[:, 3 * HEAD_DIM :], chosen)
    own_query = jnp.where(inside[None, :], placed_q, text_qkv[:HEAD_DIM])
    dec_input = jnp.where(inside[None, :], placed_in, text.astype(F32))
    query_aug = jnp.concatenate(
        [own_query, jnp.ones((1, positions), BF16), jnp.zeros((7, positions), BF16)], axis=0
    )
    all_rows = jnp.arange(cols * positions, dtype=jnp.int32)
    masks = [insert_map(all_rows, both_lengths[h], both_gaps[h])[1] for h in range(2)]
    bias = jnp.where(jnp.stack(masks), NEG, 0.0).astype(BF16).reshape(2, cols, 1, positions)
    bias = jnp.pad(jnp.transpose(bias, (1, 0, 2, 3)), ((0, 0), (0, 0), (0, 7), (0, 0)))
    item = jnp.arange(cols * merged, dtype=jnp.int32)
    merged_id = (item % merged) // pair * (pair * cols) + (item // merged) * pair + item % pair
    image_pos = jnp.stack(
        [
            sequence_position(rows_of_merged(merged_id, both_lengths[h], both_gaps[h]), h)
            for h in range(2)
        ]
    )
    image_pos = jnp.transpose(image_pos.reshape(2, cols, merged), (1, 0, 2)).reshape(-1, 1)
    image_kv = jnp.transpose(
        shared[..., HEAD_DIM : 3 * HEAD_DIM].reshape(cols * 2 * merged, 2, HEAD_DIM), (1, 2, 0)
    )
    query_pos = sequence_position(own_rows, half)
    ends = jnp.cumsum(doc_lengths, dtype=jnp.int32)
    low = jnp.max(
        jnp.where(query_pos[:, None] >= ends[None, :], ends[None, :], 0), axis=1
    )
    qpos = jnp.stack([low, query_pos - low])
    bounds = jnp.stack([jnp.min(low) // (2 * positions), col + 1]).astype(jnp.int32)
    dec_attn = decoder_attention(bounds, query_aug, all_kv, bias, image_kv, image_pos, qpos)

    all_dec = spread(dec_attn, "row").reshape(WIDTH, positions)
    delta = jnp.dot(dec_out_w, all_dec, preferred_element_type=F32)
    return (dec_input + delta).astype(BF16).T[None]


def solution(mesh):
    return jax.shard_map(
        per_device,
        mesh=mesh,
        in_specs=(
            P("grp", "row", "col"),
            P("col"),
            P("col"),
            P("col", "row"),
            P("row"),
            P("row", "col"),
            P("col"),
            P(None, "col", "row"),
            P("row"),
            P("grp", "col", "row"),
            P("row"),
            P("row", "col"),
            P("col", "row"),
            P("grp", None),
            P("grp", None),
            P(),
        ),
        out_specs=P("grp", "col", "row"),
        check_vma=False,
    )
```

time: 662 us -> 236 us (0.36)
  waiting for transfers between devices: 404 us -> 104 us
  blocking collectives: 149 us -> 0 us
  starting transfers between devices: 0.43 us -> 64 us
  matrix products: 23.8 us -> 6.88 us
  local copies, waits for them, and re-layouts: 41.8 us -> 27.4 us
  other arithmetic: 23.4 us -> 12.9 us
    reduce_scatter x5 -> x0, waiting for transfers between devices: 276 us -> none  [the longest x1 104 us: per_device(): lax.psum_scatter(product_rows(gathered_text, dec_qkv)(jnp.int32(0), lax.a...]
    all_gather x2 -> x3, waiting for transfers between devices: 128 us -> 16.6 us  [the longest x1 16.6 us: per_device(): gathered_w = lax.all_gather(packed, 'col', axis=0)]
    all_gather x5 -> x0, blocking collectives: 101 us -> none  [the longest x3 54.3 us: rows_over_col(): return lax.all_gather(values, 'col', axis=0, tiled=True)]
    all_to_all x0 -> x10, waiting for transfers between devices: none -> 87.8 us  [the longest x8 74 us: spread(): lax.all_to_all(jnp.broadcast_to(values[None], (count,) + values.shape), a...]
    all_to_all x0 -> x10, starting transfers between devices: none -> 57.7 us  [the longest x8 40.2 us: spread(): lax.all_to_all(jnp.broadcast_to(values[None], (count,) + values.shape), a...]
    psum x2 -> x0, blocking collectives: 48.4 us -> none  [the longest x1 31.1 us: per_device(): squares = lax.psum(jnp.sum(xdec * xdec, axis=1), 'row')]
    dot_general x41 -> x13, matrix products: 23.8 us -> 6.88 us  [the longest x4 1.82 us: dot0(): lax.dot_general(left, right, (((0,), (0,)), ((), ())), preferred_element_...]
    squeeze x20 -> x4, local copies, waits for them, and re-layouts: 16.3 us -> 1.35 us  [per_device(): proj_w[window]]
  transfers between devices with their start and end apart: 7 -> 15, of which waited for: 7 -> 8; matrix products, arithmetic and copies ran while one was open for 0% -> 16% of each run, Pallas kernels for 0% -> 0%
where the time goes in v1:
time: 236 us; the launch traced here: 235 us
  waiting for transfers between devices  104 us (44%)
  starting transfers between devices  64 us (27%)
  local copies, waits for them, and re-layouts  27.4 us (12%)
  between operations  16.4 us (7%)
  other arithmetic  12.9 us (5%)
  matrix products  6.88 us (3%)
  Pallas kernels  2.68 us (1%)
    all_to_all x8, waiting for transfers between devices, spread(): lax.all_to_all(jnp.broadcast_to(values[None], (count,) + values.shape), a...  74 us
    all_to_all x8, starting transfers between devices, spread(): lax.all_to_all(jnp.broadcast_to(values[None], (count,) + values.shape), a...  40.2 us
    all_to_all x2, starting transfers between devices, exchange(): return lax.all_to_all(values, axes, split_axis=0, concat_axis=0)  17.5 us
    all_gather x1, waiting for transfers between devices, per_device(): gathered_w = lax.all_gather(packed, 'col', axis=0)  16.6 us
    all_to_all x2, waiting for transfers between devices, exchange(): return lax.all_to_all(values, axes, split_axis=0, concat_axis=0)  13.8 us
    broadcast_in_dim x9, local copies, waits for them, and re-layouts, spread(): jnp.broadcast_to(values[None], (count,) + values.shape)  7.03 us
  transfers between devices with their start and end apart: 15, of which 8 were waited for; matrix products, arithmetic and copies ran while one was open for 16% of the time, Pallas kernels for 0%

profile of v1, /device:TPU:1, one launch (start us, length us, event | category | flops | bytes accessed | tf_op | source)
XLA Modules:
  0.0 234.8 jit_solution(5955847000215595205)
XLA Ops:
  6.6 1.1 copy.117
  8.6 1.8 concatenate.46
  10.4 9.0 %all-to-all-start = ((bf16[8,8,176]{2,1,0:T(8,128)(2,1)}), bf16[8,8,176]{2,1,0:T(8,128)(2,1)S(1)}, u32[]{:S(2)}, u32[]{:S(2)}) async-start(bf16[8,8,176]{2,1,0:T(8,128)(2,1)} %bitcast.205), calls=%async_computation | async-start | bytes 65536 | tf_op jit(solution)/shard_map/all_to_all | solution.py:28
  20.2 2.9 %collective-permute-start.1 = (s32[17]{0:T(128)S(1)}, s32[17]{0:T(128)S(1)}, u32[]{:S(2)}, u32[]{:S(2)}) collective-permute-start(s32[17]{0:T(128)S(1)} %pad_add_fusion.3), channel_id=1, source_target_pairs={{0,1},{1,0},{2,3},{3,2},{4,5},{5,4},{6,7},{7,6},{8,9},{9,8},{10,11... | collective-permute-start | bytes 212 | tf_op jit(solution)/shard_map/ppermute | solution.py:162
  29.6 5.7 %all-to-all-start.1 = ((bf16[16,8,1408]{2,1,0:T(8,128)(2,1)}), bf16[16,8,1408]{2,1,0:T(8,128)(2,1)}, u32[]{:S(2)}, u32[]{:S(2)}) async-start(bf16[16,8,1408]{2,1,0:T(8,128)(2,1)} %broadcast_in_dim.72), calls=%async_computation.1 | async-start | bytes 720896 | tf_op jit(solution)/shard_map/all_to_all | solution.py:22
  36.7 16.6 %all-gather.9.cloned.1.call-done = bf16[704,1584]{1,0:T(8,128)(2,1)} async-done(((bf16[88,1584]{1,0:T(8,128)(2,1)}), bf16[704,1584]{1,0:T(8,128)(2,1)}) %all-gather.9.cloned.1.call-update) | async-done | bytes 2230288 | tf_op jit(solution)/shard_map/all_gather | solution.py:178
  53.3 1.1 broadcast_in_dim.80
  54.4 4.3 %all-to-all-start.3 = ((bf16[8,176,267]{2,1,0:T(8,128)(2,1)}), bf16[8,176,267]{2,1,0:T(8,128)(2,1)S(1)}, u32[]{:S(2)}, u32[]{:S(2)}) async-start(bf16[8,176,267]{2,1,0:T(8,128)(2,1)} %broadcast_in_dim.80), calls=%async_computation.3 | async-start | bytes 2162688 | tf_op jit(solution)/shard_map/all_to_all | solution.py:22
  58.6 1.2 convert_reduce_fusion
  61.8 1.4 pad_maximum_fusion.1
  63.2 22.0 %all-to-all-done.3 = bf16[8,176,267]{2,1,0:T(8,128)(2,1)S(1)} async-done(((bf16[8,176,267]{2,1,0:T(8,128)(2,1)}), bf16[8,176,267]{2,1,0:T(8,128)(2,1)S(1)}, u32[]{:S(2)}, u32[]{:S(2)}) %all-to-all-start.3) | async-done | bytes 751904 | tf_op jit(solution)/shard_map/all_to_all | solution.py:22
  85.3 8.5 %all-to-all-start.2 = ((bf16[16,88,353]{2,1,0:T(8,128)(2,1)}), bf16[16,88,353]{2,1,0:T(8,128)(2,1)S(1)}, u32[]{:S(2)}, u32[]{:S(2)}) async-start(bf16[16,88,353]{2,1,0:T(8,128)(2,1)} %pad_maximum_fusion.1), calls=%async_computation.2 | async-start | bytes 2162688 | tf_op jit(solution)/shard_map/all_to_all | solution.py:28
  94.4 1.5 fusion.12
  95.9 13.8 %all-to-all-done.2 = bf16[16,88,353]{2,1,0:T(8,128)(2,1)S(1)} async-done(((bf16[16,88,353]{2,1,0:T(8,128)(2,1)}), bf16[16,88,353]{2,1,0:T(8,128)(2,1)S(1)}, u32[]{:S(2)}, u32[]{:S(2)}) %all-to-all-start.2) | async-done | bytes 994080 | tf_op jit(solution)/shard_map/all_to_all | solution.py:28
  110.6 3.4 %all-to-all-start.4 = ((bf16[8,128,176]{1,2,0:T(8,128)(2,1)}), bf16[8,128,176]{1,2,0:T(8,128)(2,1)S(1)}, u32[]{:S(2)}, u32[]{:S(2)}) async-start(bf16[8,128,176]{1,2,0:T(8,128)(2,1)} %broadcast_in_dim.81), calls=%async_computation.4 | async-start | bytes 720896 | tf_op jit(solution)/shard_map/all_to_all | solution.py:22
  114.4 1.8 fusion
  117.2 3.2 %collective-permute-start = (bf16[176,512]{1,0:T(8,128)(2,1)S(1)}, bf16[176,512]{1,0:T(8,128)(2,1)S(1)}, u32[]{:S(2)}, u32[]{:S(2)}) collective-permute-start(bf16[176,512]{1,0:T(8,128)(2,1)S(1)} %get-tuple-element.24), channel_id=1, source_target_pairs={{0,1},{1,0},{2,3},{3,2},{4,5},{5,4},{6,7},{7,6},{8,9},{9,8},{10,11... | collective-permute-start | bytes 540680 | tf_op jit(solution)/shard_map/ppermute | solution.py:234
  120.4 7.1 %all-to-all-done.4 = bf16[8,128,176]{1,2,0:T(8,128)(2,1)S(1)} async-done(((bf16[8,128,176]{1,2,0:T(8,128)(2,1)}), bf16[8,128,176]{1,2,0:T(8,128)(2,1)S(1)}, u32[]{:S(2)}, u32[]{:S(2)}) %all-to-all-start.4) | async-done | bytes 360480 | tf_op jit(solution)/shard_map/all_to_all | solution.py:22
  130.3 5.3 %all-to-all-start.5 = ((bf16[16,88,128]{2,1,0:T(8,128)(2,1)}), bf16[16,88,128]{2,1,0:T(8,128)(2,1)S(1)}, u32[]{:S(2)}, u32[]{:S(2)}) async-start(bf16[16,88,128]{2,1,0:T(8,128)(2,1)} %broadcast_in_dim.84), calls=%async_computation.5 | async-start | bytes 720896 | tf_op jit(solution)/shard_map/all_to_all | solution.py:22
  137.5 6.4 %all-to-all-done.5 = bf16[16,88,128]{2,1,0:T(8,128)(2,1)S(1)} async-done(((bf16[16,88,128]{2,1,0:T(8,128)(2,1)}), bf16[16,88,128]{2,1,0:T(8,128)(2,1)S(1)}, u32[]{:S(2)}, u32[]{:S(2)}) %all-to-all-start.5) | async-done | bytes 360480 | tf_op jit(solution)/shard_map/all_to_all | solution.py:22
  145.2 3.9 %all-to-all-start.6 = ((bf16[16,88,128]{2,1,0:T(8,128)(2,1)}), bf16[16,88,128]{2,1,0:T(8,128)(2,1)S(1)}, u32[]{:S(2)}, u32[]{:S(2)}) async-start(bf16[16,88,128]{2,1,0:T(8,128)(2,1)} %broadcast_in_dim.85), calls=%async_computation.6 | async-start | bytes 720896 | tf_op jit(solution)/shard_map/all_to_all | solution.py:22
  149.1 2.8 %slice.162 = bf16[8,88,704]{2,1,0:T(8,128)(2,1)} slice(bf16[8,88,1584]{2,1,0:T(8,128)(2,1)} %bitcast.182), slice={[0:8], [0:88], [704:1408]} | slice | bytes 1982464 | tf_op jit(solution)/shard_map/slice | solution.py:222
  151.9 3.7 %reshape.870 = bf16[8,88,4,176]{3,2,1,0:T(4,128)(2,1)S(1)} reshape(bf16[8,88,704]{2,1,0:T(8,128)(2,1)} %slice.162) | data formatting | bytes 1982464 | tf_op jit(solution)/shard_map/reshape | solution.py:222
  160.2 5.8 %all-to-all-start.7 = ((bf16[16,32,88]{2,1,0:T(8,128)(2,1)}), bf16[16,32,88]{2,1,0:T(8,128)(2,1)S(1)}, u32[]{:S(2)}, u32[]{:S(2)}) async-start(bf16[16,32,88]{2,1,0:T(8,128)(2,1)} %broadcast_in_dim.86), calls=%async_computation.7 | async-start | bytes 262144 | tf_op jit(solution)/shard_map/all_to_all | solution.py:22
  166.2 5.9 %all-to-all-done.7 = bf16[16,32,88]{2,1,0:T(8,128)(2,1)S(1)} async-done(((bf16[16,32,88]{2,1,0:T(8,128)(2,1)}), bf16[16,32,88]{2,1,0:T(8,128)(2,1)S(1)}, u32[]{:S(2)}, u32[]{:S(2)}) %all-to-all-start.7) | async-done | bytes 90144 | tf_op jit(solution)/shard_map/all_to_all | solution.py:22
  173.8 6.3 %all-to-all-start.8 = ((bf16[16,32,352]{2,1,0:T(8,128)(2,1)}), bf16[16,32,352]{2,1,0:T(8,128)(2,1)S(1)}, u32[]{:S(2)}, u32[]{:S(2)}) async-start(bf16[16,32,352]{2,1,0:T(8,128)(2,1)} %broadcast_in_dim.87), calls=%async_computation.8 | async-start | bytes 786432 | tf_op jit(solution)/shard_map/all_to_all | solution.py:22
  180.8 14.3 %all-to-all-done.8 = bf16[16,32,352]{2,1,0:T(8,128)(2,1)S(1)} async-done(((bf16[16,32,352]{2,1,0:T(8,128)(2,1)}), bf16[16,32,352]{2,1,0:T(8,128)(2,1)S(1)}, u32[]{:S(2)}, u32[]{:S(2)}) %all-to-all-start.8) | async-done | bytes 360480 | tf_op jit(solution)/shard_map/all_to_all | solution.py:22
  196.0 1.8 copy-done
  197.8 2.7 %decoder_attention.1 = bf16[88,512]{1,0:T(8,128)(2,1)S(1)} custom-call(s32[2]{0:T(128)S(1)} %pad_add_fusion.2.bounds_ref, bf16[96,512]{1,0:T(8,128)(2,1)S(1)} %maximum_maximum_fusion.q_ref, bf16[8,2,2,88,512]{4,3,2,1,0:T(8,128)(2,1)S(1)} %bitcast.169, bf16[8,2,8,512]{3,2,1,0:T(8,128)(2,1)S(1)} %pad.4.bias_ref, bf16[2,88,512]{2,1,0:T(8,128)(2,1)S(1)} %bitcast.170, ...), custom_call_target="tpu_custom_call" | custom-call | tf_op jit(solution)/shard_map/decoder_attention/pallas_call | solution.py:123
  200.5 1.2 broadcast_in_dim.97
  201.7 5.6 %all-to-all-start.9 = ((bf16[16,88,512]{2,1,0:T(8,128)(2,1)}), bf16[16,88,512]{2,1,0:T(8,128)(2,1)S(1)}, u32[]{:S(2)}, u32[]{:S(2)}) async-start(bf16[16,88,512]{2,1,0:T(8,128)(2,1)} %broadcast_in_dim.97), calls=%async_computation.9 | async-start | bytes 2883584 | tf_op jit(solution)/shard_map/all_to_all | solution.py:22
  209.0 18.3 %all-to-all-done.9 = bf16[16,88,512]{2,1,0:T(8,128)(2,1)S(1)} async-done(((bf16[16,88,512]{2,1,0:T(8,128)(2,1)}), bf16[16,88,512]{2,1,0:T(8,128)(2,1)S(1)}, u32[]{:S(2)}, u32[]{:S(2)}) %all-to-all-start.9) | async-done | bytes 1441824 | tf_op jit(solution)/shard_map/all_to_all | solution.py:22
  (162 shorter events, 28.1 us)
Async XLA Ops:
  6.5 20.4 %copy-start.10 = (s32[1,8]{1,0:T(1,128)S(1)}, s32[1,8]{1,0:T(1,128)}, u32[]{:S(2)}) copy-start(s32[1,8]{1,0:T(1,128)} %param.29) | copy-start | bytes 100
  6.5 20.6 %copy-start.13 = (s32[1,9]{1,0:T(1,128)S(1)}, s32[1,9]{1,0:T(1,128)}, u32[]{:S(2)}) copy-start(s32[1,9]{1,0:T(1,128)} %param.30) | copy-start | bytes 112
  6.5 20.1 %copy-start.6 = (bf16[176]{0:T(256)(128)(2,1)S(1)}, bf16[176]{0:T(256)(128)(2,1)}, u32[]{:S(2)}) copy-start(bf16[176]{0:T(256)(128)(2,1)} %param.17) | copy-start | bytes 1060
  6.5 20.2 %copy-start.7 = (bf16[176]{0:T(256)(128)(2,1)S(1)}, bf16[176]{0:T(256)(128)(2,1)}, u32[]{:S(2)}) copy-start(bf16[176]{0:T(256)(128)(2,1)} %param.18) | copy-start | bytes 1060
  6.5 20.3 %copy-start.8 = (bf16[176]{0:T(256)(128)(2,1)S(1)}, bf16[176]{0:T(256)(128)(2,1)}, u32[]{:S(2)}) copy-start(bf16[176]{0:T(256)(128)(2,1)} %param.22) | copy-start | bytes 1060
  6.5 21.9 %copy-start.3 = (bf16[176,264]{1,0:T(8,128)(2,1)S(1)}, bf16[176,264]{1,0:T(8,128)(2,1)}, u32[]{:S(2)}) copy-start(bf16[176,264]{1,0:T(8,128)(2,1)} %param.19) | copy-start | bytes 278788
  6.6 46.7 %all-gather.9.cloned.1.call-start = ((), (), s32[]{:S(2)}) async-start(), calls=%async_computation.12 | async-start | bytes 2635776 | tf_op jit(solution)/shard_map/all_gather | solution.py:178
  8.6 26.8 %copy-start.5 = (bf16[264]{0:T(512)(128)(2,1)S(1)}, bf16[264]{0:T(512)(128)(2,1)}, u32[]{:S(2)}) copy-start(bf16[264]{0:T(512)(128)(2,1)} %param.20) | copy-start | bytes 1588
  8.6 26.8 %copy-start.14 = (bf16[88]{0:T(256)(128)(2,1)S(1)}, bf16[88]{0:T(256)(128)(2,1)}, u32[]{:S(2)}) copy-start(bf16[88]{0:T(256)(128)(2,1)} %param.24) | copy-start | bytes 532
  10.4 18.3 %all-to-all-start = ((bf16[8,8,176]{2,1,0:T(8,128)(2,1)}), bf16[8,8,176]{2,1,0:T(8,128)(2,1)S(1)}, u32[]{:S(2)}, u32[]{:S(2)}) async-start(bf16[8,8,176]{2,1,0:T(8,128)(2,1)} %bitcast.205), calls=%async_computation | async-start | bytes 65536 | tf_op jit(solution)/shard_map/all_to_all | solution.py:28
  20.2 15.9 %collective-permute-start.1 = (s32[17]{0:T(128)S(1)}, s32[17]{0:T(128)S(1)}, u32[]{:S(2)}, u32[]{:S(2)}) collective-permute-start(s32[17]{0:T(128)S(1)} %pad_add_fusion.3), channel_id=1, source_target_pairs={{0,1},{1,0},{2,3},{3,2},{4,5},{5,4},{6,7},{7,6},{8,9},{9,8},{10,11... | collective-permute-start | bytes 212 | tf_op jit(solution)/shard_map/ppermute | solution.py:162
  29.6 23.6 %all-to-all-start.1 = ((bf16[16,8,1408]{2,1,0:T(8,128)(2,1)}), bf16[16,8,1408]{2,1,0:T(8,128)(2,1)}, u32[]{:S(2)}, u32[]{:S(2)}) async-start(bf16[16,8,1408]{2,1,0:T(8,128)(2,1)} %broadcast_in_dim.72), calls=%async_computation.1 | async-start | bytes 720896 | tf_op jit(solution)/shard_map/all_to_all | solution.py:22
  35.3 79.1 %all-gather.5.cloned.1.call-start = ((), (), s32[]{:S(2)}) async-start(), calls=%async_computation.10 | async-start | bytes 1531904 | tf_op jit(solution)/shard_map/all_gather | solution.py:207
  54.4 6.2 %copy-start.1 = (bf16[704,1584]{1,0:T(8,128)(2,1)S(1)}, bf16[704,1584]{1,0:T(8,128)(2,1)}, u32[]{:S(2)}) copy-start(bf16[704,1584]{1,0:T(8,128)(2,1)} %all-gather.9.cloned.1.call-done) | copy-start | bytes 6690820
  54.4 30.9 %all-to-all-start.3 = ((bf16[8,176,267]{2,1,0:T(8,128)(2,1)}), bf16[8,176,267]{2,1,0:T(8,128)(2,1)S(1)}, u32[]{:S(2)}, u32[]{:S(2)}) async-start(bf16[8,176,267]{2,1,0:T(8,128)(2,1)} %broadcast_in_dim.80), calls=%async_computation.3 | async-start | bytes 2162688 | tf_op jit(solution)/shard_map/all_to_all | solution.py:22
  61.1 0.7 copy-start.9
  85.3 24.5 %all-to-all-start.2 = ((bf16[16,88,353]{2,1,0:T(8,128)(2,1)}), bf16[16,88,353]{2,1,0:T(8,128)(2,1)S(1)}, u32[]{:S(2)}, u32[]{:S(2)}) async-start(bf16[16,88,353]{2,1,0:T(8,128)(2,1)} %pad_maximum_fusion.1), calls=%async_computation.2 | async-start | bytes 2162688 | tf_op jit(solution)/shard_map/all_to_all | solution.py:28
  93.7 0.7 copy-start.15
  110.6 16.9 %all-to-all-start.4 = ((bf16[8,128,176]{1,2,0:T(8,128)(2,1)}), bf16[8,128,176]{1,2,0:T(8,128)(2,1)S(1)}, u32[]{:S(2)}, u32[]{:S(2)}) async-start(bf16[8,128,176]{1,2,0:T(8,128)(2,1)} %broadcast_in_dim.81), calls=%async_computation.4 | async-start | bytes 720896 | tf_op jit(solution)/shard_map/all_to_all | solution.py:22
  114.0 82.0 %all-gather.7.cloned.1.call-start = ((), (), s32[]{:S(2)}) async-start(), calls=%async_computation.11 | async-start | bytes 3244032 | tf_op jit(solution)/shard_map/all_gather | solution.py:236
  114.4 1.9 copy-start.2
  117.2 10.3 %collective-permute-start = (bf16[176,512]{1,0:T(8,128)(2,1)S(1)}, bf16[176,512]{1,0:T(8,128)(2,1)S(1)}, u32[]{:S(2)}, u32[]{:S(2)}) collective-permute-start(bf16[176,512]{1,0:T(8,128)(2,1)S(1)} %get-tuple-element.24), channel_id=1, source_target_pairs={{0,1},{1,0},{2,3},{3,2},{4,5},{5,4},{6,7},{7,6},{8,9},{9,8},{10,11... | collective-permute-start | bytes 540680 | tf_op jit(solution)/shard_map/ppermute | solution.py:234
  128.7 7.0 %copy-start.11 = (s32[8,1]{0,1:T(1,128)S(1)}, s32[8,1]{0,1:T(1,128)}, u32[]{:S(2)}) copy-start(s32[8,1]{0,1:T(1,128)} %get-tuple-element.37) | copy-start | bytes 100
  130.3 13.6 %all-to-all-start.5 = ((bf16[16,88,128]{2,1,0:T(8,128)(2,1)}), bf16[16,88,128]{2,1,0:T(8,128)(2,1)S(1)}, u32[]{:S(2)}, u32[]{:S(2)}) async-start(bf16[16,88,128]{2,1,0:T(8,128)(2,1)} %broadcast_in_dim.84), calls=%async_computation.5 | async-start | bytes 720896 | tf_op jit(solution)/shard_map/all_to_all | solution.py:22
  145.2 12.8 %all-to-all-start.6 = ((bf16[16,88,128]{2,1,0:T(8,128)(2,1)}), bf16[16,88,128]{2,1,0:T(8,128)(2,1)S(1)}, u32[]{:S(2)}, u32[]{:S(2)}) async-start(bf16[16,88,128]{2,1,0:T(8,128)(2,1)} %broadcast_in_dim.85), calls=%async_computation.6 | async-start | bytes 720896 | tf_op jit(solution)/shard_map/all_to_all | solution.py:22
  156.6 1.4 copy-start.12
  160.2 11.9 %all-to-all-start.7 = ((bf16[16,32,88]{2,1,0:T(8,128)(2,1)}), bf16[16,32,88]{2,1,0:T(8,128)(2,1)S(1)}, u32[]{:S(2)}, u32[]{:S(2)}) async-start(bf16[16,32,88]{2,1,0:T(8,128)(2,1)} %broadcast_in_dim.86), calls=%async_computation.7 | async-start | bytes 262144 | tf_op jit(solution)/shard_map/all_to_all | solution.py:22
  173.8 21.2 %all-to-all-start.8 = ((bf16[16,32,352]{2,1,0:T(8,128)(2,1)}), bf16[16,32,352]{2,1,0:T(8,128)(2,1)S(1)}, u32[]{:S(2)}, u32[]{:S(2)}) async-start(bf16[16,32,352]{2,1,0:T(8,128)(2,1)} %broadcast_in_dim.87), calls=%async_computation.8 | async-start | bytes 786432 | tf_op jit(solution)/shard_map/all_to_all | solution.py:22
  196.0 1.8 copy-start
  201.7 25.6 %all-to-all-start.9 = ((bf16[16,88,512]{2,1,0:T(8,128)(2,1)}), bf16[16,88,512]{2,1,0:T(8,128)(2,1)S(1)}, u32[]{:S(2)}, u32[]{:S(2)}) async-start(bf16[16,88,512]{2,1,0:T(8,128)(2,1)} %broadcast_in_dim.97), calls=%async_computation.9 | async-start | bytes 2883584 | tf_op jit(solution)/shard_map/all_to_all | solution.py:22
  207.3 1.5 copy-start.4
Sparse Core Ops, SparseCore 0:
  10.5 42.6 all-gather.8
  55.1 37.3 all-gather.4
  128.4 39.5 all-gather.6

commit v2 on v1

v2 whole, which is shorter than its diff:
```python
import functools

import jax
import jax.numpy as jnp
from jax import lax
from jax.experimental import pallas as pl
from jax.experimental.pallas import tpu as pltpu
from jax.sharding import PartitionSpec as P

HEADS = 16
HEAD_DIM = 88
WIDTH = HEADS * HEAD_DIM
TPD = 256
LOG2E = 1.4426950408889634
NEG = -1e30
F32 = jnp.float32
BF16 = jnp.bfloat16


def spread(values, axes):
    count = lax.axis_size(axes)
    return lax.all_to_all(
        jnp.broadcast_to(values[None], (count,) + values.shape), axes, split_axis=0, concat_axis=0
    )


def exchange(values, axes):
    return lax.all_to_all(values, axes, split_axis=0, concat_axis=0)


def dot0(left, right):
    return lax.dot_general(left, right, (((0,), (0,)), ((), ())), preferred_element_type=F32)


def running(lengths):
    at = jnp.arange(lengths.shape[0], dtype=jnp.int32)
    return jnp.sum(
        jnp.where(at[None, :] <= at[:, None], lengths[None, :], 0), axis=1, dtype=jnp.int32
    )


def segment_of(index_values, lengths):
    ends = running(lengths)
    return jnp.sum(
        (index_values[:, None] >= ends[None, :]).astype(jnp.int32), axis=1, dtype=jnp.int32
    )


def image_starts(lengths, gaps):
    offsets = running(lengths) - lengths
    return running(gaps)[: lengths.shape[0]] + offsets, offsets


def insert_map(text_rows, lengths, gaps):
    starts, offsets = image_starts(lengths, gaps)
    inside = (text_rows[:, None] >= starts[None, :]) & (
        text_rows[:, None] < (starts + lengths)[None, :]
    )
    source = jnp.sum(
        jnp.where(inside, offsets[None, :] + text_rows[:, None] - starts[None, :], 0),
        axis=1,
        dtype=jnp.int32,
    )
    return source, jnp.any(inside, axis=1)


def rows_of_merged(merged, lengths, gaps):
    starts, offsets = image_starts(lengths, gaps)
    inside = (merged[:, None] >= offsets[None, :]) & (
        merged[:, None] < (offsets + lengths)[None, :]
    )
    return jnp.sum(
        jnp.where(inside, starts[None, :] + merged[:, None] - offsets[None, :], 0),
        axis=1,
        dtype=jnp.int32,
    )


def sequence_position(rows, half):
    return (rows // TPD) * (2 * TPD) + half * TPD + rows % TPD


def decoder_kernel(
    bounds_ref, q_ref, kv_ref, image_kv_ref, image_pos_ref, qpos_ref, out_ref, acc_ref
):
    rows = q_ref.shape[1]
    block = kv_ref.shape[3]
    key_rows = q_ref.shape[0]
    factor = LOG2E * HEAD_DIM ** (-0.5)
    query = q_ref[...]
    low = qpos_ref[0:1, :]
    span = qpos_ref[1:2, :]
    acc_ref[...] = jnp.zeros_like(acc_ref)

    def fold(state, keys, values, key_pos):
        best, total = state
        scores = dot0(keys, query)
        offset = key_pos - low
        allowed = (offset >= 0) & (offset <= span)
        scores = jnp.where(allowed, scores, NEG)
        new_best = jnp.maximum(best, jnp.max(scores, axis=0, keepdims=True))
        weights = jnp.exp2((scores - new_best) * factor)
        keep = jnp.exp2((best - new_best) * factor)
        total = total * keep + jnp.sum(weights, axis=0, keepdims=True)
        acc_ref[...] = acc_ref[...] * keep + jnp.dot(
            values, weights.astype(BF16), preferred_element_type=F32
        )
        return new_best, total

    state = (jnp.full((1, rows), NEG, F32), jnp.zeros((1, rows), F32))
    state = fold(state, image_kv_ref[:key_rows], image_kv_ref[key_rows:], image_pos_ref[...])
    step = lax.broadcasted_iota(jnp.int32, (block, 1), 0)
    in_pair = jnp.where(step >= TPD, step + TPD, step)

    def chunk(index, state):
        for half in range(2):
            keys = kv_ref[index, half, :key_rows]
            values = kv_ref[index, half, key_rows:]
            base = index * (2 * block) + half * TPD
            state = fold(state, keys, values, in_pair + base)
        return state

    best, total = lax.fori_loop(bounds_ref[0], bounds_ref[1], chunk, state)
    out_ref[...] = (acc_ref[...] / total).astype(BF16)


def decoder_attention(bounds, query, keyval, image_keyval, image_pos, qpos):
    vmem = pl.BlockSpec(memory_space=pltpu.VMEM)
    return pl.pallas_call(
        decoder_kernel,
        out_shape=jax.ShapeDtypeStruct((HEAD_DIM, query.shape[1]), BF16),
        in_specs=[pl.BlockSpec(memory_space=pltpu.SMEM)] + [vmem] * 5,
        out_specs=vmem,
        scratch_shapes=[pltpu.VMEM((HEAD_DIM, query.shape[1]), F32)],
        compiler_params=pltpu.CompilerParams(vmem_limit_bytes=32 * 1024 * 1024),
        name="decoder_attention",
    )(bounds, query, keyval, image_keyval, image_pos, qpos)


def per_device(
    patches,
    vis_gain,
    vis_bias,
    vis_qkv,
    vis_qkv_bias,
    vis_out,
    vis_out_bias,
    proj_weight,
    proj_bias,
    text_embeds,
    dec_gain,
    dec_qkv,
    dec_out,
    image_tokens,
    text_gaps,
    doc_lengths,
):
    cols = lax.axis_size("col")
    rows = lax.axis_size("row")
    row = lax.axis_index("row")
    col = lax.axis_index("col")
    half = lax.axis_index("grp")
    scale = HEAD_DIM ** (-0.5)

    feat_c = vis_out.shape[1]
    vis_n = vis_qkv.shape[1]
    unit = -(-(vis_n + HEAD_DIM) // 128) * 128
    fill = jnp.zeros((HEAD_DIM, unit - vis_n - HEAD_DIM), BF16)
    sides = (slice(0, HEAD_DIM), slice(HEAD_DIM, 2 * HEAD_DIM))
    units = [
        [dec_qkv[:, at * vis_n : (at + 1) * vis_n], vis_out[:, side], fill]
        for at, side in enumerate(sides)
    ]
    units += [[vis_qkv[side], dec_out[side], fill] for side in sides]
    units += [[proj_weight[window, side] for window in range(4)] + [fill] for side in sides]
    packed = jnp.stack([jnp.concatenate(pieces, axis=1) for pieces in units])
    gathered_w = lax.all_gather(packed, "col", axis=0)

    def pair(number):
        return gathered_w[:, 2 * number : 2 * number + 2]

    rows_b = patches.shape[1]
    part = rows_b // cols
    affine_own = jnp.stack([vis_gain, vis_bias, vis_out_bias])
    affine_own = jnp.pad(affine_own, ((0, 8 - affine_own.shape[0]), (0, 0)))
    mine = exchange(
        jnp.concatenate(
            [
                patches[0].reshape(cols, part, feat_c),
                jnp.broadcast_to(affine_own[None], (cols, 8, feat_c)),
            ],
            axis=1,
        ),
        "col",
    )
    mine = jnp.transpose(mine, (1, 0, 2)).reshape(part + 8, WIDTH)
    affine = mine[part : part + 3].astype(F32)

    text = text_embeds[0].T
    positions = text.shape[1]
    folds = -(-(WIDTH + HEAD_DIM) // positions)
    spare = folds * positions - WIDTH
    gain = jnp.broadcast_to(jnp.pad(dec_gain, (0, spare - HEAD_DIM))[None], (part, spare))
    folded = jnp.concatenate([mine[:part], gain], axis=1)
    folded = jnp.transpose(folded.reshape(part, folds, positions), (1, 0, 2))
    both = spread(
        jnp.concatenate([text, folded.reshape(folds * part, positions)], axis=0), "row"
    )
    text_all = both[:, :HEAD_DIM].reshape(WIDTH, positions)
    raw = jnp.transpose(
        both[:, HEAD_DIM:].reshape(rows, folds, part, positions), (0, 2, 1, 3)
    ).reshape(rows, part, folds * positions)
    gain_all = raw[:, 0, WIDTH : WIDTH + HEAD_DIM].reshape(WIDTH, 1).astype(F32)
    raw = raw[:, :, :WIDTH].reshape(rows * part, WIDTH)
    xtext = text_all.astype(F32)
    squares = jnp.sum(xtext * xtext, axis=0, keepdims=True)
    text_normed = (xtext * lax.rsqrt(squares / WIDTH + 1e-05) * gain_all).astype(BF16)

    row_w = exchange(pair(0).reshape(rows, HEAD_DIM, unit), "row").reshape(WIDTH, unit)

    vis_w = pair(1).reshape(WIDTH, unit)
    xfull = raw.astype(F32)
    mean = jnp.sum(xfull, axis=1, keepdims=True) / WIDTH
    variance = jnp.sum(xfull * xfull, axis=1, keepdims=True) / WIDTH - mean * mean
    normed = (
        (xfull - mean) * lax.rsqrt(variance + 1e-06) * affine[0:1] + affine[1:2]
    ).astype(BF16)
    qkv_rows = (
        jnp.dot(normed, vis_w, preferred_element_type=F32)[:, :vis_n]
        + vis_qkv_bias.astype(F32)
    ).astype(BF16)
    count = rows * part
    query = qkv_rows[:, :HEAD_DIM]
    row_w, vis_kv = lax.optimization_barrier((row_w, qkv_rows[:, HEAD_DIM:]))
    lengths, gaps = image_tokens[0], text_gaps[0]
    own_rows = col * positions + jnp.arange(positions, dtype=jnp.int32)
    source, inside = insert_map(own_rows, lengths, gaps)
    keyval = spread(vis_kv, "col").reshape(cols * count, 2 * HEAD_DIM)
    proj_w = pair(2).reshape(WIDTH, unit)
    dec_out_w = vis_w[:, vis_n : vis_n + HEAD_DIM]

    text_qkv = dot0(row_w, text_normed)[:vis_n].astype(BF16)
    bias = jnp.where(inside, NEG, 0.0).astype(BF16)[None]
    own_kv = jnp.concatenate(
        [
            text_qkv[HEAD_DIM : 2 * HEAD_DIM],
            jnp.pad(bias, ((0, 7), (0, 0))),
            text_qkv[2 * HEAD_DIM :],
        ],
        axis=0,
    )
    other_kv = lax.ppermute(own_kv, "grp", [(0, 1), (1, 0)])
    pair_kv = jnp.where(half == 0, jnp.stack([own_kv, other_kv]), jnp.stack([other_kv, own_kv]))
    pair_kv, keyval = lax.optimization_barrier((pair_kv, keyval))
    all_kv = lax.all_gather(pair_kv, "col", axis=0)

    keys, values = keyval[:, :HEAD_DIM], keyval[:, HEAD_DIM:]

    def patch_index(col_index, inner):
        return (inner // part) * rows_b + col_index * part + inner % part

    inner = jnp.arange(count, dtype=jnp.int32)
    query_ids = segment_of(patch_index(col, inner) // 4, lengths)
    every = jnp.arange(cols * count, dtype=jnp.int32)
    key_ids = segment_of(patch_index(every // count, every % count) // 4, lengths)
    allowed = query_ids[:, None] == key_ids[None, :]
    scores = (
        lax.dot_general(query, keys, (((1,), (1,)), ((), ())), preferred_element_type=F32) * scale
    )
    scores = jnp.where(allowed, scores, NEG)
    weights = jnp.where(allowed, jnp.exp(scores - jnp.max(scores, axis=1, keepdims=True)), 0.0)
    total = jnp.sum(weights, axis=1, keepdims=True)
    vis_attn = (jnp.dot(weights.astype(BF16), values, preferred_element_type=F32) / total).astype(
        BF16
    )

    def window_first(array):
        features = array.shape[1]
        return jnp.transpose(
            array.reshape(rows, part // 4, 4, features), (2, 0, 1, 3)
        ).reshape(count, features)

    raw_at = row * HEAD_DIM
    own_raw = window_first(lax.dynamic_slice(raw, (0, raw_at), (count, HEAD_DIM)))
    own_bias = lax.dynamic_slice(affine[2], (raw_at,), (HEAD_DIM,))
    all_attn = spread(window_first(vis_attn).T, "row").reshape(WIDTH, count)
    resid = (own_raw.T.astype(F32) + dot0(row_w, all_attn)[vis_n : vis_n + HEAD_DIM] + own_bias[:, None]).astype(BF16)
    all_resid = spread(resid, "row").reshape(WIDTH, count)
    merged = count // 4
    windows = dot0(proj_w, all_resid)
    projected = proj_bias.astype(F32)[:, None]
    for window in range(4):
        projected = projected + windows[
            window * HEAD_DIM : (window + 1) * HEAD_DIM, window * merged : (window + 1) * merged
        ]
    image_in = projected.T.astype(BF16)

    image_all = jnp.transpose(spread(image_in, "row"), (1, 0, 2)).reshape(merged, WIDTH)
    ximage = image_all.astype(F32)
    squares = jnp.sum(ximage * ximage, axis=1, keepdims=True)
    image_normed = (
        ximage * lax.rsqrt(squares / WIDTH + 1e-05) * gain_all[:, 0][None, :]
    ).astype(BF16)
    image_qkv = jnp.dot(image_normed, row_w, preferred_element_type=F32)[:, :vis_n].astype(BF16)
    pack = part // 4
    item = jnp.arange(merged, dtype=jnp.int32)
    merged_id = item // pack * (pack * cols) + col * pack + item % pack
    place = sequence_position(rows_of_merged(merged_id, lengths, gaps), half)
    place = jnp.stack([place // 64, place % 64], axis=1).astype(BF16)
    shared = spread(
        jnp.concatenate(
            [
                image_qkv[:, : 2 * HEAD_DIM],
                jnp.zeros((merged, 8), BF16),
                image_qkv[:, 2 * HEAD_DIM :],
                image_in,
                place,
            ],
            axis=1,
        ),
        ("col", "grp"),
    )
    key_at, in_at = HEAD_DIM, 3 * HEAD_DIM + 8
    place_at = in_at + HEAD_DIM
    everything = shared.reshape(cols * 2 * merged, -1)
    shared = shared.reshape(cols, 2, merged, -1)

    slot = (source // pack % cols) * merged + source // (pack * cols) * pack + source % pack
    chosen = (
        (slot[None, :] == jnp.arange(cols * merged, dtype=jnp.int32)[:, None]) & inside[None, :]
    ).astype(BF16)
    own_half = lax.dynamic_index_in_dim(shared, half, axis=1, keepdims=False)
    own_half = own_half.reshape(cols * merged, -1)
    placed = dot0(own_half, chosen)
    own_query = jnp.where(
        inside[None, :], placed[:HEAD_DIM].astype(BF16), text_qkv[:HEAD_DIM]
    )
    dec_input = jnp.where(inside[None, :], placed[in_at : in_at + HEAD_DIM], text.astype(F32))
    query_aug = jnp.concatenate(
        [own_query, jnp.ones((1, positions), BF16), jnp.zeros((7, positions), BF16)], axis=0
    )
    image_kv = everything[:, key_at:in_at].T
    place = everything[:, place_at : place_at + 2].astype(jnp.int32)
    image_pos = place[:, :1] * 64 + place[:, 1:]
    query_pos = sequence_position(own_rows, half)
    ends = running(doc_lengths)
    low = jnp.max(
        jnp.where(query_pos[:, None] >= ends[None, :], ends[None, :], 0), axis=1
    )
    qpos = jnp.stack([low, query_pos - low])
    bounds = jnp.stack([jnp.min(low) // (2 * positions), col + 1]).astype(jnp.int32)
    dec_attn = decoder_attention(bounds, query_aug, all_kv, image_kv, image_pos, qpos)

    all_dec = spread(dec_attn, "row").reshape(WIDTH, positions)
    delta = dot0(dec_out_w, all_dec)
    return (dec_input + delta).astype(BF16).T[None]


def solution(mesh):
    return jax.shard_map(
        per_device,
        mesh=mesh,
        in_specs=(
            P("grp", "row", "col"),
            P("col"),
            P("col"),
            P("col", "row"),
            P("row"),
            P("row", "col"),
            P("col"),
            P(None, "col", "row"),
            P("row"),
            P("grp", "col", "row"),
            P("row"),
            P("row", "col"),
            P("col", "row"),
            P("grp", None),
            P("grp", None),
            P(),
        ),
        out_specs=P("grp", "col", "row"),
        check_vma=False,
    )
```

time: 236 us -> 213 us (0.903)
  blocking collectives: 0 us -> 25.1 us
  waiting for transfers between devices: 104 us -> 82.8 us
  starting transfers between devices: 64 us -> 46.5 us
  local copies, waits for them, and re-layouts: 27.4 us -> 20.7 us
    all_to_all x0 -> x1, blocking collectives: none -> 25.1 us  [spread(): lax.all_to_all(jnp.broadcast_to(values[None], (count,) + values.shape), a...]
    all_gather x1, waiting for transfers between devices: 16.6 us -> 0.01 us  [per_device(): gathered_w = lax.all_gather(packed, 'col', axis=0)]
    all_to_all x8 -> x6, waiting for transfers between devices: 74 us -> 59.1 us  [spread(): lax.all_to_all(jnp.broadcast_to(values[None], (count,) + values.shape), a...]
    all_to_all x8 -> x6, starting transfers between devices: 40.2 us -> 29.5 us  [spread(): lax.all_to_all(jnp.broadcast_to(values[None], (count,) + values.shape), a...]
    reshape x8 -> x2, local copies, waits for them, and re-layouts: 6.53 us -> 0.06 us  [the longest x1 0.03 us: per_device(): keyval = spread(vis_kv, 'col').reshape(cols * count, 2 * HEAD_DIM)]
    all_to_all x2, waiting for transfers between devices: 13.8 us -> 20.1 us  [exchange(): return lax.all_to_all(values, axes, split_axis=0, concat_axis=0)]
    slice x5 -> x15, local copies, waits for them, and re-layouts: 3.12 us -> 8.35 us  [the longest x1 3.71 us: pair(): return gathered_w[:, 2 * number:2 * number + 2]]
    dot_general x7 -> x2, matrix products: 4.38 us -> 0.89 us  [the longest x1 0.57 us: per_device(): jnp.dot(normed, vis_w, preferred_element_type=F32)[:, :vis_n]]
  transfers between devices with their start and end apart: 15 -> 11, of which waited for: 8 -> 9; matrix products, arithmetic and copies ran while one was open for 16% -> 11% of each run, Pallas kernels for 0% -> 0%
where the time goes in v2:
time: 213 us; the launch traced here: 212 us
  waiting for transfers between devices  82.8 us (39%)
  starting transfers between devices  46.5 us (22%)
  blocking collectives  25.1 us (12%)
  local copies, waits for them, and re-layouts  20.7 us (10%)
  between operations  16.7 us (8%)
  other arithmetic  11.5 us (5%)
  matrix products  5.71 us (3%)
  Pallas kernels  2.7 us (1%)
    all_to_all x6, waiting for transfers between devices, spread(): lax.all_to_all(jnp.broadcast_to(values[None], (count,) + values.shape), a...  59.1 us
    all_to_all x6, starting transfers between devices, spread(): lax.all_to_all(jnp.broadcast_to(values[None], (count,) + values.shape), a...  29.5 us
    all_to_all x1, blocking collectives, spread(): lax.all_to_all(jnp.broadcast_to(values[None], (count,) + values.shape), a...  25.1 us
    all_to_all x2, waiting for transfers between devices, exchange(): return lax.all_to_all(values, axes, split_axis=0, concat_axis=0)  20.1 us
    all_to_all x2, starting transfers between devices, exchange(): return lax.all_to_all(values, axes, split_axis=0, concat_axis=0)  14.2 us
    broadcast_in_dim x7, local copies, waits for them, and re-layouts, spread(): jnp.broadcast_to(values[None], (count,) + values.shape)  5.38 us
  transfers between devices with their start and end apart: 11, of which 9 were waited for; matrix products, arithmetic and copies ran while one was open for 11% of the time, Pallas kernels for 0%

profile of v2, /device:TPU:1, one launch (start us, length us, event | category | flops | bytes accessed | tf_op | source)
XLA Modules:
  0.0 211.8 jit_solution(697438450595914254)
XLA Ops:
  6.6 0.9 slice_bitcast_fusion.2
  7.5 1.0 fusion.123
  8.6 0.9 fusion.125
  9.5 0.9 fusion.122
  13.4 9.0 %all-to-all-start = ((bf16[8,16,176]{2,1,0:T(8,128)(2,1)}), bf16[8,16,176]{2,1,0:T(8,128)(2,1)S(1)}, u32[]{:S(2)}, u32[]{:S(2)}) async-start(bf16[8,16,176]{2,1,0:T(8,128)(2,1)} %pad_maximum_fusion.5), calls=%async_computation | async-start | bytes 131072 | tf_op jit(solution)/shard_map/all_to_all | solution.py:28
  22.7 6.9 %all-to-all-done = bf16[8,16,176]{2,1,0:T(8,128)(2,1)S(1)} async-done(((bf16[8,16,176]{2,1,0:T(8,128)(2,1)}), bf16[8,16,176]{2,1,0:T(8,128)(2,1)S(1)}, u32[]{:S(2)}, u32[]{:S(2)}) %all-to-all-start) | async-done | bytes 45088 | tf_op jit(solution)/shard_map/all_to_all | solution.py:28
  29.8 1.4 broadcast_in_dim.137
  31.3 7.5 %all-to-all-start.1 = ((bf16[16,112,512]{2,1,0:T(8,128)(2,1)}), bf16[16,112,512]{2,1,0:T(8,128)(2,1)S(1)}, u32[]{:S(2)}, u32[]{:S(2)}) async-start(bf16[16,112,512]{2,1,0:T(8,128)(2,1)} %broadcast_in_dim.137), calls=%async_computation.1 | async-start | bytes 3670016 | tf_op jit(solution)/shard_map/all_to_all | solution.py:22
  41.5 21.4 %all-to-all-done.1 = bf16[16,112,512]{2,1,0:T(8,128)(2,1)S(1)} async-done(((bf16[16,112,512]{2,1,0:T(8,128)(2,1)}), bf16[16,112,512]{2,1,0:T(8,128)(2,1)S(1)}, u32[]{:S(2)}, u32[]{:S(2)}) %all-to-all-start.1) | async-done | bytes 1835040 | tf_op jit(solution)/shard_map/all_to_all | solution.py:22
  63.7 2.0 slice_convert_fusion
  65.7 3.7 %fusion.120 = (bf16[8,2,88,384]{3,2,1,0:T(8,128)(2,1)}, bf16[8,2,88,384]{3,2,1,0:T(8,128)(2,1)}, bf16[8,2,88,384]{3,2,1,0:T(8,128)(2,1)}) fusion(bf16[8,6,88,384]{3,2,1,0:T(8,128)(2,1)} %bitcast.139), kind=kLoop, calls=%fused_computation.263 | loop fusion | bytes 6488064 | tf_op jit(solution)/shard_map/slice | solution.py:180
  69.4 5.2 %all-to-all-start.2 = ((bf16[16,88,384]{2,1,0:T(8,128)(2,1)}), bf16[16,88,384]{2,1,0:T(8,128)(2,1)S(1)}, u32[]{:S(2)}, u32[]{:S(2)}) async-start(bf16[16,88,384]{2,1,0:T(8,128)(2,1)} %bitcast.33), calls=%async_computation.2 | async-start | bytes 2162688 | tf_op jit(solution)/shard_map/all_to_all | solution.py:28
  74.6 2.2 %fusion.1 = bf16[1408,512]{1,0:T(8,128)(2,1)S(1)} fusion(f32[16,88,512]{2,1,0:T(8,128)} %slice_convert_fusion, f32[1408]{0:T(1024)S(1)} %reshape.657, f32[512]{0:T(512)S(1)} %add_rsqrt_fusion.1), kind=kLoop, calls=%fused_computation.2 | loop fusion | flops 2162688 | bytes 4333056 | tf_op jit(solution)/shard_map/convert_element_type | solution.py:217
  77.4 13.2 %all-to-all-done.2 = bf16[16,88,384]{2,1,0:T(8,128)(2,1)S(1)} async-done(((bf16[16,88,384]{2,1,0:T(8,128)(2,1)}), bf16[16,88,384]{2,1,0:T(8,128)(2,1)S(1)}, u32[]{:S(2)}, u32[]{:S(2)}) %all-to-all-start.2) | async-done | bytes 1081376 | tf_op jit(solution)/shard_map/all_to_all | solution.py:28
  91.4 3.4 %all-to-all-start.3 = ((bf16[8,128,176]{1,2,0:T(8,128)(2,1)}), bf16[8,128,176]{1,2,0:T(8,128)(2,1)S(1)}, u32[]{:S(2)}, u32[]{:S(2)}) async-start(bf16[8,128,176]{1,2,0:T(8,128)(2,1)} %broadcast_in_dim.144), calls=%async_computation.3 | async-start | bytes 720896 | tf_op jit(solution)/shard_map/all_to_all | solution.py:22
  96.5 2.7 %collective-permute-start = (bf16[184,512]{1,0:T(8,128)(2,1)S(1)}, bf16[184,512]{1,0:T(8,128)(2,1)S(1)}, u32[]{:S(2)}, u32[]{:S(2)}) collective-permute-start(bf16[184,512]{1,0:T(8,128)(2,1)S(1)} %fusion.40), channel_id=1, source_target_pairs={{0,1},{1,0},{2,3},{3,2},{4,5},{5,4},{6,7},{7,6},{8,9},{9,8},{10,11... | collective-permute-start | bytes 565256 | tf_op jit(solution)/shard_map/ppermute | solution.py:252
  100.0 3.5 %collective-permute-done = bf16[184,512]{1,0:T(8,128)(2,1)S(1)} collective-permute-done((bf16[184,512]{1,0:T(8,128)(2,1)S(1)}, bf16[184,512]{1,0:T(8,128)(2,1)S(1)}, u32[]{:S(2)}, u32[]{:S(2)}) %collective-permute-start) | collective-permute-done | bytes 188448 | tf_op jit(solution)/shard_map/ppermute | solution.py:252
  103.5 0.8 maximum_select_fusion
  104.3 4.0 %all-to-all-done.3 = bf16[8,128,176]{1,2,0:T(8,128)(2,1)S(1)} async-done(((bf16[8,128,176]{1,2,0:T(8,128)(2,1)}), bf16[8,128,176]{1,2,0:T(8,128)(2,1)S(1)}, u32[]{:S(2)}, u32[]{:S(2)}) %all-to-all-start.3) | async-done | bytes 360480 | tf_op jit(solution)/shard_map/all_to_all | solution.py:22
  110.4 5.3 %all-to-all-start.4 = ((bf16[16,88,128]{2,1,0:T(8,128)(2,1)}), bf16[16,88,128]{2,1,0:T(8,128)(2,1)S(1)}, u32[]{:S(2)}, u32[]{:S(2)}) async-start(bf16[16,88,128]{2,1,0:T(8,128)(2,1)} %broadcast_in_dim.147), calls=%async_computation.4 | async-start | bytes 720896 | tf_op jit(solution)/shard_map/all_to_all | solution.py:22
  116.0 8.0 %all-to-all-done.4 = bf16[16,88,128]{2,1,0:T(8,128)(2,1)S(1)} async-done(((bf16[16,88,128]{2,1,0:T(8,128)(2,1)}), bf16[16,88,128]{2,1,0:T(8,128)(2,1)S(1)}, u32[]{:S(2)}, u32[]{:S(2)}) %all-to-all-start.4) | async-done | bytes 360480 | tf_op jit(solution)/shard_map/all_to_all | solution.py:22
  125.2 3.9 %all-to-all-start.5 = ((bf16[16,88,128]{2,1,0:T(8,128)(2,1)}), bf16[16,88,128]{2,1,0:T(8,128)(2,1)S(1)}, u32[]{:S(2)}, u32[]{:S(2)}) async-start(bf16[16,88,128]{2,1,0:T(8,128)(2,1)} %broadcast_in_dim.242), calls=%async_computation.5 | async-start | bytes 720896 | tf_op jit(solution)/shard_map/all_to_all | solution.py:22
  129.3 8.2 %all-to-all-done.5 = bf16[16,88,128]{2,1,0:T(8,128)(2,1)S(1)} async-done(((bf16[16,88,128]{2,1,0:T(8,128)(2,1)}), bf16[16,88,128]{2,1,0:T(8,128)(2,1)S(1)}, u32[]{:S(2)}, u32[]{:S(2)}) %all-to-all-start.5) | async-done | bytes 360480 | tf_op jit(solution)/shard_map/all_to_all | solution.py:22
  138.7 4.0 %all-to-all-start.6 = ((bf16[16,32,88]{2,1,0:T(8,128)(2,1)}), bf16[16,32,88]{2,1,0:T(8,128)(2,1)S(1)}, u32[]{:S(2)}, u32[]{:S(2)}) async-start(bf16[16,32,88]{2,1,0:T(8,128)(2,1)} %broadcast_in_dim.243), calls=%async_computation.6 | async-start | bytes 262144 | tf_op jit(solution)/shard_map/all_to_all | solution.py:22
  146.0 2.9 %all-to-all-done.6 = bf16[16,32,88]{2,1,0:T(8,128)(2,1)S(1)} async-done(((bf16[16,32,88]{2,1,0:T(8,128)(2,1)}), bf16[16,32,88]{2,1,0:T(8,128)(2,1)S(1)}, u32[]{:S(2)}, u32[]{:S(2)}) %all-to-all-start.6) | async-done | bytes 90144 | tf_op jit(solution)/shard_map/all_to_all | solution.py:22
  150.7 5.3 %all-to-all-start.7 = ((bf16[16,32,362]{2,1,0:T(8,128)(2,1)}), bf16[16,32,362]{2,1,0:T(8,128)(2,1)S(1)}, u32[]{:S(2)}, u32[]{:S(2)}) async-start(bf16[16,32,362]{2,1,0:T(8,128)(2,1)} %broadcast_in_dim.246), calls=%async_computation.7 | async-start | bytes 786432 | tf_op jit(solution)/shard_map/all_to_all | solution.py:22
  156.5 14.6 %all-to-all-done.7 = bf16[16,32,362]{2,1,0:T(8,128)(2,1)S(1)} async-done(((bf16[16,32,362]{2,1,0:T(8,128)(2,1)}), bf16[16,32,362]{2,1,0:T(8,128)(2,1)S(1)}, u32[]{:S(2)}, u32[]{:S(2)}) %all-to-all-start.7) | async-done | bytes 370720 | tf_op jit(solution)/shard_map/all_to_all | solution.py:22
  171.7 0.9 fusion.43
  173.0 1.8 copy-done
  174.8 2.7 %decoder_attention.1 = bf16[88,512]{1,0:T(8,128)(2,1)S(1)} custom-call(s32[2]{0:T(128)S(1)} %pad_add_fusion.1.bounds_ref, bf16[96,512]{1,0:T(8,128)(2,1)S(1)} %maximum_maximum_fusion.q_ref, bf16[8,2,184,512]{3,2,1,0:T(8,128)(2,1)S(1)} %bitcast.133, bf16[184,512]{1,0:T(8,128)(2,1)S(1)} %copy.73.image_kv_ref, s32[512,1]{1,0:T(8,128)S(1)} %slice_add_fusion.image_pos_ref, ...), custom_call_target="tpu_custom_call" | custom-call | tf_op jit(solution)/shard_map/decoder_attention/pallas_call | solution.py:129
  177.7 25.1 %all_to_all.45 = bf16[16,88,512]{2,1,0:T(8,128)(2,1)S(1)} all-to-all(bf16[16,88,512]{2,1,0:T(8,128)(2,1)S(1)} %broadcast_in_dim.253), channel_id=1, replica_groups=mesh['row'=16,'col'=8,'grp'=2] {'row'}, dimensions={0} | all-to-all | bytes 2883584 | tf_op jit(solution)/shard_map/all_to_all | solution.py:22
  202.8 2.2 %fusion.5 = bf16[1,512,88]{1,2,0:T(8,128)(2,1)} fusion(bf16[1408,512]{1,0:T(8,128)(2,1)S(1)} %bitcast.137, bf16[1408,384]{1,0:T(8,128)(2,1)} %bitcast.147, f32[362,512]{1,0:T(8,128)S(1)} %fusion.16, pred[512]{0:T(512)(128)(4,1)S(1)} %fusion.66, bf16[1,512,88]{1,2,0:T(8,128)(2,1)S(1)} %copy-done.5), kind=kOutput, calls=%fused_computation.12 | convolution fusion | flops 127057920 | bytes 2163200 | tf_op jit(solution)/shard_map/dot_general | solution.py:32
  (158 shorter events, 19.2 us)
Async XLA Ops:
  6.5 6.1 %copy-start.16 = (bf16[176]{0:T(256)(128)(2,1)S(1)}, bf16[176]{0:T(256)(128)(2,1)}, u32[]{:S(2)}) copy-start(bf16[176]{0:T(256)(128)(2,1)} %param.17) | copy-start | bytes 1060
  6.5 6.2 %copy-start.17 = (bf16[176]{0:T(256)(128)(2,1)S(1)}, bf16[176]{0:T(256)(128)(2,1)}, u32[]{:S(2)}) copy-start(bf16[176]{0:T(256)(128)(2,1)} %param.18) | copy-start | bytes 1060
  6.5 6.2 %copy-start.18 = (bf16[176]{0:T(256)(128)(2,1)S(1)}, bf16[176]{0:T(256)(128)(2,1)}, u32[]{:S(2)}) copy-start(bf16[176]{0:T(256)(128)(2,1)} %param.22) | copy-start | bytes 1060
  6.5 6.2 %copy-start.6 = (bf16[1,64,176]{2,1,0:T(8,128)(2,1)S(1)}, bf16[1,64,176]{2,1,0:T(8,128)(2,1)}, u32[]{:S(2)}) copy-start(bf16[1,64,176]{2,1,0:T(8,128)(2,1)} %param.16) | copy-start | bytes 67588
  6.5 59.1 %all-gather.5.cloned.1.call-start = ((), (), s32[]{:S(2)}) async-start(), calls=%async_computation.9 | async-start | bytes 3649536 | tf_op jit(solution)/shard_map/all_gather | solution.py:177
  7.5 15.0 %copy-start.14 = (bf16[88]{0:T(256)(128)(2,1)S(1)}, bf16[88]{0:T(256)(128)(2,1)}, u32[]{:S(2)}) copy-start(bf16[88]{0:T(256)(128)(2,1)} %param.26) | copy-start | bytes 532
  7.5 15.0 %copy-start.15 = (s32[1,8]{1,0:T(1,128)S(1)}, s32[1,8]{1,0:T(1,128)}, u32[]{:S(2)}) copy-start(s32[1,8]{1,0:T(1,128)} %param.29) | copy-start | bytes 100
  7.5 15.1 %copy-start.19 = (s32[1,9]{1,0:T(1,128)S(1)}, s32[1,9]{1,0:T(1,128)}, u32[]{:S(2)}) copy-start(s32[1,9]{1,0:T(1,128)} %param.30) | copy-start | bytes 112
  8.6 21.3 %copy-start.5 = (bf16[1,512,88]{1,2,0:T(8,128)(2,1)S(1)}, bf16[1,512,88]{1,2,0:T(8,128)(2,1)}, u32[]{:S(2)}) copy-start(bf16[1,512,88]{1,2,0:T(8,128)(2,1)} %param.25) | copy-start | bytes 270340
  13.4 16.3 %all-to-all-start = ((bf16[8,16,176]{2,1,0:T(8,128)(2,1)}), bf16[8,16,176]{2,1,0:T(8,128)(2,1)S(1)}, u32[]{:S(2)}, u32[]{:S(2)}) async-start(bf16[8,16,176]{2,1,0:T(8,128)(2,1)} %pad_maximum_fusion.5), calls=%async_computation | async-start | bytes 131072 | tf_op jit(solution)/shard_map/all_to_all | solution.py:28
  22.7 16.1 %copy-start.7 = (s32[8]{0:T(128)}, s32[8]{0:T(128)S(1)}, u32[]{:S(2)}) copy-start(s32[8]{0:T(128)S(1)} %get-tuple-element.20) | copy-start | bytes 100
  31.3 7.6 %copy-start.13 = (bf16[264]{0:T(512)(128)(2,1)S(1)}, bf16[264]{0:T(512)(128)(2,1)}, u32[]{:S(2)}) copy-start(bf16[264]{0:T(512)(128)(2,1)} %param.20) | copy-start | bytes 1588
  31.3 31.7 %all-to-all-start.1 = ((bf16[16,112,512]{2,1,0:T(8,128)(2,1)}), bf16[16,112,512]{2,1,0:T(8,128)(2,1)S(1)}, u32[]{:S(2)}, u32[]{:S(2)}) async-start(bf16[16,112,512]{2,1,0:T(8,128)(2,1)} %broadcast_in_dim.137), calls=%async_computation.1 | async-start | bytes 3670016 | tf_op jit(solution)/shard_map/all_to_all | solution.py:22
  39.6 1.1 copy-start.10
  69.4 21.2 %all-to-all-start.2 = ((bf16[16,88,384]{2,1,0:T(8,128)(2,1)}), bf16[16,88,384]{2,1,0:T(8,128)(2,1)S(1)}, u32[]{:S(2)}, u32[]{:S(2)}) async-start(bf16[16,88,384]{2,1,0:T(8,128)(2,1)} %bitcast.33), calls=%async_computation.2 | async-start | bytes 2162688 | tf_op jit(solution)/shard_map/all_to_all | solution.py:28
  74.6 2.2 %copy-start.2 = (bf16[8,2,88,384]{3,2,1,0:T(8,128)(2,1)S(1)}, bf16[8,2,88,384]{3,2,1,0:T(8,128)(2,1)}, u32[]{:S(2)}) copy-start(bf16[8,2,88,384]{3,2,1,0:T(8,128)(2,1)} %get-tuple-element.23) | copy-start | bytes 3244036
  74.6 2.2 %copy-start.9 = (f32[264]{0:T(512)S(1)}, f32[264]{0:T(512)}, u32[]{:S(2)}) copy-start(f32[264]{0:T(512)} %convert_element_type.147) | copy-start | bytes 3172
  91.4 16.9 %all-to-all-start.3 = ((bf16[8,128,176]{1,2,0:T(8,128)(2,1)}), bf16[8,128,176]{1,2,0:T(8,128)(2,1)S(1)}, u32[]{:S(2)}, u32[]{:S(2)}) async-start(bf16[8,128,176]{1,2,0:T(8,128)(2,1)} %broadcast_in_dim.144), calls=%async_computation.3 | async-start | bytes 720896 | tf_op jit(solution)/shard_map/all_to_all | solution.py:22
  94.8 78.1 %all-gather.7.cloned.1.call-start = ((), (), s32[]{:S(2)}) async-start(), calls=%async_computation.10 | async-start | bytes 3391488 | tf_op jit(solution)/shard_map/all_gather | solution.py:255
  95.7 0.8 copy-start.3
  96.5 11.9 %copy-start.12 = (s32[128]{0:T(128)S(1)}, s32[128]{0:T(128)}, u32[]{:S(2)}) copy-start(s32[128]{0:T(128)} %convert_reduce_fusion.2) | copy-start | bytes 1540
  96.5 7.0 %collective-permute-start = (bf16[184,512]{1,0:T(8,128)(2,1)S(1)}, bf16[184,512]{1,0:T(8,128)(2,1)S(1)}, u32[]{:S(2)}, u32[]{:S(2)}) collective-permute-start(bf16[184,512]{1,0:T(8,128)(2,1)S(1)} %fusion.40), channel_id=1, source_target_pairs={{0,1},{1,0},{2,3},{3,2},{4,5},{5,4},{6,7},{7,6},{8,9},{9,8},{10,11... | collective-permute-start | bytes 565256 | tf_op jit(solution)/shard_map/ppermute | solution.py:252
  110.4 13.6 %all-to-all-start.4 = ((bf16[16,88,128]{2,1,0:T(8,128)(2,1)}), bf16[16,88,128]{2,1,0:T(8,128)(2,1)S(1)}, u32[]{:S(2)}, u32[]{:S(2)}) async-start(bf16[16,88,128]{2,1,0:T(8,128)(2,1)} %broadcast_in_dim.147), calls=%async_computation.4 | async-start | bytes 720896 | tf_op jit(solution)/shard_map/all_to_all | solution.py:22
  115.7 13.5 %copy-start.20 = (bf16[88]{0:T(256)(128)(2,1)S(1)}, bf16[88]{0:T(256)(128)(2,1)}, u32[]{:S(2)}) copy-start(bf16[88]{0:T(256)(128)(2,1)} %param.24) | copy-start | bytes 532
  115.7 13.5 %copy-start.21 = (s32[4]{0:T(128)S(1)}, s32[4]{0:T(128)}, u32[]{:S(2)}) copy-start(s32[4]{0:T(128)} %param.31) | copy-start | bytes 52
  115.7 21.8 %copy-start.1 = (bf16[8,2,88,384]{3,2,1,0:T(8,128)(2,1)S(1)}, bf16[8,2,88,384]{3,2,1,0:T(8,128)(2,1)}, u32[]{:S(2)}) copy-start(bf16[8,2,88,384]{3,2,1,0:T(8,128)(2,1)} %get-tuple-element.22) | copy-start | bytes 3244036
  125.2 12.3 %all-to-all-start.5 = ((bf16[16,88,128]{2,1,0:T(8,128)(2,1)}), bf16[16,88,128]{2,1,0:T(8,128)(2,1)S(1)}, u32[]{:S(2)}, u32[]{:S(2)}) async-start(bf16[16,88,128]{2,1,0:T(8,128)(2,1)} %broadcast_in_dim.242), calls=%async_computation.5 | async-start | bytes 720896 | tf_op jit(solution)/shard_map/all_to_all | solution.py:22
  138.7 10.2 %all-to-all-start.6 = ((bf16[16,32,88]{2,1,0:T(8,128)(2,1)}), bf16[16,32,88]{2,1,0:T(8,128)(2,1)S(1)}, u32[]{:S(2)}, u32[]{:S(2)}) async-start(bf16[16,32,88]{2,1,0:T(8,128)(2,1)} %broadcast_in_dim.243), calls=%async_computation.6 | async-start | bytes 262144 | tf_op jit(solution)/shard_map/all_to_all | solution.py:22
  149.2 7.1 %copy-start.8 = (s32[8]{0:T(128)S(1)}, s32[8]{0:T(128)}, u32[]{:S(2)}) copy-start(s32[8]{0:T(128)} %copy-done.7) | copy-start | bytes 100
  149.3 7.1 %copy-start.11 = (s32[8]{0:T(128)S(1)}, s32[8]{0:T(128)}, u32[]{:S(2)}) copy-start(s32[8]{0:T(128)} %copy-done.10) | copy-start | bytes 100
  150.7 20.3 %all-to-all-start.7 = ((bf16[16,32,362]{2,1,0:T(8,128)(2,1)}), bf16[16,32,362]{2,1,0:T(8,128)(2,1)S(1)}, u32[]{:S(2)}, u32[]{:S(2)}) async-start(bf16[16,32,362]{2,1,0:T(8,128)(2,1)} %broadcast_in_dim.246), calls=%async_computation.7 | async-start | bytes 786432 | tf_op jit(solution)/shard_map/all_to_all | solution.py:22
  173.0 1.9 copy-start
  (1 other events, 0.8 us)
Sparse Core Ops, SparseCore 0:
  12.8 49.6 all-gather.4
  108.5 39.8 all-gather.6

commit v3 on v2

v3 whole, which is shorter than its diff:
```python
import functools

import jax
import jax.numpy as jnp
from jax import lax
from jax.experimental import pallas as pl
from jax.experimental.pallas import tpu as pltpu
from jax.sharding import PartitionSpec as P

HEADS = 16
HEAD_DIM = 88
WIDTH = HEADS * HEAD_DIM
TPD = 256
LOG2E = 1.4426950408889634
NEG = -1e30
F32 = jnp.float32
BF16 = jnp.bfloat16


def spread(values, axes):
    count = lax.axis_size(axes)
    return lax.all_to_all(
        jnp.broadcast_to(values[None], (count,) + values.shape), axes, split_axis=0, concat_axis=0
    )


def exchange(values, axes):
    return lax.all_to_all(values, axes, split_axis=0, concat_axis=0)


def dot0(left, right):
    return lax.dot_general(left, right, (((0,), (0,)), ((), ())), preferred_element_type=F32)


def running(lengths):
    at = jnp.arange(lengths.shape[0], dtype=jnp.int32)
    return jnp.sum(
        jnp.where(at[None, :] <= at[:, None], lengths[None, :], 0), axis=1, dtype=jnp.int32
    )


def segment_of(index_values, lengths):
    ends = running(lengths)
    return jnp.sum(
        (index_values[:, None] >= ends[None, :]).astype(jnp.int32), axis=1, dtype=jnp.int32
    )


def image_starts(lengths, gaps):
    offsets = running(lengths) - lengths
    return running(gaps)[: lengths.shape[0]] + offsets, offsets


def insert_map(text_rows, lengths, gaps):
    starts, offsets = image_starts(lengths, gaps)
    inside = (text_rows[:, None] >= starts[None, :]) & (
        text_rows[:, None] < (starts + lengths)[None, :]
    )
    source = jnp.sum(
        jnp.where(inside, offsets[None, :] + text_rows[:, None] - starts[None, :], 0),
        axis=1,
        dtype=jnp.int32,
    )
    return source, jnp.any(inside, axis=1)


def rows_of_merged(merged, lengths, gaps):
    starts, offsets = image_starts(lengths, gaps)
    inside = (merged[:, None] >= offsets[None, :]) & (
        merged[:, None] < (offsets + lengths)[None, :]
    )
    return jnp.sum(
        jnp.where(inside, starts[None, :] + merged[:, None] - offsets[None, :], 0),
        axis=1,
        dtype=jnp.int32,
    )


def sequence_position(rows, half):
    return (rows // TPD) * (2 * TPD) + half * TPD + rows % TPD


def fold_block(state, query, keys, values, key_pos, low, span, chosen=None):
    best, total, mixed = state
    factor = LOG2E * HEAD_DIM ** (-0.5)
    scores = dot0(keys, query)
    offset = key_pos - low
    allowed = (offset >= 0) & (offset <= span)
    if chosen is not None:
        allowed = allowed & chosen
    scores = jnp.where(allowed, scores, NEG)
    new_best = jnp.maximum(best, jnp.max(scores, axis=0, keepdims=True))
    weights = jnp.exp2((scores - new_best) * factor)
    keep = jnp.exp2((best - new_best) * factor)
    total = total * keep + jnp.sum(weights, axis=0, keepdims=True)
    added = jnp.dot(values, weights.astype(BF16), preferred_element_type=F32)
    return new_best, total, mixed * keep + added


def fold_text(bounds_ref, kv_ref, state, query, low, span, chosen=None):
    block = kv_ref.shape[3]
    key_rows = query.shape[0]
    step = lax.broadcasted_iota(jnp.int32, (block, 1), 0)
    in_pair = jnp.where(step >= TPD, step + TPD, step)

    def chunk(index, state):
        for half in range(2):
            keys = kv_ref[index, half, :key_rows]
            values = kv_ref[index, half, key_rows:]
            key_pos = in_pair + (index * (2 * block) + half * TPD)
            state = fold_block(state, query, keys, values, key_pos, low, span, chosen)
        return state

    return lax.fori_loop(bounds_ref[0], bounds_ref[1], chunk, state)


def text_kernel(bounds_ref, q_ref, kv_ref, qpos_ref, mix_ref, stat_ref):
    count = q_ref.shape[1]
    state = (
        jnp.full((1, count), NEG, F32),
        jnp.zeros((1, count), F32),
        jnp.zeros((HEAD_DIM, count), F32),
    )
    best, total, mixed = fold_text(
        bounds_ref, kv_ref, state, q_ref[...], qpos_ref[0:1, :], qpos_ref[1:2, :]
    )
    stat_ref[0:1, :] = best
    stat_ref[1:2, :] = total
    mix_ref[...] = mixed


KEY_AT = HEAD_DIM
VALUE_AT = 2 * HEAD_DIM + 8
INPUT_AT = VALUE_AT + HEAD_DIM
PLACE_AT = INPUT_AT + HEAD_DIM


def image_kernel(
    bounds_ref,
    busy_ref,
    shared_ref,
    text_ref,
    text_q_ref,
    kv_ref,
    qpos_ref,
    text_mix_ref,
    text_stat_ref,
    out_ref,
    input_ref,
    query_ref,
    mix_ref,
    stat_ref,
):
    shared = shared_ref[...]
    slot = qpos_ref[2:3, :]
    is_image = slot >= 0
    low, span = qpos_ref[0:1, :], qpos_ref[1:2, :]
    item = lax.broadcasted_iota(jnp.int32, (shared.shape[0], 1), 0)
    placed = dot0(shared, jnp.where(item == slot, 1.0, 0.0).astype(BF16))
    input_ref[...] = jnp.where(
        is_image, placed[INPUT_AT:PLACE_AT], text_ref[...].astype(F32)
    ).astype(BF16)
    query = jnp.where(is_image, placed[:HEAD_DIM].astype(BF16), text_q_ref[:HEAD_DIM])
    query_ref[:HEAD_DIM] = query
    query_ref[HEAD_DIM:] = text_q_ref[HEAD_DIM:]
    place = shared[:, PLACE_AT : PLACE_AT + 2].astype(F32).astype(jnp.int32)
    key_pos = place[:, :1] * 64 + place[:, 1:]
    keys = shared[:, KEY_AT : KEY_AT + HEAD_DIM]
    scores = jnp.dot(keys, query, preferred_element_type=F32)
    factor = LOG2E * HEAD_DIM ** (-0.5)
    offset = key_pos - low
    scores = jnp.where((offset >= 0) & (offset <= span), scores, NEG)
    best = jnp.where(is_image, NEG, text_stat_ref[0:1, :])
    new_best = jnp.maximum(best, jnp.max(scores, axis=0, keepdims=True))
    weights = jnp.exp2((scores - new_best) * factor)
    keep = jnp.where(is_image, 0.0, jnp.exp2((best - new_best) * factor))
    stat_ref[0:1, :] = new_best
    stat_ref[1:2, :] = text_stat_ref[1:2, :] * keep + jnp.sum(weights, axis=0, keepdims=True)
    added = dot0(shared, weights.astype(BF16))[VALUE_AT:INPUT_AT]
    mix_ref[...] = text_mix_ref[...] * keep + added
    tiles = busy_ref.shape[0]
    width = slot.shape[1] // tiles
    for tile in range(tiles):
        lanes = slice(tile * width, (tile + 1) * width)

        @pl.when(busy_ref[tile] > 0)
        def _():
            best, total, mixed = fold_text(
                bounds_ref,
                kv_ref,
                (stat_ref[0:1, lanes], stat_ref[1:2, lanes], mix_ref[:, lanes]),
                query_ref[:, lanes],
                qpos_ref[0:1, lanes],
                qpos_ref[1:2, lanes],
                qpos_ref[2:3, lanes] >= 0,
            )
            stat_ref[0:1, lanes] = best
            stat_ref[1:2, lanes] = total
            mix_ref[:, lanes] = mixed

    out_ref[...] = (mix_ref[...] / stat_ref[1:2, :]).astype(BF16)


def attention_params():
    return pltpu.CompilerParams(vmem_limit_bytes=24 * 1024 * 1024)


def text_attention(bounds, query, keyval, qpos):
    vmem = pl.BlockSpec(memory_space=pltpu.VMEM)
    count = query.shape[1]
    pairs = count * keyval.shape[0] * keyval.shape[1] * keyval.shape[3]
    return pl.pallas_call(
        text_kernel,
        out_shape=(
            jax.ShapeDtypeStruct((HEAD_DIM, count), F32),
            jax.ShapeDtypeStruct((8, count), F32),
        ),
        in_specs=[pl.BlockSpec(memory_space=pltpu.SMEM)] + [vmem] * 3,
        out_specs=(vmem, vmem),
        compiler_params=attention_params(),
        cost_estimate=pl.CostEstimate(
            flops=4 * HEAD_DIM * pairs, bytes_accessed=2 * keyval.size, transcendentals=pairs
        ),
        name="text_attention",
    )(bounds, query, keyval, qpos)


def image_attention(bounds, busy, shared, text, text_query, keyval, qpos, mixed, stats):
    vmem = pl.BlockSpec(memory_space=pltpu.VMEM)
    count = text.shape[1]
    return pl.pallas_call(
        image_kernel,
        out_shape=(
            jax.ShapeDtypeStruct((HEAD_DIM, count), BF16),
            jax.ShapeDtypeStruct((HEAD_DIM, count), BF16),
        ),
        in_specs=[pl.BlockSpec(memory_space=pltpu.SMEM)] * 2 + [vmem] * 7,
        out_specs=(vmem, vmem),
        scratch_shapes=[
            pltpu.VMEM(text_query.shape, BF16),
            pltpu.VMEM((HEAD_DIM, count), F32),
            pltpu.VMEM((8, count), F32),
        ],
        compiler_params=attention_params(),
        name="image_attention",
    )(bounds, busy, shared, text, text_query, keyval, qpos, mixed, stats)


def vision_kernel(part, pitch, ends_ref, q_ref, kv_ref, marks_ref, out_ref):
    keyval = kv_ref[...]
    scores = lax.dot_general(
        keyval, q_ref[...], (((1,), (1,)), ((), ())), preferred_element_type=F32
    ) * (HEAD_DIM ** (-0.5))
    count = q_ref.shape[0]
    item = lax.broadcasted_iota(jnp.int32, (keyval.shape[0], 1), 0)
    inner = item % count
    merged = (inner // part * pitch + item // count * part + inner % part) // 4
    marks = jnp.zeros_like(merged)
    for index in range(ends_ref.shape[0]):
        marks = marks + (merged >= ends_ref[index]).astype(jnp.int32)
    allowed = marks == marks_ref[...]
    scores = jnp.where(allowed, scores, NEG)
    best = jnp.max(scores, axis=0, keepdims=True)
    weights = jnp.where(allowed, jnp.exp(scores - best), 0.0)
    total = jnp.sum(weights, axis=0, keepdims=True)
    mixed = dot0(keyval, weights.astype(BF16))[HEAD_DIM:]
    out_ref[...] = jnp.broadcast_to((mixed / total).astype(BF16)[None], out_ref.shape)


def vision_attention(part, pitch, copies, ends, query, keyval, marks):
    vmem = pl.BlockSpec(memory_space=pltpu.VMEM)
    return pl.pallas_call(
        functools.partial(vision_kernel, part, pitch),
        out_shape=jax.ShapeDtypeStruct((copies, HEAD_DIM, query.shape[0]), BF16),
        in_specs=[pl.BlockSpec(memory_space=pltpu.SMEM)] + [vmem] * 3,
        out_specs=vmem,
        compiler_params=pltpu.CompilerParams(vmem_limit_bytes=16 * 1024 * 1024),
        name="vision_attention",
    )(ends, query, keyval, marks)


def per_device(
    patches,
    vis_gain,
    vis_bias,
    vis_qkv,
    vis_qkv_bias,
    vis_out,
    vis_out_bias,
    proj_weight,
    proj_bias,
    text_embeds,
    dec_gain,
    dec_qkv,
    dec_out,
    image_tokens,
    text_gaps,
    doc_lengths,
):
    cols = lax.axis_size("col")
    rows = lax.axis_size("row")
    row = lax.axis_index("row")
    col = lax.axis_index("col")
    half = lax.axis_index("grp")

    feat_c = vis_out.shape[1]
    vis_n = vis_qkv.shape[1]
    unit = -(-(vis_n + HEAD_DIM) // 128) * 128
    fill = jnp.zeros((HEAD_DIM, unit - vis_n - HEAD_DIM), BF16)
    sides = (slice(0, HEAD_DIM), slice(HEAD_DIM, 2 * HEAD_DIM))
    units = [
        [dec_qkv[:, at * vis_n : (at + 1) * vis_n], vis_out[:, side], fill]
        for at, side in enumerate(sides)
    ]
    units += [[vis_qkv[side], dec_out[side], fill] for side in sides]
    units += [[proj_weight[window, side] for window in range(4)] + [fill] for side in sides]
    packed = jnp.stack([jnp.concatenate(pieces, axis=1) for pieces in units])
    gathered_w = lax.all_gather(packed, "col", axis=0)

    def pair(number):
        return lax.slice_in_dim(gathered_w, 2 * number, 2 * number + 2, axis=1)

    rows_b = patches.shape[1]
    part = rows_b // cols
    affine_own = jnp.stack([vis_gain, vis_bias, vis_out_bias])
    affine_own = jnp.pad(affine_own, ((0, 8 - affine_own.shape[0]), (0, 0)))
    mine = exchange(
        jnp.concatenate(
            [
                patches[0].reshape(cols, part, feat_c),
                jnp.broadcast_to(affine_own[None], (cols, 8, feat_c)),
            ],
            axis=1,
        ),
        "col",
    )
    mine = jnp.transpose(mine, (1, 0, 2)).reshape(part + 8, WIDTH)
    affine = mine[part : part + 3].astype(F32)

    text = text_embeds[0].T
    positions = text.shape[1]
    folds = -(-(WIDTH + HEAD_DIM) // positions)
    spare = folds * positions - WIDTH
    gain = jnp.broadcast_to(jnp.pad(dec_gain, (0, spare - HEAD_DIM))[None], (part, spare))
    folded = jnp.concatenate([mine[:part], gain], axis=1)
    folded = jnp.transpose(folded.reshape(part, folds, positions), (1, 0, 2))
    both = spread(
        jnp.concatenate([text, folded.reshape(folds * part, positions)], axis=0), "row"
    )
    text_all = both[:, :HEAD_DIM].reshape(WIDTH, positions)
    raw = jnp.transpose(
        both[:, HEAD_DIM:].reshape(rows, folds, part, positions), (0, 2, 1, 3)
    ).reshape(rows, part, folds * positions)
    gain_all = raw[:, 0, WIDTH : WIDTH + HEAD_DIM].reshape(WIDTH, 1).astype(F32)
    raw = raw[:, :, :WIDTH].reshape(rows * part, WIDTH)

    row_pack, gathered_w = lax.optimization_barrier((pair(0), gathered_w))
    row_w = exchange(row_pack.reshape(rows, HEAD_DIM, unit), "row").reshape(WIDTH, unit)

    vis_w = pair(1).reshape(WIDTH, unit)
    xfull = raw.astype(F32)
    mean = jnp.sum(xfull, axis=1, keepdims=True) / WIDTH
    variance = jnp.sum(xfull * xfull, axis=1, keepdims=True) / WIDTH - mean * mean
    normed = (
        (xfull - mean) * lax.rsqrt(variance + 1e-06) * affine[0:1] + affine[1:2]
    ).astype(BF16)
    qkv_rows = (
        jnp.dot(normed, vis_w, preferred_element_type=F32)[:, :vis_n]
        + vis_qkv_bias.astype(F32)
    ).astype(BF16)
    text_all, qkv_rows = lax.optimization_barrier((text_all, qkv_rows))
    xtext = text_all.astype(F32)
    squares = jnp.sum(xtext * xtext, axis=0, keepdims=True)
    text_normed = (xtext * lax.rsqrt(squares / WIDTH + 1e-05) * gain_all).astype(BF16)
    count = rows * part
    query = qkv_rows[:, :HEAD_DIM]
    lengths, gaps = image_tokens[0], text_gaps[0]
    own_rows = col * positions + jnp.arange(positions, dtype=jnp.int32)
    source, inside = insert_map(own_rows, lengths, gaps)
    query_pos = sequence_position(own_rows, half)
    ends = running(doc_lengths)
    low = jnp.max(
        jnp.where(query_pos[:, None] >= ends[None, :], ends[None, :], 0), axis=1
    )
    bounds = jnp.stack([jnp.min(low) // (2 * positions), col + 1]).astype(jnp.int32)
    merged = count // 4
    pack = part // 4
    item = jnp.arange(merged, dtype=jnp.int32)
    merged_id = item // pack * (pack * cols) + col * pack + item % pack
    marks = jnp.tile(segment_of(merged_id, lengths), 4)[None]
    image_ends = running(lengths)
    place = sequence_position(rows_of_merged(merged_id, lengths, gaps), half)
    place = jnp.stack([place // 64, place % 64], axis=1).astype(BF16)
    slot = (source // pack % cols * 2 + half) * merged
    slot = slot + source // (pack * cols) * pack + source % pack
    slot = jnp.where(inside, slot, -1)
    qpos = jnp.stack([low, query_pos - low, slot])
    busy = jnp.max(inside.astype(jnp.int32).reshape(4, positions // 4), axis=1)
    bias = jnp.where(inside, NEG, 0.0).astype(BF16)[None]
    row_w, vis_kv, qpos, bounds, marks, image_ends, place, busy, bias = (
        lax.optimization_barrier(
            (
                row_w,
                qkv_rows[:, HEAD_DIM:],
                qpos,
                bounds,
                marks,
                image_ends,
                place,
                busy,
                bias,
            )
        )
    )
    keyval = spread(vis_kv, "col").reshape(cols * count, 2 * HEAD_DIM)
    proj_w = pair(2).reshape(WIDTH, unit)
    dec_out_w = vis_w[:, vis_n : vis_n + HEAD_DIM]

    text_qkv = dot0(row_w, text_normed)[:vis_n].astype(BF16)
    own_kv = jnp.concatenate(
        [
            text_qkv[HEAD_DIM : 2 * HEAD_DIM],
            jnp.pad(bias, ((0, 7), (0, 0))),
            text_qkv[2 * HEAD_DIM :],
        ],
        axis=0,
    )
    other_kv = lax.ppermute(own_kv, "grp", [(0, 1), (1, 0)])
    pair_kv = jnp.where(half == 0, jnp.stack([own_kv, other_kv]), jnp.stack([other_kv, own_kv]))
    pair_kv, keyval = lax.optimization_barrier((pair_kv, keyval))
    all_kv = lax.all_gather(pair_kv, "col", axis=0)

    def window_first(array):
        features = array.shape[1]
        return jnp.transpose(
            array.reshape(rows, part // 4, 4, features), (2, 0, 1, 3)
        ).reshape(count, features)

    query = jnp.pad(window_first(query), ((0, 0), (0, HEAD_DIM)))
    all_attn = exchange(
        vision_attention(part, rows_b, rows, image_ends, query, keyval, marks), "row"
    ).reshape(WIDTH, count)
    raw_at = row * HEAD_DIM
    own_raw = window_first(lax.dynamic_slice(raw, (0, raw_at), (count, HEAD_DIM)))
    own_bias = lax.dynamic_slice(affine[2], (raw_at,), (HEAD_DIM,))
    resid = (own_raw.T.astype(F32) + dot0(row_w, all_attn)[vis_n : vis_n + HEAD_DIM] + own_bias[:, None]).astype(BF16)
    all_resid = spread(resid, "row").reshape(WIDTH, count)
    windows = dot0(proj_w, all_resid)
    projected = proj_bias.astype(F32)[:, None]
    for window in range(4):
        projected = projected + windows[
            window * HEAD_DIM : (window + 1) * HEAD_DIM, window * merged : (window + 1) * merged
        ]
    image_in = projected.T.astype(BF16)

    image_all = jnp.transpose(spread(image_in, "row"), (1, 0, 2)).reshape(merged, WIDTH)
    ximage = image_all.astype(F32)
    squares = jnp.sum(ximage * ximage, axis=1, keepdims=True)
    image_normed = (
        ximage * lax.rsqrt(squares / WIDTH + 1e-05) * gain_all[:, 0][None, :]
    ).astype(BF16)
    all_kv, image_normed = lax.optimization_barrier((all_kv, image_normed))
    image_qkv = jnp.dot(image_normed, row_w, preferred_element_type=F32)[:, :vis_n].astype(BF16)

    def with_mask_row(query):
        return jnp.concatenate(
            [query, jnp.ones((1, positions), BF16), jnp.zeros((7, positions), BF16)], axis=0
        )

    text_query = with_mask_row(text_qkv[:HEAD_DIM])
    mixed, stats = text_attention(bounds, text_query, all_kv, qpos)
    shared = spread(
        jnp.concatenate(
            [
                image_qkv[:, : 2 * HEAD_DIM],
                jnp.zeros((merged, 8), BF16),
                image_qkv[:, 2 * HEAD_DIM :],
                image_in,
                place,
            ],
            axis=1,
        ),
        ("col", "grp"),
    )
    shared, mixed = lax.optimization_barrier((shared, mixed))
    shared = shared.reshape(cols * 2 * merged, -1)
    dec_attn, dec_input = image_attention(
        bounds, busy, shared, text, text_query, all_kv, qpos, mixed, stats
    )

    all_dec = spread(dec_attn, "row").reshape(WIDTH, positions)
    delta = dot0(dec_out_w, all_dec)
    return (dec_input.astype(F32) + delta).astype(BF16).T[None]


def solution(mesh):
    return jax.shard_map(
        per_device,
        mesh=mesh,
        in_specs=(
            P("grp", "row", "col"),
            P("col"),
            P("col"),
            P("col", "row"),
            P("row"),
            P("row", "col"),
            P("col"),
            P(None, "col", "row"),
            P("row"),
            P("grp", "col", "row"),
            P("row"),
            P("row", "col"),
            P("col", "row"),
            P("grp", None),
            P("grp", None),
            P(),
        ),
        out_specs=P("grp", "col", "row"),
        check_vma=False,
    )
```

time: 213 us -> 213 us (level)
  other arithmetic: 11.5 us -> 4.77 us
  Pallas kernels: 2.7 us -> 8.78 us
  waiting for transfers between devices: 82.8 us -> 78 us
  starting transfers between devices: 46.5 us -> 48.8 us
    all_to_all x6 -> x5, waiting for transfers between devices: 59.1 us -> 49.8 us  [spread(): lax.all_to_all(jnp.broadcast_to(values[None], (count,) + values.shape), a...]
    all_to_all x2 -> x3, starting transfers between devices: 14.2 us -> 20.7 us  [exchange(): return lax.all_to_all(values, axes, split_axis=0, concat_axis=0)]
    pallas_call x1 -> x3, Pallas kernels: 2.7 us -> 8.78 us  [the longest x1 4 us: image_attention(): pl.pallas_call(image_kernel, out_shape=(jax.ShapeDtypeStruct((HEAD_DIM, c...]
    convert_element_type x3 -> x1, other arithmetic: 4.32 us -> 0.09 us  [per_device(): image_normed = (ximage * lax.rsqrt(squares / WIDTH + 1e-05) * gain_all[:,...]
    all_to_all x6 -> x5, starting transfers between devices: 29.5 us -> 25.3 us  [spread(): lax.all_to_all(jnp.broadcast_to(values[None], (count,) + values.shape), a...]
    all_to_all x2 -> x3, waiting for transfers between devices: 20.1 us -> 24 us  [exchange(): return lax.all_to_all(values, axes, split_axis=0, concat_axis=0)]
    unnamed x45 -> x39, local copies, waits for them, and re-layouts: 3.47 us -> 5.14 us
    slice x3 -> x7, local copies, waits for them, and re-layouts: 3.73 us -> 4.93 us  [the longest x2 4.7 us: pair(): return lax.slice_in_dim(gathered_w, 2 * number, 2 * number + 2, axis=1)]
  transfers between devices with their start and end apart: 11 -> 11, of which waited for: 9 -> 9; matrix products, arithmetic and copies ran while one was open for 11% -> 7% of each run, Pallas kernels for 0% -> 2%
where the time goes in v3:
time: 213 us; the launch traced here: 211 us
  waiting for transfers between devices  78 us (37%)
  starting transfers between devices  48.8 us (23%)
  blocking collectives  26.1 us (12%)
  local copies, waits for them, and re-layouts  22.3 us (10%)
  between operations  16.5 us (8%)
  Pallas kernels  8.78 us (4%)
  matrix products  6.15 us (3%)
  other arithmetic  4.77 us (2%)
    all_to_all x5, waiting for transfers between devices, spread(): lax.all_to_all(jnp.broadcast_to(values[None], (count,) + values.shape), a...  49.8 us
    all_to_all x1, blocking collectives, spread(): lax.all_to_all(jnp.broadcast_to(values[None], (count,) + values.shape), a...  26.1 us
    all_to_all x5, starting transfers between devices, spread(): lax.all_to_all(jnp.broadcast_to(values[None], (count,) + values.shape), a...  25.3 us
    all_to_all x3, waiting for transfers between devices, exchange(): return lax.all_to_all(values, axes, split_axis=0, concat_axis=0)  24 us
    all_to_all x3, starting transfers between devices, exchange(): return lax.all_to_all(values, axes, split_axis=0, concat_axis=0)  20.7 us
    dot_general x4, matrix products, dot0(): lax.dot_general(left, right, (((0,), (0,)), ((), ())), preferred_element_...  5.31 us
    unnamed x39, local copies, waits for them, and re-layouts  5.14 us
    slice x2, local copies, waits for them, and re-layouts, pair(): return lax.slice_in_dim(gathered_w, 2 * number, 2 * number + 2, axis=1)  4.7 us
  transfers between devices with their start and end apart: 11, of which 9 were waited for; matrix products, arithmetic and copies ran while one was open for 7% of the time, Pallas kernels for 2%

profile of v3, /device:TPU:1, one launch (start us, length us, event | category | flops | bytes accessed | tf_op | source)
XLA Modules:
  0.0 211.5 jit_solution(16924402307600140547)
XLA Ops:
  7.5 1.0 fusion.77
  9.5 0.9 fusion.76
  13.4 9.0 %all-to-all-start.1 = ((bf16[8,16,176]{2,1,0:T(8,128)(2,1)}), bf16[8,16,176]{2,1,0:T(8,128)(2,1)S(1)}, u32[]{:S(2)}, u32[]{:S(2)}) async-start(bf16[8,16,176]{2,1,0:T(8,128)(2,1)} %pad_maximum_fusion.5), calls=%async_computation.1 | async-start | bytes 131072 | tf_op jit(solution)/shard_map/all_to_all | solution.py:28
  26.3 3.4 %all-to-all-done.1 = bf16[8,16,176]{2,1,0:T(8,128)(2,1)S(1)} async-done(((bf16[8,16,176]{2,1,0:T(8,128)(2,1)}), bf16[8,16,176]{2,1,0:T(8,128)(2,1)S(1)}, u32[]{:S(2)}, u32[]{:S(2)}) %all-to-all-start.1) | async-done | bytes 45088 | tf_op jit(solution)/shard_map/all_to_all | solution.py:28
  29.8 1.4 broadcast_in_dim.113
  31.3 7.5 %all-to-all-start.2 = ((bf16[16,112,512]{2,1,0:T(8,128)(2,1)}), bf16[16,112,512]{2,1,0:T(8,128)(2,1)S(1)}, u32[]{:S(2)}, u32[]{:S(2)}) async-start(bf16[16,112,512]{2,1,0:T(8,128)(2,1)} %broadcast_in_dim.113), calls=%async_computation.2 | async-start | bytes 3670016 | tf_op jit(solution)/shard_map/all_to_all | solution.py:22
  39.7 23.3 %all-to-all-done.2 = bf16[16,112,512]{2,1,0:T(8,128)(2,1)S(1)} async-done(((bf16[16,112,512]{2,1,0:T(8,128)(2,1)}), bf16[16,112,512]{2,1,0:T(8,128)(2,1)S(1)}, u32[]{:S(2)}, u32[]{:S(2)}) %all-to-all-start.2) | async-done | bytes 1835040 | tf_op jit(solution)/shard_map/all_to_all | solution.py:22
  63.2 2.4 %slice.195 = bf16[8,2,88,384]{3,2,1,0:T(8,128)(2,1)} slice(bf16[8,6,88,384]{3,2,1,0:T(8,128)(2,1)} %bitcast.153), slice={[0:8], [0:2], [0:88], [0:384]} | slice | bytes 2162688 | tf_op jit(solution)/shard_map/slice | solution.py:321
  65.6 5.2 %all-to-all-start = ((bf16[16,88,384]{2,1,0:T(8,128)(2,1)}), bf16[16,88,384]{2,1,0:T(8,128)(2,1)S(1)}, u32[]{:S(2)}, u32[]{:S(2)}) async-start(bf16[16,88,384]{2,1,0:T(8,128)(2,1)} %bitcast.152), calls=%async_computation | async-start | bytes 2162688 | tf_op jit(solution)/shard_map/all_to_all | solution.py:28
  71.0 2.3 %fusion.74 = (bf16[8,2,88,384]{3,2,1,0:T(8,128)(2,1)S(1)}, bf16[8,2,88,384]{3,2,1,0:T(8,128)(2,1)S(1)}) fusion(bf16[8,6,88,384]{3,2,1,0:T(8,128)(2,1)} %bitcast.154), kind=kLoop, calls=%fused_computation.180 | loop fusion | bytes 4325376 | tf_op jit(solution)/shard_map/slice | solution.py:321
  74.3 12.5 %all-to-all-done = bf16[16,88,384]{2,1,0:T(8,128)(2,1)S(1)} async-done(((bf16[16,88,384]{2,1,0:T(8,128)(2,1)}), bf16[16,88,384]{2,1,0:T(8,128)(2,1)S(1)}, u32[]{:S(2)}, u32[]{:S(2)}) %all-to-all-start) | async-done | bytes 1081376 | tf_op jit(solution)/shard_map/all_to_all | solution.py:28
  87.6 4.1 %all-to-all-start.3 = ((bf16[8,128,176]{1,2,0:T(8,128)(2,1)}), bf16[8,128,176]{1,2,0:T(8,128)(2,1)}, u32[]{:S(2)}, u32[]{:S(2)}) async-start(bf16[8,128,176]{1,2,0:T(8,128)(2,1)} %broadcast_in_dim.206), calls=%async_computation.3 | async-start | bytes 720896 | tf_op jit(solution)/shard_map/all_to_all | solution.py:22
  91.8 2.3 %fusion.7 = bf16[384,512]{1,0:T(8,128)(2,1)S(1)} fusion(bf16[1408,384]{1,0:T(8,128)(2,1)S(1)} %bitcast.145, bf16[1408,512]{1,0:T(8,128)(2,1)} %bitcast.149, f32[1408]{0:T(1024)S(1)} %reshape.644, f32[512]{0:T(512)S(1)} %add_rsqrt_fusion.1), kind=kOutput, calls=%fused_computation.8 | convolution fusion | flops 556728320 | bytes 2924032 | tf_op jit(solution)/shard_map/dot_general | solution.py:32
  94.1 2.7 %collective-permute-start = (bf16[184,512]{1,0:T(8,128)(2,1)S(1)}, bf16[184,512]{1,0:T(8,128)(2,1)S(1)}, u32[]{:S(2)}, u32[]{:S(2)}) collective-permute-start(bf16[184,512]{1,0:T(8,128)(2,1)S(1)} %fusion.34), channel_id=1, source_target_pairs={{0,1},{1,0},{2,3},{3,2},{4,5},{5,4},{6,7},{7,6},{8,9},{9,8},{10,11... | collective-permute-start | bytes 565256 | tf_op jit(solution)/shard_map/ppermute | solution.py:428
  96.8 4.1 %collective-permute-done = bf16[184,512]{1,0:T(8,128)(2,1)S(1)} collective-permute-done((bf16[184,512]{1,0:T(8,128)(2,1)S(1)}, bf16[184,512]{1,0:T(8,128)(2,1)S(1)}, u32[]{:S(2)}, u32[]{:S(2)}) %collective-permute-start) | collective-permute-done | bytes 188448 | tf_op jit(solution)/shard_map/ppermute | solution.py:428
  101.7 2.4 %all-to-all-done.3 = bf16[8,128,176]{1,2,0:T(8,128)(2,1)} async-done(((bf16[8,128,176]{1,2,0:T(8,128)(2,1)}), bf16[8,128,176]{1,2,0:T(8,128)(2,1)}, u32[]{:S(2)}, u32[]{:S(2)}) %all-to-all-start.3) | async-done | bytes 360480 | tf_op jit(solution)/shard_map/all_to_all | solution.py:22
  104.1 1.2 copy.42
  105.7 2.6 %vision_attention.1 = bf16[16,88,128]{2,1,0:T(8,128)(2,1)} custom-call(s32[8]{0:T(128)S(1)} %select_reduce_fusion.4.ends_ref, bf16[128,176]{1,0:T(8,128)(2,1)S(1)} %pad.19.q_ref, bf16[1024,176]{1,0:T(8,128)(2,1)S(1)} %bitcast.141, s32[1,128]{1,0:T(1,128)S(1)} %broadcast_in_dim_tile.3.marks_ref), custom_call_target="tpu_custom_call" | custom-call | tf_op jit(solution)/shard_map/vision_attention/pallas_call | solution.py:272
  108.3 6.5 %all-to-all-start.4 = ((bf16[16,88,128]{2,1,0:T(8,128)(2,1)}), bf16[16,88,128]{2,1,0:T(8,128)(2,1)S(1)}, u32[]{:S(2)}, u32[]{:S(2)}) async-start(bf16[16,88,128]{2,1,0:T(8,128)(2,1)} %vision_attention.1), calls=%async_computation.4 | async-start | bytes 720896 | tf_op jit(solution)/shard_map/all_to_all | solution.py:28
  115.1 8.0 %all-to-all-done.4 = bf16[16,88,128]{2,1,0:T(8,128)(2,1)S(1)} async-done(((bf16[16,88,128]{2,1,0:T(8,128)(2,1)}), bf16[16,88,128]{2,1,0:T(8,128)(2,1)S(1)}, u32[]{:S(2)}, u32[]{:S(2)}) %all-to-all-start.4) | async-done | bytes 360480 | tf_op jit(solution)/shard_map/all_to_all | solution.py:28
  124.4 3.9 %all-to-all-start.5 = ((bf16[16,88,128]{2,1,0:T(8,128)(2,1)}), bf16[16,88,128]{2,1,0:T(8,128)(2,1)S(1)}, u32[]{:S(2)}, u32[]{:S(2)}) async-start(bf16[16,88,128]{2,1,0:T(8,128)(2,1)} %broadcast_in_dim.207), calls=%async_computation.5 | async-start | bytes 720896 | tf_op jit(solution)/shard_map/all_to_all | solution.py:22
  128.3 8.4 %all-to-all-done.5 = bf16[16,88,128]{2,1,0:T(8,128)(2,1)S(1)} async-done(((bf16[16,88,128]{2,1,0:T(8,128)(2,1)}), bf16[16,88,128]{2,1,0:T(8,128)(2,1)S(1)}, u32[]{:S(2)}, u32[]{:S(2)}) %all-to-all-start.5) | async-done | bytes 360480 | tf_op jit(solution)/shard_map/all_to_all | solution.py:22
  137.9 4.0 %all-to-all-start.6 = ((bf16[16,32,88]{2,1,0:T(8,128)(2,1)}), bf16[16,32,88]{2,1,0:T(8,128)(2,1)S(1)}, u32[]{:S(2)}, u32[]{:S(2)}) async-start(bf16[16,32,88]{2,1,0:T(8,128)(2,1)} %broadcast_in_dim.208), calls=%async_computation.6 | async-start | bytes 262144 | tf_op jit(solution)/shard_map/all_to_all | solution.py:22
  141.9 6.1 %all-to-all-done.6 = bf16[16,32,88]{2,1,0:T(8,128)(2,1)S(1)} async-done(((bf16[16,32,88]{2,1,0:T(8,128)(2,1)}), bf16[16,32,88]{2,1,0:T(8,128)(2,1)S(1)}, u32[]{:S(2)}, u32[]{:S(2)}) %all-to-all-start.6) | async-done | bytes 90144 | tf_op jit(solution)/shard_map/all_to_all | solution.py:22
  149.9 5.8 %all-to-all-start.7 = ((bf16[16,32,362]{2,1,0:T(8,128)(2,1)}), bf16[16,32,362]{2,1,0:T(8,128)(2,1)S(1)}, u32[]{:S(2)}, u32[]{:S(2)}) async-start(bf16[16,32,362]{2,1,0:T(8,128)(2,1)} %broadcast_in_dim.210), calls=%async_computation.7 | async-start | bytes 786432 | tf_op jit(solution)/shard_map/all_to_all | solution.py:22
  156.0 1.8 copy-done
  157.9 2.1 %text_attention.1 = (f32[88,512]{1,0:T(8,128)S(1)}, f32[8,512]{1,0:T(8,128)S(1)}) custom-call(s32[2]{0:T(128)S(1)} %pad_add_fusion.1.bounds_ref, bf16[96,512]{1,0:T(8,128)(2,1)S(1)} %maximum_maximum_fusion.q_ref.text_q_ref, bf16[8,2,184,512]{3,2,1,0:T(8,128)(2,1)S(1)} %bitcast.139, s32[3,512]{1,0:T(4,128)S(1)} %pad_add_fusion.qpos_ref), custom_call_target="tpu_custom_call" | custom-call | flops 1476395008 | bytes 3014656 | tf_op jit(solution)/shard_map/text_attention/pallas_call | solution.py:212
  160.7 9.7 %all-to-all-done.7 = bf16[16,32,362]{2,1,0:T(8,128)(2,1)S(1)} async-done(((bf16[16,32,362]{2,1,0:T(8,128)(2,1)}), bf16[16,32,362]{2,1,0:T(8,128)(2,1)S(1)}, u32[]{:S(2)}, u32[]{:S(2)}) %all-to-all-start.7) | async-done | bytes 370720 | tf_op jit(solution)/shard_map/all_to_all | solution.py:22
  171.3 0.9 copy-done.5
  172.2 4.0 %image_attention.1 = (bf16[88,512]{1,0:T(8,128)(2,1)S(1)}, bf16[88,512]{1,0:T(8,128)(2,1)S(1)}) custom-call(s32[2]{0:T(128)S(1)} %pad_add_fusion.1.bounds_ref, s32[4]{0:T(128)S(1)} %bitcast_reduce_fusion.busy_ref, bf16[512,362]{1,0:T(8,128)(2,1)S(1)} %bitcast.142, bf16[88,512]{1,0:T(8,128)(2,1)S(1)} %bitcast.144, ...), custom_call_target="tpu_custom_call" | custom-call | tf_op jit(solution)/shard_map/image_attention/pallas_call | solution.py:231
  176.3 26.1 %all_to_all.45 = bf16[16,88,512]{2,1,0:T(8,128)(2,1)S(1)} all-to-all(bf16[16,88,512]{2,1,0:T(8,128)(2,1)S(1)} %broadcast_in_dim.213), channel_id=1, replica_groups=mesh['row'=16,'col'=8,'grp'=2] {'row'}, dimensions={0} | all-to-all | bytes 2883584 | tf_op jit(solution)/shard_map/all_to_all | solution.py:22
  202.4 2.2 %fusion.12 = bf16[1,512,88]{1,2,0:T(8,128)(2,1)} fusion(bf16[1408,512]{1,0:T(8,128)(2,1)S(1)} %bitcast.150, bf16[1408,384]{1,0:T(8,128)(2,1)} %bitcast.160, bf16[88,512]{1,0:T(8,128)(2,1)S(1)} %get-tuple-element.49), kind=kOutput, calls=%fused_computation.13 | convolution fusion | flops 127012864 | bytes 1982464 | tf_op jit(solution)/shard_map/dot_general | solution.py:32
  (142 shorter events, 16.9 us)
Async XLA Ops:
  6.5 6.1 %copy-start.13 = (bf16[176]{0:T(256)(128)(2,1)S(1)}, bf16[176]{0:T(256)(128)(2,1)}, u32[]{:S(2)}) copy-start(bf16[176]{0:T(256)(128)(2,1)} %param.17) | copy-start | bytes 1060
  6.5 6.2 %copy-start.14 = (bf16[176]{0:T(256)(128)(2,1)S(1)}, bf16[176]{0:T(256)(128)(2,1)}, u32[]{:S(2)}) copy-start(bf16[176]{0:T(256)(128)(2,1)} %param.18) | copy-start | bytes 1060
  6.5 6.2 %copy-start.15 = (bf16[176]{0:T(256)(128)(2,1)S(1)}, bf16[176]{0:T(256)(128)(2,1)}, u32[]{:S(2)}) copy-start(bf16[176]{0:T(256)(128)(2,1)} %param.22) | copy-start | bytes 1060
  6.5 6.2 %copy-start.9 = (bf16[1,64,176]{2,1,0:T(8,128)(2,1)S(1)}, bf16[1,64,176]{2,1,0:T(8,128)(2,1)}, u32[]{:S(2)}) copy-start(bf16[1,64,176]{2,1,0:T(8,128)(2,1)} %param.16) | copy-start | bytes 67588
  6.5 56.6 %all-gather.5.cloned.1.call-start = ((), (), s32[]{:S(2)}) async-start(), calls=%async_computation.9 | async-start | bytes 3649536 | tf_op jit(solution)/shard_map/all_gather | solution.py:318
  7.5 15.0 %copy-start.16 = (s32[4]{0:T(128)S(1)}, s32[4]{0:T(128)}, u32[]{:S(2)}) copy-start(s32[4]{0:T(128)} %param.31) | copy-start | bytes 52
  7.5 18.4 %copy-start.11 = (s32[1,8]{1,0:T(1,128)S(1)}, s32[1,8]{1,0:T(1,128)}, u32[]{:S(2)}) copy-start(s32[1,8]{1,0:T(1,128)} %param.29) | copy-start | bytes 100
  7.5 18.5 %copy-start.17 = (s32[1,9]{1,0:T(1,128)S(1)}, s32[1,9]{1,0:T(1,128)}, u32[]{:S(2)}) copy-start(s32[1,9]{1,0:T(1,128)} %param.30) | copy-start | bytes 112
  7.5 18.7 %copy-start.12 = (bf16[88]{0:T(256)(128)(2,1)S(1)}, bf16[88]{0:T(256)(128)(2,1)}, u32[]{:S(2)}) copy-start(bf16[88]{0:T(256)(128)(2,1)} %param.26) | copy-start | bytes 532
  8.6 21.2 %copy-start.2 = (bf16[1,512,88]{1,2,0:T(8,128)(2,1)S(1)}, bf16[1,512,88]{1,2,0:T(8,128)(2,1)}, u32[]{:S(2)}) copy-start(bf16[1,512,88]{1,2,0:T(8,128)(2,1)} %param.25) | copy-start | bytes 270340
  11.9 0.8 copy-start.8
  13.4 16.3 %all-to-all-start.1 = ((bf16[8,16,176]{2,1,0:T(8,128)(2,1)}), bf16[8,16,176]{2,1,0:T(8,128)(2,1)S(1)}, u32[]{:S(2)}, u32[]{:S(2)}) async-start(bf16[8,16,176]{2,1,0:T(8,128)(2,1)} %pad_maximum_fusion.5), calls=%async_computation.1 | async-start | bytes 131072 | tf_op jit(solution)/shard_map/all_to_all | solution.py:28
  31.3 7.6 %copy-start.10 = (bf16[264]{0:T(512)(128)(2,1)S(1)}, bf16[264]{0:T(512)(128)(2,1)}, u32[]{:S(2)}) copy-start(bf16[264]{0:T(512)(128)(2,1)} %param.20) | copy-start | bytes 1588
  31.3 31.7 %all-to-all-start.2 = ((bf16[16,112,512]{2,1,0:T(8,128)(2,1)}), bf16[16,112,512]{2,1,0:T(8,128)(2,1)S(1)}, u32[]{:S(2)}, u32[]{:S(2)}) async-start(bf16[16,112,512]{2,1,0:T(8,128)(2,1)} %broadcast_in_dim.113), calls=%async_computation.2 | async-start | bytes 3670016 | tf_op jit(solution)/shard_map/all_to_all | solution.py:22
  65.6 21.3 %all-to-all-start = ((bf16[16,88,384]{2,1,0:T(8,128)(2,1)}), bf16[16,88,384]{2,1,0:T(8,128)(2,1)S(1)}, u32[]{:S(2)}, u32[]{:S(2)}) async-start(bf16[16,88,384]{2,1,0:T(8,128)(2,1)} %bitcast.152), calls=%async_computation | async-start | bytes 2162688 | tf_op jit(solution)/shard_map/all_to_all | solution.py:28
  71.0 2.9 %copy-start.6 = (bf16[16,88,512]{2,1,0:T(8,128)(2,1)}, bf16[16,88,512]{2,1,0:T(8,128)(2,1)S(1)}, u32[]{:S(2)}) copy-start(bf16[16,88,512]{2,1,0:T(8,128)(2,1)S(1)} %slice.197) | copy-start | bytes 4325380
  73.3 1.0 copy-start.7
  87.6 16.5 %all-to-all-start.3 = ((bf16[8,128,176]{1,2,0:T(8,128)(2,1)}), bf16[8,128,176]{1,2,0:T(8,128)(2,1)}, u32[]{:S(2)}, u32[]{:S(2)}) async-start(bf16[8,128,176]{1,2,0:T(8,128)(2,1)} %broadcast_in_dim.206), calls=%async_computation.3 | async-start | bytes 720896 | tf_op jit(solution)/shard_map/all_to_all | solution.py:22
  91.7 56.9 %all-gather.7.cloned.1.call-start = ((), (), s32[]{:S(2)}) async-start(), calls=%async_computation.10 | async-start | bytes 3391488 | tf_op jit(solution)/shard_map/all_gather | solution.py:431
  94.1 6.8 %collective-permute-start = (bf16[184,512]{1,0:T(8,128)(2,1)S(1)}, bf16[184,512]{1,0:T(8,128)(2,1)S(1)}, u32[]{:S(2)}, u32[]{:S(2)}) collective-permute-start(bf16[184,512]{1,0:T(8,128)(2,1)S(1)} %fusion.34), channel_id=1, source_target_pairs={{0,1},{1,0},{2,3},{3,2},{4,5},{5,4},{6,7},{7,6},{8,9},{9,8},{10,11... | collective-permute-start | bytes 565256 | tf_op jit(solution)/shard_map/ppermute | solution.py:428
  108.3 14.8 %all-to-all-start.4 = ((bf16[16,88,128]{2,1,0:T(8,128)(2,1)}), bf16[16,88,128]{2,1,0:T(8,128)(2,1)S(1)}, u32[]{:S(2)}, u32[]{:S(2)}) async-start(bf16[16,88,128]{2,1,0:T(8,128)(2,1)} %vision_attention.1), calls=%async_computation.4 | async-start | bytes 720896 | tf_op jit(solution)/shard_map/all_to_all | solution.py:28
  114.8 13.5 %copy-start.18 = (bf16[88]{0:T(256)(128)(2,1)S(1)}, bf16[88]{0:T(256)(128)(2,1)}, u32[]{:S(2)}) copy-start(bf16[88]{0:T(256)(128)(2,1)} %param.24) | copy-start | bytes 532
  124.4 12.3 %all-to-all-start.5 = ((bf16[16,88,128]{2,1,0:T(8,128)(2,1)}), bf16[16,88,128]{2,1,0:T(8,128)(2,1)S(1)}, u32[]{:S(2)}, u32[]{:S(2)}) async-start(bf16[16,88,128]{2,1,0:T(8,128)(2,1)} %broadcast_in_dim.207), calls=%async_computation.5 | async-start | bytes 720896 | tf_op jit(solution)/shard_map/all_to_all | solution.py:22
  137.9 10.2 %all-to-all-start.6 = ((bf16[16,32,88]{2,1,0:T(8,128)(2,1)}), bf16[16,32,88]{2,1,0:T(8,128)(2,1)S(1)}, u32[]{:S(2)}, u32[]{:S(2)}) async-start(bf16[16,32,88]{2,1,0:T(8,128)(2,1)} %broadcast_in_dim.208), calls=%async_computation.6 | async-start | bytes 262144 | tf_op jit(solution)/shard_map/all_to_all | solution.py:22
  149.9 20.4 %all-to-all-start.7 = ((bf16[16,32,362]{2,1,0:T(8,128)(2,1)}), bf16[16,32,362]{2,1,0:T(8,128)(2,1)S(1)}, u32[]{:S(2)}, u32[]{:S(2)}) async-start(bf16[16,32,362]{2,1,0:T(8,128)(2,1)} %broadcast_in_dim.210), calls=%async_computation.7 | async-start | bytes 786432 | tf_op jit(solution)/shard_map/all_to_all | solution.py:22
  156.0 1.9 copy-start
  157.9 12.5 %copy-start.1 = (bf16[16,184,512]{2,1,0:T(8,128)(2,1)S(1)}, bf16[16,184,512]{2,1,0:T(8,128)(2,1)}, u32[]{:S(2)}) copy-start(bf16[16,184,512]{2,1,0:T(8,128)(2,1)} %all-gather.7.cloned.1.call-done) | copy-start | bytes 9043972
  160.0 0.7 copy-start.4
  170.4 0.9 copy-start.3
  171.3 0.9 copy-start.5
Sparse Core Ops, SparseCore 0:
  12.8 49.7 all-gather.4
  105.5 41.5 all-gather.6

commit v4 on v3

--- a/solution.py
+++ b/solution.py
@@ -80,14 +80,12 @@
     return (rows // TPD) * (2 * TPD) + half * TPD + rows % TPD
 
 
-def fold_block(state, query, keys, values, key_pos, low, span, chosen=None):
+def fold_block(state, query, keys, values, key_pos, low, span):
     best, total, mixed = state
     factor = LOG2E * HEAD_DIM ** (-0.5)
     scores = dot0(keys, query)
     offset = key_pos - low
     allowed = (offset >= 0) & (offset <= span)
-    if chosen is not None:
-        allowed = allowed & chosen
     scores = jnp.where(allowed, scores, NEG)
     new_best = jnp.maximum(best, jnp.max(scores, axis=0, keepdims=True))
     weights = jnp.exp2((scores - new_best) * factor)
@@ -97,7 +95,7 @@
     return new_best, total, mixed * keep + added
 
 
-def fold_text(bounds_ref, kv_ref, state, query, low, span, chosen=None):
+def fold_text(bounds_ref, kv_ref, state, query, low, span):
     block = kv_ref.shape[3]
     key_rows = query.shape[0]
     step = lax.broadcasted_iota(jnp.int32, (block, 1), 0)
@@ -108,7 +106,7 @@
             keys = kv_ref[index, half, :key_rows]
             values = kv_ref[index, half, key_rows:]
             key_pos = in_pair + (index * (2 * block) + half * TPD)
-            state = fold_block(state, query, keys, values, key_pos, low, span, chosen)
+            state = fold_block(state, query, keys, values, key_pos, low, span)
         return state
 
     return lax.fori_loop(bounds_ref[0], bounds_ref[1], chunk, state)
@@ -135,70 +133,69 @@
 PLACE_AT = INPUT_AT + HEAD_DIM
 
 
+KEY_AT = HEAD_DIM
+VALUE_AT = 2 * HEAD_DIM + 8
+INPUT_AT = VALUE_AT + HEAD_DIM
+PLACE_AT = INPUT_AT + HEAD_DIM
+TILE = 128
+
+
 def image_kernel(
     bounds_ref,
-    busy_ref,
     shared_ref,
     text_ref,
     text_q_ref,
     kv_ref,
     qpos_ref,
+    packed_ref,
     text_mix_ref,
     text_stat_ref,
     out_ref,
     input_ref,
-    query_ref,
-    mix_ref,
-    stat_ref,
+    found_ref,
 ):
     shared = shared_ref[...]
-    slot = qpos_ref[2:3, :]
-    is_image = slot >= 0
-    low, span = qpos_ref[0:1, :], qpos_ref[1:2, :]
-    item = lax.broadcasted_iota(jnp.int32, (shared.shape[0], 1), 0)
-    placed = dot0(shared, jnp.where(item == slot, 1.0, 0.0).astype(BF16))
-    input_ref[...] = jnp.where(
-        is_image, placed[INPUT_AT:PLACE_AT], text_ref[...].astype(F32)
-    ).astype(BF16)
-    query = jnp.where(is_image, placed[:HEAD_DIM].astype(BF16), text_q_ref[:HEAD_DIM])
-    query_ref[:HEAD_DIM] = query
-    query_ref[HEAD_DIM:] = text_q_ref[HEAD_DIM:]
     place = shared[:, PLACE_AT : PLACE_AT + 2].astype(F32).astype(jnp.int32)
     key_pos = place[:, :1] * 64 + place[:, 1:]
-    keys = shared[:, KEY_AT : KEY_AT + HEAD_DIM]
-    scores = jnp.dot(keys, query, preferred_element_type=F32)
-    factor = LOG2E * HEAD_DIM ** (-0.5)
-    offset = key_pos - low
-    scores = jnp.where((offset >= 0) & (offset <= span), scores, NEG)
-    best = jnp.where(is_image, NEG, text_stat_ref[0:1, :])
-    new_best = jnp.maximum(best, jnp.max(scores, axis=0, keepdims=True))
-    weights = jnp.exp2((scores - new_best) * factor)
-    keep = jnp.where(is_image, 0.0, jnp.exp2((best - new_best) * factor))
-    stat_ref[0:1, :] = new_best
-    stat_ref[1:2, :] = text_stat_ref[1:2, :] * keep + jnp.sum(weights, axis=0, keepdims=True)
-    added = dot0(shared, weights.astype(BF16))[VALUE_AT:INPUT_AT]
-    mix_ref[...] = text_mix_ref[...] * keep + added
-    tiles = busy_ref.shape[0]
-    width = slot.shape[1] // tiles
-    for tile in range(tiles):
-        lanes = slice(tile * width, (tile + 1) * width)
-
-        @pl.when(busy_ref[tile] > 0)
+    keys = jnp.concatenate(
+        [shared[:, KEY_AT : KEY_AT + HEAD_DIM].T, jnp.zeros((8, shared.shape[0]), BF16)], axis=0
+    )
+    values = shared[:, VALUE_AT:INPUT_AT].T
+    state = (text_stat_ref[0:1, :], text_stat_ref[1:2, :], text_mix_ref[...])
+    best, total, mixed = fold_block(
+        state, text_q_ref[...], keys, values, key_pos, qpos_ref[0:1, :], qpos_ref[1:2, :]
+    )
+    mixed = (mixed / total).astype(BF16)
+
+    found_ref[...] = jnp.zeros_like(found_ref)
+    item = lax.broadcasted_iota(jnp.int32, (shared.shape[0], 1), 0)
+    for tile in range(packed_ref.shape[1] // TILE):
+        lanes = slice(tile * TILE, (tile + 1) * TILE)
+
+        @pl.when(bounds_ref[2] > tile * TILE)
         def _():
-            best, total, mixed = fold_text(
-                bounds_ref,
-                kv_ref,
-                (stat_ref[0:1, lanes], stat_ref[1:2, lanes], mix_ref[:, lanes]),
-                query_ref[:, lanes],
-                qpos_ref[0:1, lanes],
-                qpos_ref[1:2, lanes],
-                qpos_ref[2:3, lanes] >= 0,
+            low, span = packed_ref[0:1, lanes], packed_ref[1:2, lanes]
+            slot = packed_ref[2:3, lanes]
+            placed = dot0(shared, jnp.where(item == slot, 1.0, 0.0).astype(BF16)).astype(BF16)
+            query = jnp.concatenate([placed[:HEAD_DIM], text_q_ref[HEAD_DIM:, :TILE]], axis=0)
+            state = (
+                jnp.full((1, TILE), NEG, F32),
+                jnp.zeros((1, TILE), F32),
+                jnp.zeros((HEAD_DIM, TILE), F32),
             )
-            stat_ref[0:1, lanes] = best
-            stat_ref[1:2, lanes] = total
-            mix_ref[:, lanes] = mixed
-
-    out_ref[...] = (mix_ref[...] / stat_ref[1:2, :]).astype(BF16)
+            state = fold_block(state, query, keys, values, key_pos, low, span)
+            best, total, mixed = fold_text(bounds_ref, kv_ref, state, query, low, span)
+            found_ref[:HEAD_DIM, lanes] = (mixed / total).astype(BF16)
+            found_ref[HEAD_DIM:, lanes] = placed[INPUT_AT:PLACE_AT]
+
+    rank = qpos_ref[2:3, :]
+    spot = lax.broadcasted_iota(jnp.int32, (packed_ref.shape[1], 1), 0)
+    spread_out = jnp.dot(
+        found_ref[...], jnp.where(spot == rank, 1.0, 0.0).astype(BF16), preferred_element_type=F32
+    ).astype(BF16)
+    is_image = rank >= 0
+    out_ref[...] = jnp.where(is_image, spread_out[:HEAD_DIM], mixed)
+    input_ref[...] = jnp.where(is_image, spread_out[HEAD_DIM:], text_ref[...])
 
 
 def attention_params():
@@ -225,7 +222,7 @@
     )(bounds, query, keyval, qpos)
 
 
-def image_attention(bounds, busy, shared, text, text_query, keyval, qpos, mixed, stats):
+def image_attention(bounds, shared, text, text_query, keyval, qpos, packed, mixed, stats):
     vmem = pl.BlockSpec(memory_space=pltpu.VMEM)
     count = text.shape[1]
     return pl.pallas_call(
@@ -234,16 +231,12 @@
             jax.ShapeDtypeStruct((HEAD_DIM, count), BF16),
             jax.ShapeDtypeStruct((HEAD_DIM, count), BF16),
         ),
-        in_specs=[pl.BlockSpec(memory_space=pltpu.SMEM)] * 2 + [vmem] * 7,
+        in_specs=[pl.BlockSpec(memory_space=pltpu.SMEM)] + [vmem] * 8,
         out_specs=(vmem, vmem),
-        scratch_shapes=[
-            pltpu.VMEM(text_query.shape, BF16),
-            pltpu.VMEM((HEAD_DIM, count), F32),
-            pltpu.VMEM((8, count), F32),
-        ],
+        scratch_shapes=[pltpu.VMEM((2 * HEAD_DIM, packed.shape[1]), BF16)],
         compiler_params=attention_params(),
         name="image_attention",
-    )(bounds, busy, shared, text, text_query, keyval, qpos, mixed, stats)
+    )(bounds, shared, text, text_query, keyval, qpos, packed, mixed, stats)
 
 
 def vision_kernel(part, pitch, ends_ref, q_ref, kv_ref, marks_ref, out_ref):
@@ -382,7 +375,6 @@
     low = jnp.max(
         jnp.where(query_pos[:, None] >= ends[None, :], ends[None, :], 0), axis=1
     )
-    bounds = jnp.stack([jnp.min(low) // (2 * positions), col + 1]).astype(jnp.int32)
     merged = count // 4
     pack = part // 4
     item = jnp.arange(merged, dtype=jnp.int32)
@@ -391,13 +383,21 @@
     image_ends = running(lengths)
     place = sequence_position(rows_of_merged(merged_id, lengths, gaps), half)
     place = jnp.stack([place // 64, place % 64], axis=1).astype(BF16)
-    slot = (source // pack % cols * 2 + half) * merged
-    slot = slot + source // (pack * cols) * pack + source % pack
-    slot = jnp.where(inside, slot, -1)
-    qpos = jnp.stack([low, query_pos - low, slot])
-    busy = jnp.max(inside.astype(jnp.int32).reshape(4, positions // 4), axis=1)
+    total_merged = cols * merged
+    first = jnp.min(jnp.where(inside, source, total_merged))
+    found = jnp.sum(inside.astype(jnp.int32), dtype=jnp.int32)
+    rank = jnp.where(inside, source - first, -1)
+    near = jnp.arange(total_merged, dtype=jnp.int32)
+    row_of = first + near
+    slot = (row_of // pack % cols * 2 + half) * merged
+    slot = slot + row_of // (pack * cols) * pack + row_of % pack
+    near_pos = sequence_position(rows_of_merged(row_of, lengths, gaps), half)
+    near_low = jnp.max(jnp.where(near_pos[:, None] >= ends[None, :], ends[None, :], 0), axis=1)
+    packed = jnp.stack([near_low, near_pos - near_low, jnp.where(near < found, slot, -1)])
+    qpos = jnp.stack([low, query_pos - low, rank])
+    bounds = jnp.stack([jnp.min(low) // (2 * positions), col + 1, found]).astype(jnp.int32)
     bias = jnp.where(inside, NEG, 0.0).astype(BF16)[None]
-    row_w, vis_kv, qpos, bounds, marks, image_ends, place, busy, bias = (
+    row_w, vis_kv, qpos, bounds, marks, image_ends, place, packed, bias = (
         lax.optimization_barrier(
             (
                 row_w,
@@ -407,7 +407,7 @@
                 marks,
                 image_ends,
                 place,
-                busy,
+                packed,
                 bias,
             )
         )
@@ -485,7 +485,7 @@
     shared, mixed = lax.optimization_barrier((shared, mixed))
     shared = shared.reshape(cols * 2 * merged, -1)
     dec_attn, dec_input = image_attention(
-        bounds, busy, shared, text, text_query, all_kv, qpos, mixed, stats
+        bounds, shared, text, text_query, all_kv, qpos, packed, mixed, stats
     )
 
     all_dec = spread(dec_attn, "row").reshape(WIDTH, positions)

time: 213 us -> 213 us (level)
  waiting for transfers between devices: 78 us -> 73.8 us
  other arithmetic: 4.77 us -> 8.6 us
    all_to_all x3, waiting for transfers between devices: 24 us -> 21.4 us  [exchange(): return lax.all_to_all(values, axes, split_axis=0, concat_axis=0)]
    unnamed x39 -> x43, local copies, waits for them, and re-layouts: 5.14 us -> 5.15 us
  transfers between devices with their start and end apart: 11 -> 11, of which waited for: 9 -> 9; matrix products, arithmetic and copies ran while one was open for 7% -> 9% of each run, Pallas kernels for 2% -> 2%
where the time goes in v4:
time: 213 us; the launch traced here: 212 us
  waiting for transfers between devices  73.8 us (35%)
  starting transfers between devices  50.4 us (24%)
  blocking collectives  26.1 us (12%)
  local copies, waits for them, and re-layouts  22.9 us (11%)
  between operations  16.3 us (8%)
  other arithmetic  8.6 us (4%)
  Pallas kernels  8.06 us (4%)
  matrix products  6.1 us (3%)
    all_to_all x5, waiting for transfers between devices, spread(): lax.all_to_all(jnp.broadcast_to(values[None], (count,) + values.shape), a...  48.3 us
    all_to_all x5, starting transfers between devices, spread(): lax.all_to_all(jnp.broadcast_to(values[None], (count,) + values.shape), a...  26.9 us
    all_to_all x1, blocking collectives, spread(): lax.all_to_all(jnp.broadcast_to(values[None], (count,) + values.shape), a...  26.1 us
    all_to_all x3, waiting for transfers between devices, exchange(): return lax.all_to_all(values, axes, split_axis=0, concat_axis=0)  21.4 us
    all_to_all x3, starting transfers between devices, exchange(): return lax.all_to_all(values, axes, split_axis=0, concat_axis=0)  20.7 us
    dot_general x4, matrix products, dot0(): lax.dot_general(left, right, (((0,), (0,)), ((), ())), preferred_element_...  5.26 us
    unnamed x43, local copies, waits for them, and re-layouts  5.15 us
    slice x2, local copies, waits for them, and re-layouts, pair(): return lax.slice_in_dim(gathered_w, 2 * number, 2 * number + 2, axis=1)  4.65 us
  transfers between devices with their start and end apart: 11, of which 9 were waited for; matrix products, arithmetic and copies ran while one was open for 9% of the time, Pallas kernels for 2%

profile of v4, /device:TPU:1, one launch (start us, length us, event | category | flops | bytes accessed | tf_op | source)
XLA Modules:
  0.0 212.3 jit_solution(5631761940905910888)
XLA Ops:
  7.5 1.0 fusion.79
  9.5 1.0 fusion.78
  13.4 9.0 %all-to-all-start.1 = ((bf16[8,16,176]{2,1,0:T(8,128)(2,1)}), bf16[8,16,176]{2,1,0:T(8,128)(2,1)S(1)}, u32[]{:S(2)}, u32[]{:S(2)}) async-start(bf16[8,16,176]{2,1,0:T(8,128)(2,1)} %pad_maximum_fusion.5), calls=%async_computation.1 | async-start | bytes 131072 | tf_op jit(solution)/shard_map/all_to_all | solution.py:28
  27.4 1.2 compare_select_fusion.5
  29.8 1.4 broadcast_in_dim.138
  31.3 7.5 %all-to-all-start.2 = ((bf16[16,112,512]{2,1,0:T(8,128)(2,1)}), bf16[16,112,512]{2,1,0:T(8,128)(2,1)S(1)}, u32[]{:S(2)}, u32[]{:S(2)}) async-start(bf16[16,112,512]{2,1,0:T(8,128)(2,1)} %broadcast_in_dim.138), calls=%async_computation.2 | async-start | bytes 3670016 | tf_op jit(solution)/shard_map/all_to_all | solution.py:22
  40.8 22.2 %all-to-all-done.2 = bf16[16,112,512]{2,1,0:T(8,128)(2,1)S(1)} async-done(((bf16[16,112,512]{2,1,0:T(8,128)(2,1)}), bf16[16,112,512]{2,1,0:T(8,128)(2,1)S(1)}, u32[]{:S(2)}, u32[]{:S(2)}) %all-to-all-start.2) | async-done | bytes 1835040 | tf_op jit(solution)/shard_map/all_to_all | solution.py:22
  63.2 2.3 %slice.196 = bf16[8,2,88,384]{3,2,1,0:T(8,128)(2,1)} slice(bf16[8,6,88,384]{3,2,1,0:T(8,128)(2,1)} %bitcast.154), slice={[0:8], [0:2], [0:88], [0:384]} | slice | bytes 2162688 | tf_op jit(solution)/shard_map/slice | solution.py:314
  65.5 5.2 %all-to-all-start = ((bf16[16,88,384]{2,1,0:T(8,128)(2,1)}), bf16[16,88,384]{2,1,0:T(8,128)(2,1)S(1)}, u32[]{:S(2)}, u32[]{:S(2)}) async-start(bf16[16,88,384]{2,1,0:T(8,128)(2,1)} %bitcast.153), calls=%async_computation | async-start | bytes 2162688 | tf_op jit(solution)/shard_map/all_to_all | solution.py:28
  71.0 2.3 %fusion.76 = (bf16[8,2,88,384]{3,2,1,0:T(8,128)(2,1)S(1)}, bf16[8,2,88,384]{3,2,1,0:T(8,128)(2,1)S(1)}) fusion(bf16[8,6,88,384]{3,2,1,0:T(8,128)(2,1)} %bitcast.155), kind=kLoop, calls=%fused_computation.198 | loop fusion | bytes 4325376 | tf_op jit(solution)/shard_map/slice | solution.py:314
  74.3 12.5 %all-to-all-done = bf16[16,88,384]{2,1,0:T(8,128)(2,1)S(1)} async-done(((bf16[16,88,384]{2,1,0:T(8,128)(2,1)}), bf16[16,88,384]{2,1,0:T(8,128)(2,1)S(1)}, u32[]{:S(2)}, u32[]{:S(2)}) %all-to-all-start) | async-done | bytes 1081376 | tf_op jit(solution)/shard_map/all_to_all | solution.py:28
  87.6 4.9 %all-to-all-start.3 = ((bf16[8,128,176]{1,2,0:T(8,128)(2,1)}), bf16[8,128,176]{1,2,0:T(8,128)(2,1)}, u32[]{:S(2)}, u32[]{:S(2)}) async-start(bf16[8,128,176]{1,2,0:T(8,128)(2,1)} %broadcast_in_dim.247), calls=%async_computation.3 | async-start | bytes 720896 | tf_op jit(solution)/shard_map/all_to_all | solution.py:22
  92.6 2.2 %fusion.7 = bf16[384,512]{1,0:T(8,128)(2,1)S(1)} fusion(bf16[1408,384]{1,0:T(8,128)(2,1)S(1)} %bitcast.146, bf16[1408,512]{1,0:T(8,128)(2,1)} %bitcast.150, f32[1408]{0:T(1024)S(1)} %reshape.785, f32[512]{0:T(512)S(1)} %add_rsqrt_fusion.1), kind=kOutput, calls=%fused_computation.8 | convolution fusion | flops 556728320 | bytes 2924032 | tf_op jit(solution)/shard_map/dot_general | solution.py:32
  95.5 2.7 %collective-permute-start = (bf16[184,512]{1,0:T(8,128)(2,1)S(1)}, bf16[184,512]{1,0:T(8,128)(2,1)S(1)}, u32[]{:S(2)}, u32[]{:S(2)}) collective-permute-start(bf16[184,512]{1,0:T(8,128)(2,1)S(1)} %fusion.34), channel_id=1, source_target_pairs={{0,1},{1,0},{2,3},{3,2},{4,5},{5,4},{6,7},{7,6},{8,9},{9,8},{10,11... | collective-permute-start | bytes 565256 | tf_op jit(solution)/shard_map/ppermute | solution.py:428
  98.2 4.0 %collective-permute-done = bf16[184,512]{1,0:T(8,128)(2,1)S(1)} collective-permute-done((bf16[184,512]{1,0:T(8,128)(2,1)S(1)}, bf16[184,512]{1,0:T(8,128)(2,1)S(1)}, u32[]{:S(2)}, u32[]{:S(2)}) %collective-permute-start) | collective-permute-done | bytes 188448 | tf_op jit(solution)/shard_map/ppermute | solution.py:428
  103.0 1.9 all-to-all-done.3
  105.0 1.2 copy.42
  106.6 2.6 %vision_attention.1 = bf16[16,88,128]{2,1,0:T(8,128)(2,1)} custom-call(s32[8]{0:T(128)S(1)} %select_reduce_fusion.6.ends_ref, bf16[128,176]{1,0:T(8,128)(2,1)S(1)} %pad.19.q_ref, bf16[1024,176]{1,0:T(8,128)(2,1)S(1)} %bitcast.142, s32[1,128]{1,0:T(1,128)S(1)} %broadcast_in_dim_tile.3.marks_ref), custom_call_target="tpu_custom_call" | custom-call | tf_op jit(solution)/shard_map/vision_attention/pallas_call | solution.py:265
  109.2 6.5 %all-to-all-start.4 = ((bf16[16,88,128]{2,1,0:T(8,128)(2,1)}), bf16[16,88,128]{2,1,0:T(8,128)(2,1)S(1)}, u32[]{:S(2)}, u32[]{:S(2)}) async-start(bf16[16,88,128]{2,1,0:T(8,128)(2,1)} %vision_attention.1), calls=%async_computation.4 | async-start | bytes 720896 | tf_op jit(solution)/shard_map/all_to_all | solution.py:28
  116.0 8.0 %all-to-all-done.4 = bf16[16,88,128]{2,1,0:T(8,128)(2,1)S(1)} async-done(((bf16[16,88,128]{2,1,0:T(8,128)(2,1)}), bf16[16,88,128]{2,1,0:T(8,128)(2,1)S(1)}, u32[]{:S(2)}, u32[]{:S(2)}) %all-to-all-start.4) | async-done | bytes 360480 | tf_op jit(solution)/shard_map/all_to_all | solution.py:28
  125.2 3.9 %all-to-all-start.5 = ((bf16[16,88,128]{2,1,0:T(8,128)(2,1)}), bf16[16,88,128]{2,1,0:T(8,128)(2,1)S(1)}, u32[]{:S(2)}, u32[]{:S(2)}) async-start(bf16[16,88,128]{2,1,0:T(8,128)(2,1)} %broadcast_in_dim.248), calls=%async_computation.5 | async-start | bytes 720896 | tf_op jit(solution)/shard_map/all_to_all | solution.py:22
  129.2 8.4 %all-to-all-done.5 = bf16[16,88,128]{2,1,0:T(8,128)(2,1)S(1)} async-done(((bf16[16,88,128]{2,1,0:T(8,128)(2,1)}), bf16[16,88,128]{2,1,0:T(8,128)(2,1)S(1)}, u32[]{:S(2)}, u32[]{:S(2)}) %all-to-all-start.5) | async-done | bytes 360480 | tf_op jit(solution)/shard_map/all_to_all | solution.py:22
  138.7 4.0 %all-to-all-start.6 = ((bf16[16,32,88]{2,1,0:T(8,128)(2,1)}), bf16[16,32,88]{2,1,0:T(8,128)(2,1)S(1)}, u32[]{:S(2)}, u32[]{:S(2)}) async-start(bf16[16,32,88]{2,1,0:T(8,128)(2,1)} %broadcast_in_dim.249), calls=%async_computation.6 | async-start | bytes 262144 | tf_op jit(solution)/shard_map/all_to_all | solution.py:22
  142.8 6.1 %all-to-all-done.6 = bf16[16,32,88]{2,1,0:T(8,128)(2,1)S(1)} async-done(((bf16[16,32,88]{2,1,0:T(8,128)(2,1)}), bf16[16,32,88]{2,1,0:T(8,128)(2,1)S(1)}, u32[]{:S(2)}, u32[]{:S(2)}) %all-to-all-start.6) | async-done | bytes 90144 | tf_op jit(solution)/shard_map/all_to_all | solution.py:22
  150.8 6.5 %all-to-all-start.7 = ((bf16[16,32,362]{2,1,0:T(8,128)(2,1)}), bf16[16,32,362]{2,1,0:T(8,128)(2,1)S(1)}, u32[]{:S(2)}, u32[]{:S(2)}) async-start(bf16[16,32,362]{2,1,0:T(8,128)(2,1)} %broadcast_in_dim.251), calls=%async_computation.7 | async-start | bytes 786432 | tf_op jit(solution)/shard_map/all_to_all | solution.py:22
  157.6 1.8 copy-done
  159.4 2.1 %text_attention.1 = (f32[88,512]{1,0:T(8,128)S(1)}, f32[8,512]{1,0:T(8,128)S(1)}) custom-call(s32[3]{0:T(128)S(1)} %pad_add_fusion.2.bounds_ref, bf16[96,512]{1,0:T(8,128)(2,1)S(1)} %maximum_maximum_fusion.q_ref.text_q_ref, bf16[8,2,184,512]{3,2,1,0:T(8,128)(2,1)S(1)} %bitcast.140, s32[3,512]{1,0:T(4,128)S(1)} %pad_add_fusion.qpos_ref), custom_call_target="tpu_custom_call" | custom-call | flops 1476395008 | bytes 3014656 | tf_op jit(solution)/shard_map/text_attention/pallas_call | solution.py:209
  162.2 9.7 %all-to-all-done.7 = bf16[16,32,362]{2,1,0:T(8,128)(2,1)S(1)} async-done(((bf16[16,32,362]{2,1,0:T(8,128)(2,1)}), bf16[16,32,362]{2,1,0:T(8,128)(2,1)S(1)}, u32[]{:S(2)}, u32[]{:S(2)}) %all-to-all-start.7) | async-done | bytes 370720 | tf_op jit(solution)/shard_map/all_to_all | solution.py:22
  172.8 0.9 copy-done.5
  173.7 3.3 %image_attention.1 = (bf16[88,512]{1,0:T(8,128)(2,1)S(1)}, bf16[88,512]{1,0:T(8,128)(2,1)S(1)}) custom-call(s32[3]{0:T(128)S(1)} %pad_add_fusion.2.bounds_ref, bf16[512,362]{1,0:T(8,128)(2,1)S(1)} %bitcast.143, bf16[88,512]{1,0:T(8,128)(2,1)S(1)} %bitcast.145, bf16[96,512]{1,0:T(8,128)(2,1)S(1)} %maximum_maximum_fusion.q_ref.text_q_ref, ...), custom_call_target="tpu_custom_call" | custom-call | tf_op jit(solution)/shard_map/image_attention/pallas_call | solution.py:228
  177.1 26.1 %all_to_all.45 = bf16[16,88,512]{2,1,0:T(8,128)(2,1)S(1)} all-to-all(bf16[16,88,512]{2,1,0:T(8,128)(2,1)S(1)} %broadcast_in_dim.254), channel_id=1, replica_groups=mesh['row'=16,'col'=8,'grp'=2] {'row'}, dimensions={0} | all-to-all | bytes 2883584 | tf_op jit(solution)/shard_map/all_to_all | solution.py:22
  203.3 2.2 %fusion.12 = bf16[1,512,88]{1,2,0:T(8,128)(2,1)} fusion(bf16[1408,512]{1,0:T(8,128)(2,1)S(1)} %bitcast.151, bf16[1408,384]{1,0:T(8,128)(2,1)} %bitcast.161, bf16[88,512]{1,0:T(8,128)(2,1)S(1)} %get-tuple-element.49), kind=kOutput, calls=%fused_computation.13 | convolution fusion | flops 127012864 | bytes 1982464 | tf_op jit(solution)/shard_map/dot_general | solution.py:32
  (155 shorter events, 20.9 us)
Async XLA Ops:
  6.5 6.1 %copy-start.15 = (bf16[176]{0:T(256)(128)(2,1)S(1)}, bf16[176]{0:T(256)(128)(2,1)}, u32[]{:S(2)}) copy-start(bf16[176]{0:T(256)(128)(2,1)} %param.17) | copy-start | bytes 1060
  6.5 6.1 %copy-start.16 = (bf16[176]{0:T(256)(128)(2,1)S(1)}, bf16[176]{0:T(256)(128)(2,1)}, u32[]{:S(2)}) copy-start(bf16[176]{0:T(256)(128)(2,1)} %param.18) | copy-start | bytes 1060
  6.5 6.2 %copy-start.17 = (bf16[176]{0:T(256)(128)(2,1)S(1)}, bf16[176]{0:T(256)(128)(2,1)}, u32[]{:S(2)}) copy-start(bf16[176]{0:T(256)(128)(2,1)} %param.22) | copy-start | bytes 1060
  6.5 6.2 %copy-start.11 = (bf16[1,64,176]{2,1,0:T(8,128)(2,1)S(1)}, bf16[1,64,176]{2,1,0:T(8,128)(2,1)}, u32[]{:S(2)}) copy-start(bf16[1,64,176]{2,1,0:T(8,128)(2,1)} %param.16) | copy-start | bytes 67588
  6.5 56.6 %all-gather.5.cloned.1.call-start = ((), (), s32[]{:S(2)}) async-start(), calls=%async_computation.9 | async-start | bytes 3649536 | tf_op jit(solution)/shard_map/all_gather | solution.py:311
  7.5 15.0 %copy-start.18 = (s32[4]{0:T(128)S(1)}, s32[4]{0:T(128)}, u32[]{:S(2)}) copy-start(s32[4]{0:T(128)} %param.31) | copy-start | bytes 52
  7.5 18.1 %copy-start.13 = (s32[1,8]{1,0:T(1,128)S(1)}, s32[1,8]{1,0:T(1,128)}, u32[]{:S(2)}) copy-start(s32[1,8]{1,0:T(1,128)} %param.29) | copy-start | bytes 100
  7.5 18.2 %copy-start.19 = (s32[1,9]{1,0:T(1,128)S(1)}, s32[1,9]{1,0:T(1,128)}, u32[]{:S(2)}) copy-start(s32[1,9]{1,0:T(1,128)} %param.30) | copy-start | bytes 112
  7.5 21.1 %copy-start.14 = (bf16[88]{0:T(256)(128)(2,1)S(1)}, bf16[88]{0:T(256)(128)(2,1)}, u32[]{:S(2)}) copy-start(bf16[88]{0:T(256)(128)(2,1)} %param.26) | copy-start | bytes 532
  9.5 20.4 %copy-start.2 = (bf16[1,512,88]{1,2,0:T(8,128)(2,1)S(1)}, bf16[1,512,88]{1,2,0:T(8,128)(2,1)}, u32[]{:S(2)}) copy-start(bf16[1,512,88]{1,2,0:T(8,128)(2,1)} %param.25) | copy-start | bytes 270340
  11.9 0.7 copy-start.8
  13.4 16.3 %all-to-all-start.1 = ((bf16[8,16,176]{2,1,0:T(8,128)(2,1)}), bf16[8,16,176]{2,1,0:T(8,128)(2,1)S(1)}, u32[]{:S(2)}, u32[]{:S(2)}) async-start(bf16[8,16,176]{2,1,0:T(8,128)(2,1)} %pad_maximum_fusion.5), calls=%async_computation.1 | async-start | bytes 131072 | tf_op jit(solution)/shard_map/all_to_all | solution.py:28
  31.3 8.2 %copy-start.12 = (bf16[264]{0:T(512)(128)(2,1)S(1)}, bf16[264]{0:T(512)(128)(2,1)}, u32[]{:S(2)}) copy-start(bf16[264]{0:T(512)(128)(2,1)} %param.20) | copy-start | bytes 1588
  31.3 31.7 %all-to-all-start.2 = ((bf16[16,112,512]{2,1,0:T(8,128)(2,1)}), bf16[16,112,512]{2,1,0:T(8,128)(2,1)S(1)}, u32[]{:S(2)}, u32[]{:S(2)}) async-start(bf16[16,112,512]{2,1,0:T(8,128)(2,1)} %broadcast_in_dim.138), calls=%async_computation.2 | async-start | bytes 3670016 | tf_op jit(solution)/shard_map/all_to_all | solution.py:22
  65.5 21.3 %all-to-all-start = ((bf16[16,88,384]{2,1,0:T(8,128)(2,1)}), bf16[16,88,384]{2,1,0:T(8,128)(2,1)S(1)}, u32[]{:S(2)}, u32[]{:S(2)}) async-start(bf16[16,88,384]{2,1,0:T(8,128)(2,1)} %bitcast.153), calls=%async_computation | async-start | bytes 2162688 | tf_op jit(solution)/shard_map/all_to_all | solution.py:28
  71.0 3.3 %copy-start.6 = (bf16[16,88,512]{2,1,0:T(8,128)(2,1)}, bf16[16,88,512]{2,1,0:T(8,128)(2,1)S(1)}, u32[]{:S(2)}) copy-start(bf16[16,88,512]{2,1,0:T(8,128)(2,1)S(1)} %slice.198) | copy-start | bytes 4325380
  73.3 1.0 copy-start.7
  73.9 18.7 %copy-start.10 = (bf16[128,264]{0,1:T(8,128)(2,1)}, bf16[128,264]{0,1:T(8,128)(2,1)S(1)}, u32[]{:S(2)}) copy-start(bf16[128,264]{0,1:T(8,128)(2,1)S(1)} %fusion.11) | copy-start | bytes 202756
  87.6 17.4 %all-to-all-start.3 = ((bf16[8,128,176]{1,2,0:T(8,128)(2,1)}), bf16[8,128,176]{1,2,0:T(8,128)(2,1)}, u32[]{:S(2)}, u32[]{:S(2)}) async-start(bf16[8,128,176]{1,2,0:T(8,128)(2,1)} %broadcast_in_dim.247), calls=%async_computation.3 | async-start | bytes 720896 | tf_op jit(solution)/shard_map/all_to_all | solution.py:22
  92.5 57.0 %all-gather.7.cloned.1.call-start = ((), (), s32[]{:S(2)}) async-start(), calls=%async_computation.10 | async-start | bytes 3391488 | tf_op jit(solution)/shard_map/all_gather | solution.py:431
  95.5 10.9 %slice-start = ((bf16[128,264]{0,1:T(8,128)(2,1)}), bf16[128,88]{0,1:T(8,128)(2,1)S(1)}, s32[]{:S(2)}) async-start(bf16[128,264]{0,1:T(8,128)(2,1)} %copy-done.10), calls=%async_computation.11 | async-start | bytes 45056 | tf_op jit(solution)/shard_map/slice | solution.py:369
  95.5 6.8 %collective-permute-start = (bf16[184,512]{1,0:T(8,128)(2,1)S(1)}, bf16[184,512]{1,0:T(8,128)(2,1)S(1)}, u32[]{:S(2)}, u32[]{:S(2)}) collective-permute-start(bf16[184,512]{1,0:T(8,128)(2,1)S(1)} %fusion.34), channel_id=1, source_target_pairs={{0,1},{1,0},{2,3},{3,2},{4,5},{5,4},{6,7},{7,6},{8,9},{9,8},{10,11... | collective-permute-start | bytes 565256 | tf_op jit(solution)/shard_map/ppermute | solution.py:428
  109.2 14.8 %all-to-all-start.4 = ((bf16[16,88,128]{2,1,0:T(8,128)(2,1)}), bf16[16,88,128]{2,1,0:T(8,128)(2,1)S(1)}, u32[]{:S(2)}, u32[]{:S(2)}) async-start(bf16[16,88,128]{2,1,0:T(8,128)(2,1)} %vision_attention.1), calls=%async_computation.4 | async-start | bytes 720896 | tf_op jit(solution)/shard_map/all_to_all | solution.py:28
  115.7 13.5 %copy-start.20 = (bf16[88]{0:T(256)(128)(2,1)S(1)}, bf16[88]{0:T(256)(128)(2,1)}, u32[]{:S(2)}) copy-start(bf16[88]{0:T(256)(128)(2,1)} %param.24) | copy-start | bytes 532
  125.2 12.3 %all-to-all-start.5 = ((bf16[16,88,128]{2,1,0:T(8,128)(2,1)}), bf16[16,88,128]{2,1,0:T(8,128)(2,1)S(1)}, u32[]{:S(2)}, u32[]{:S(2)}) async-start(bf16[16,88,128]{2,1,0:T(8,128)(2,1)} %broadcast_in_dim.248), calls=%async_computation.5 | async-start | bytes 720896 | tf_op jit(solution)/shard_map/all_to_all | solution.py:22
  138.7 10.2 %all-to-all-start.6 = ((bf16[16,32,88]{2,1,0:T(8,128)(2,1)}), bf16[16,32,88]{2,1,0:T(8,128)(2,1)S(1)}, u32[]{:S(2)}, u32[]{:S(2)}) async-start(bf16[16,32,88]{2,1,0:T(8,128)(2,1)} %broadcast_in_dim.249), calls=%async_computation.6 | async-start | bytes 262144 | tf_op jit(solution)/shard_map/all_to_all | solution.py:22
  149.4 8.1 %copy-start.9 = (bf16[88,512]{1,0:T(8,128)(2,1)S(1)}, bf16[88,512]{1,0:T(8,128)(2,1)}, u32[]{:S(2)}) copy-start(bf16[88,512]{1,0:T(8,128)(2,1)} %get-tuple-element.64) | copy-start | bytes 270340
  150.8 21.1 %all-to-all-start.7 = ((bf16[16,32,362]{2,1,0:T(8,128)(2,1)}), bf16[16,32,362]{2,1,0:T(8,128)(2,1)S(1)}, u32[]{:S(2)}, u32[]{:S(2)}) async-start(bf16[16,32,362]{2,1,0:T(8,128)(2,1)} %broadcast_in_dim.251), calls=%async_computation.7 | async-start | bytes 786432 | tf_op jit(solution)/shard_map/all_to_all | solution.py:22
  157.6 1.9 copy-start
  159.4 12.5 %copy-start.1 = (bf16[16,184,512]{2,1,0:T(8,128)(2,1)S(1)}, bf16[16,184,512]{2,1,0:T(8,128)(2,1)}, u32[]{:S(2)}) copy-start(bf16[16,184,512]{2,1,0:T(8,128)(2,1)} %all-gather.7.cloned.1.call-done) | copy-start | bytes 9043972
  171.9 0.9 copy-start.3
  172.8 0.9 copy-start.5
  (1 other events, 0.7 us)
Sparse Core Ops, SparseCore 0:
  12.8 49.7 all-gather.4
  106.3 42.1 all-gather.6

commit v5 on v4

--- a/solution.py
+++ b/solution.py
@@ -237,6 +237,61 @@
         compiler_params=attention_params(),
         name="image_attention",
     )(bounds, shared, text, text_query, keyval, qpos, packed, mixed, stats)
+
+
+def pack_kernel(
+    dec_qkv_ref,
+    vis_out_ref,
+    vis_qkv_ref,
+    dec_out_ref,
+    proj_ref,
+    patch_ref,
+    gain_ref,
+    bias_ref,
+    out_bias_ref,
+    out_ref,
+    rows_ref,
+):
+    parts = rows_ref.shape[0]
+    deep = patch_ref.shape[1] // parts
+    affine = jnp.stack([gain_ref[...], bias_ref[...], out_bias_ref[...]])
+    affine = jnp.concatenate([affine, jnp.zeros((5, affine.shape[1]), BF16)], axis=0)
+    for at in range(parts):
+        rows_ref[at, :deep] = patch_ref[0, at * deep : (at + 1) * deep]
+        rows_ref[at, deep:] = affine
+    width = vis_qkv_ref.shape[1]
+    for at in range(2):
+        side = slice(at * HEAD_DIM, (at + 1) * HEAD_DIM)
+        fill = jnp.zeros((HEAD_DIM, out_ref.shape[2] - width - HEAD_DIM), BF16)
+        out_ref[at, :, :width] = dec_qkv_ref[:, at * width : (at + 1) * width]
+        out_ref[at, :, width : width + HEAD_DIM] = vis_out_ref[:, side]
+        out_ref[at, :, width + HEAD_DIM :] = fill
+        out_ref[2 + at, :, :width] = vis_qkv_ref[side]
+        out_ref[2 + at, :, width : width + HEAD_DIM] = dec_out_ref[side]
+        out_ref[2 + at, :, width + HEAD_DIM :] = fill
+        for window in range(4):
+            lanes = slice(window * HEAD_DIM, (window + 1) * HEAD_DIM)
+            out_ref[4 + at, :, lanes] = proj_ref[window, side]
+        out_ref[4 + at, :, 4 * HEAD_DIM :] = jnp.zeros(
+            (HEAD_DIM, out_ref.shape[2] - 4 * HEAD_DIM), BF16
+        )
+
+
+def pack_arguments(unit, parts, *arrays):
+    vmem = pl.BlockSpec(memory_space=pltpu.VMEM)
+    return pl.pallas_call(
+        pack_kernel,
+        out_shape=(
+            jax.ShapeDtypeStruct((6, HEAD_DIM, unit), BF16),
+            jax.ShapeDtypeStruct(
+                (parts, arrays[5].shape[1] // parts + 8, arrays[5].shape[2]), BF16
+            ),
+        ),
+        in_specs=[vmem] * 9,
+        out_specs=(vmem, vmem),
+        compiler_params=pltpu.CompilerParams(vmem_limit_bytes=62 * 1024 * 1024),
+        name="pack_arguments",
+    )(*arrays)
 
 
 def vision_kernel(part, pitch, ends_ref, q_ref, kv_ref, marks_ref, out_ref):
@@ -299,15 +354,19 @@
     feat_c = vis_out.shape[1]
     vis_n = vis_qkv.shape[1]
     unit = -(-(vis_n + HEAD_DIM) // 128) * 128
-    fill = jnp.zeros((HEAD_DIM, unit - vis_n - HEAD_DIM), BF16)
-    sides = (slice(0, HEAD_DIM), slice(HEAD_DIM, 2 * HEAD_DIM))
-    units = [
-        [dec_qkv[:, at * vis_n : (at + 1) * vis_n], vis_out[:, side], fill]
-        for at, side in enumerate(sides)
-    ]
-    units += [[vis_qkv[side], dec_out[side], fill] for side in sides]
-    units += [[proj_weight[window, side] for window in range(4)] + [fill] for side in sides]
-    packed = jnp.stack([jnp.concatenate(pieces, axis=1) for pieces in units])
+    packed, own_rows_out = pack_arguments(
+        unit,
+        cols,
+        dec_qkv,
+        vis_out,
+        vis_qkv,
+        dec_out,
+        proj_weight,
+        patches,
+        vis_gain,
+        vis_bias,
+        vis_out_bias,
+    )
     gathered_w = lax.all_gather(packed, "col", axis=0)
 
     def pair(number):
@@ -315,18 +374,7 @@
 
     rows_b = patches.shape[1]
     part = rows_b // cols
-    affine_own = jnp.stack([vis_gain, vis_bias, vis_out_bias])
-    affine_own = jnp.pad(affine_own, ((0, 8 - affine_own.shape[0]), (0, 0)))
-    mine = exchange(
-        jnp.concatenate(
-            [
-                patches[0].reshape(cols, part, feat_c),
-                jnp.broadcast_to(affine_own[None], (cols, 8, feat_c)),
-            ],
-            axis=1,
-        ),
-        "col",
-    )
+    mine = exchange(own_rows_out, "col")
     mine = jnp.transpose(mine, (1, 0, 2)).reshape(part + 8, WIDTH)
     affine = mine[part : part + 3].astype(F32)
 

time: 213 us -> 211 us (level)
  local copies, waits for them, and re-layouts: 22.9 us -> 16.7 us
  other arithmetic: 8.6 us -> 11.5 us
    slice x4 -> x0, local copies, waits for them, and re-layouts: 3.66 us -> none  [the longest x2 1.72 us: per_device(): units += [[vis_qkv[side], dec_out[side], fill] for side in sides]]
    unnamed x43 -> x20, local copies, waits for them, and re-layouts: 5.15 us -> 4.36 us
  transfers between devices with their start and end apart: 11 -> 11, of which waited for: 9 -> 8; matrix products, arithmetic and copies ran while one was open for 9% -> 11% of each run, Pallas kernels for 2% -> 2%
where the time goes in v5:
time: 211 us; the launch traced here: 209 us
  waiting for transfers between devices  73.5 us (35%)
  starting transfers between devices  50.6 us (24%)
  blocking collectives  26.1 us (12%)
  local copies, waits for them, and re-layouts  16.7 us (8%)
  between operations  16.1 us (8%)
  other arithmetic  11.5 us (5%)
  Pallas kernels  8.77 us (4%)
  matrix products  6.15 us (3%)
    all_to_all x5, waiting for transfers between devices, spread(): lax.all_to_all(jnp.broadcast_to(values[None], (count,) + values.shape), a...  48.8 us
    all_to_all x5, starting transfers between devices, spread(): lax.all_to_all(jnp.broadcast_to(values[None], (count,) + values.shape), a...  27.1 us
    all_to_all x1, blocking collectives, spread(): lax.all_to_all(jnp.broadcast_to(values[None], (count,) + values.shape), a...  26.1 us
    all_to_all x3, starting transfers between devices, exchange(): return lax.all_to_all(values, axes, split_axis=0, concat_axis=0)  20.7 us
    all_to_all x3, waiting for transfers between devices, exchange(): return lax.all_to_all(values, axes, split_axis=0, concat_axis=0)  20.6 us
    dot_general x4, matrix products, dot0(): lax.dot_general(left, right, (((0,), (0,)), ((), ())), preferred_element_...  5.32 us
    slice x2, local copies, waits for them, and re-layouts, pair(): return lax.slice_in_dim(gathered_w, 2 * number, 2 * number + 2, axis=1)  4.68 us
    broadcast_in_dim x6, local copies, waits for them, and re-layouts, spread(): jnp.broadcast_to(values[None], (count,) + values.shape)  4.59 us
  transfers between devices with their start and end apart: 11, of which 8 were waited for; matrix products, arithmetic and copies ran while one was open for 11% of the time, Pallas kernels for 2%

profile of v5, /device:TPU:1, one launch (start us, length us, event | category | flops | bytes accessed | tf_op | source)
XLA Modules:
  0.0 209.5 jit_solution(5640886483825892025)
XLA Ops:
  6.5 2.1 %pack_arguments.1 = (bf16[6,88,384]{2,1,0:T(8,128)(2,1)}, bf16[8,16,176]{2,1,0:T(8,128)(2,1)}) custom-call(bf16[88,528]{1,0:T(8,128)(2,1)} %dec_qkv_ref.1, bf16[88,176]{1,0:T(8,128)(2,1)} %vis_out_ref.1, bf16[176,264]{1,0:T(8,128)(2,1)} %vis_qkv_ref.1, bf16[176,88]{1,0:T(8,128)(2,1)} %dec_out_ref.1, bf16[4,176,88]{2,1,0:T(8,128)(2,1)} %proj_ref.1, ...), custom_call_target="tpu_custom_call" | custom-call | tf_op jit(solution)/shard_map/pack_arguments/pallas_call | solution.py:282
  8.7 9.0 %all-to-all-start.1 = ((bf16[8,16,176]{2,1,0:T(8,128)(2,1)}), bf16[8,16,176]{2,1,0:T(8,128)(2,1)S(1)}, u32[]{:S(2)}, u32[]{:S(2)}) async-start(bf16[8,16,176]{2,1,0:T(8,128)(2,1)} %get-tuple-element.32), calls=%async_computation.1 | async-start | bytes 131072 | tf_op jit(solution)/shard_map/all_to_all | solution.py:28
  25.9 1.2 compare_select_fusion.5
  28.2 1.4 broadcast_in_dim.132
  29.6 6.4 %all-to-all-start.2 = ((bf16[16,112,512]{2,1,0:T(8,128)(2,1)}), bf16[16,112,512]{2,1,0:T(8,128)(2,1)S(1)}, u32[]{:S(2)}, u32[]{:S(2)}) async-start(bf16[16,112,512]{2,1,0:T(8,128)(2,1)} %broadcast_in_dim.132), calls=%async_computation.2 | async-start | bytes 3670016 | tf_op jit(solution)/shard_map/all_to_all | solution.py:22
  38.0 22.2 %all-to-all-done.2 = bf16[16,112,512]{2,1,0:T(8,128)(2,1)S(1)} async-done(((bf16[16,112,512]{2,1,0:T(8,128)(2,1)}), bf16[16,112,512]{2,1,0:T(8,128)(2,1)S(1)}, u32[]{:S(2)}, u32[]{:S(2)}) %all-to-all-start.2) | async-done | bytes 1835040 | tf_op jit(solution)/shard_map/all_to_all | solution.py:22
  60.4 2.4 %slice.132 = bf16[8,2,88,384]{3,2,1,0:T(8,128)(2,1)} slice(bf16[8,6,88,384]{3,2,1,0:T(8,128)(2,1)} %bitcast.117), slice={[0:8], [0:2], [0:88], [0:384]} | slice | bytes 2162688 | tf_op jit(solution)/shard_map/slice | solution.py:373
  62.8 5.2 %all-to-all-start = ((bf16[16,88,384]{2,1,0:T(8,128)(2,1)}), bf16[16,88,384]{2,1,0:T(8,128)(2,1)S(1)}, u32[]{:S(2)}, u32[]{:S(2)}) async-start(bf16[16,88,384]{2,1,0:T(8,128)(2,1)} %bitcast.116), calls=%async_computation | async-start | bytes 2162688 | tf_op jit(solution)/shard_map/all_to_all | solution.py:28
  68.2 2.3 %fusion.63 = (bf16[8,2,88,384]{3,2,1,0:T(8,128)(2,1)S(1)}, bf16[8,2,88,384]{3,2,1,0:T(8,128)(2,1)S(1)}) fusion(bf16[8,6,88,384]{3,2,1,0:T(8,128)(2,1)} %bitcast.118), kind=kLoop, calls=%fused_computation.169 | loop fusion | bytes 4325376 | tf_op jit(solution)/shard_map/slice | solution.py:373
  71.5 12.5 %all-to-all-done = bf16[16,88,384]{2,1,0:T(8,128)(2,1)S(1)} async-done(((bf16[16,88,384]{2,1,0:T(8,128)(2,1)}), bf16[16,88,384]{2,1,0:T(8,128)(2,1)S(1)}, u32[]{:S(2)}, u32[]{:S(2)}) %all-to-all-start) | async-done | bytes 1081376 | tf_op jit(solution)/shard_map/all_to_all | solution.py:28
  84.8 6.9 %all-to-all-start.3 = ((bf16[8,128,176]{1,2,0:T(8,128)(2,1)}), bf16[8,128,176]{1,2,0:T(8,128)(2,1)}, u32[]{:S(2)}, u32[]{:S(2)}) async-start(bf16[8,128,176]{1,2,0:T(8,128)(2,1)} %broadcast_in_dim.236), calls=%async_computation.3 | async-start | bytes 720896 | tf_op jit(solution)/shard_map/all_to_all | solution.py:22
  91.8 2.3 %fusion.7 = bf16[384,512]{1,0:T(8,128)(2,1)S(1)} fusion(bf16[1408,384]{1,0:T(8,128)(2,1)S(1)} %bitcast.109, bf16[1408,512]{1,0:T(8,128)(2,1)} %bitcast.113, f32[1408]{0:T(1024)S(1)} %reshape.784, f32[512]{0:T(512)S(1)} %add_rsqrt_fusion.1), kind=kOutput, calls=%fused_computation.8 | convolution fusion | flops 556728320 | bytes 2924032 | tf_op jit(solution)/shard_map/dot_general | solution.py:32
  94.1 2.7 %collective-permute-start = (bf16[184,512]{1,0:T(8,128)(2,1)S(1)}, bf16[184,512]{1,0:T(8,128)(2,1)S(1)}, u32[]{:S(2)}, u32[]{:S(2)}) collective-permute-start(bf16[184,512]{1,0:T(8,128)(2,1)S(1)} %fusion.34), channel_id=1, source_target_pairs={{0,1},{1,0},{2,3},{3,2},{4,5},{5,4},{6,7},{7,6},{8,9},{9,8},{10,11... | collective-permute-start | bytes 565256 | tf_op jit(solution)/shard_map/ppermute | solution.py:476
  96.9 4.0 %collective-permute-done = bf16[184,512]{1,0:T(8,128)(2,1)S(1)} collective-permute-done((bf16[184,512]{1,0:T(8,128)(2,1)S(1)}, bf16[184,512]{1,0:T(8,128)(2,1)S(1)}, u32[]{:S(2)}, u32[]{:S(2)}) %collective-permute-start) | collective-permute-done | bytes 188448 | tf_op jit(solution)/shard_map/ppermute | solution.py:476
  101.7 2.5 %all-to-all-done.3 = bf16[8,128,176]{1,2,0:T(8,128)(2,1)} async-done(((bf16[8,128,176]{1,2,0:T(8,128)(2,1)}), bf16[8,128,176]{1,2,0:T(8,128)(2,1)}, u32[]{:S(2)}, u32[]{:S(2)}) %all-to-all-start.3) | async-done | bytes 360480 | tf_op jit(solution)/shard_map/all_to_all | solution.py:22
  104.2 1.2 copy.42
  105.8 2.6 %vision_attention.1 = bf16[16,88,128]{2,1,0:T(8,128)(2,1)} custom-call(s32[8]{0:T(128)S(1)} %select_reduce_fusion.6.ends_ref, bf16[128,176]{1,0:T(8,128)(2,1)S(1)} %pad.14.q_ref, bf16[1024,176]{1,0:T(8,128)(2,1)S(1)} %bitcast.105, s32[1,128]{1,0:T(1,128)S(1)} %broadcast_in_dim_tile.3.marks_ref), custom_call_target="tpu_custom_call" | custom-call | tf_op jit(solution)/shard_map/vision_attention/pallas_call | solution.py:320
  108.4 6.5 %all-to-all-start.4 = ((bf16[16,88,128]{2,1,0:T(8,128)(2,1)}), bf16[16,88,128]{2,1,0:T(8,128)(2,1)S(1)}, u32[]{:S(2)}, u32[]{:S(2)}) async-start(bf16[16,88,128]{2,1,0:T(8,128)(2,1)} %vision_attention.1), calls=%async_computation.4 | async-start | bytes 720896 | tf_op jit(solution)/shard_map/all_to_all | solution.py:28
  115.2 8.0 %all-to-all-done.4 = bf16[16,88,128]{2,1,0:T(8,128)(2,1)S(1)} async-done(((bf16[16,88,128]{2,1,0:T(8,128)(2,1)}), bf16[16,88,128]{2,1,0:T(8,128)(2,1)S(1)}, u32[]{:S(2)}, u32[]{:S(2)}) %all-to-all-start.4) | async-done | bytes 360480 | tf_op jit(solution)/shard_map/all_to_all | solution.py:28
  124.5 3.9 %all-to-all-start.5 = ((bf16[16,88,128]{2,1,0:T(8,128)(2,1)}), bf16[16,88,128]{2,1,0:T(8,128)(2,1)S(1)}, u32[]{:S(2)}, u32[]{:S(2)}) async-start(bf16[16,88,128]{2,1,0:T(8,128)(2,1)} %broadcast_in_dim.237), calls=%async_computation.5 | async-start | bytes 720896 | tf_op jit(solution)/shard_map/all_to_all | solution.py:22
  128.4 8.4 %all-to-all-done.5 = bf16[16,88,128]{2,1,0:T(8,128)(2,1)S(1)} async-done(((bf16[16,88,128]{2,1,0:T(8,128)(2,1)}), bf16[16,88,128]{2,1,0:T(8,128)(2,1)S(1)}, u32[]{:S(2)}, u32[]{:S(2)}) %all-to-all-start.5) | async-done | bytes 360480 | tf_op jit(solution)/shard_map/all_to_all | solution.py:22
  138.0 4.0 %all-to-all-start.6 = ((bf16[16,32,88]{2,1,0:T(8,128)(2,1)}), bf16[16,32,88]{2,1,0:T(8,128)(2,1)S(1)}, u32[]{:S(2)}, u32[]{:S(2)}) async-start(bf16[16,32,88]{2,1,0:T(8,128)(2,1)} %broadcast_in_dim.238), calls=%async_computation.6 | async-start | bytes 262144 | tf_op jit(solution)/shard_map/all_to_all | solution.py:22
  142.0 6.1 %all-to-all-done.6 = bf16[16,32,88]{2,1,0:T(8,128)(2,1)S(1)} async-done(((bf16[16,32,88]{2,1,0:T(8,128)(2,1)}), bf16[16,32,88]{2,1,0:T(8,128)(2,1)S(1)}, u32[]{:S(2)}, u32[]{:S(2)}) %all-to-all-start.6) | async-done | bytes 90144 | tf_op jit(solution)/shard_map/all_to_all | solution.py:22
  150.0 5.9 %all-to-all-start.7 = ((bf16[16,32,362]{2,1,0:T(8,128)(2,1)}), bf16[16,32,362]{2,1,0:T(8,128)(2,1)S(1)}, u32[]{:S(2)}, u32[]{:S(2)}) async-start(bf16[16,32,362]{2,1,0:T(8,128)(2,1)} %broadcast_in_dim.240), calls=%async_computation.7 | async-start | bytes 786432 | tf_op jit(solution)/shard_map/all_to_all | solution.py:22
  156.2 1.8 copy-done
  158.1 2.1 %text_attention.1 = (f32[88,512]{1,0:T(8,128)S(1)}, f32[8,512]{1,0:T(8,128)S(1)}) custom-call(s32[3]{0:T(128)S(1)} %pad_add_fusion.2.bounds_ref, bf16[96,512]{1,0:T(8,128)(2,1)S(1)} %maximum_maximum_fusion.q_ref.text_q_ref, bf16[8,2,184,512]{3,2,1,0:T(8,128)(2,1)S(1)} %bitcast.103, s32[3,512]{1,0:T(4,128)S(1)} %pad_add_fusion.qpos_ref), custom_call_target="tpu_custom_call" | custom-call | flops 1476395008 | bytes 3014656 | tf_op jit(solution)/shard_map/text_attention/pallas_call | solution.py:209
  160.9 9.7 %all-to-all-done.7 = bf16[16,32,362]{2,1,0:T(8,128)(2,1)S(1)} async-done(((bf16[16,32,362]{2,1,0:T(8,128)(2,1)}), bf16[16,32,362]{2,1,0:T(8,128)(2,1)S(1)}, u32[]{:S(2)}, u32[]{:S(2)}) %all-to-all-start.7) | async-done | bytes 370720 | tf_op jit(solution)/shard_map/all_to_all | solution.py:22
  170.5 0.9 copy-done.3
  171.4 0.9 copy-done.5
  172.4 1.9 image_attention.1
  174.4 26.1 %all_to_all.45 = bf16[16,88,512]{2,1,0:T(8,128)(2,1)S(1)} all-to-all(bf16[16,88,512]{2,1,0:T(8,128)(2,1)S(1)} %broadcast_in_dim.243), channel_id=1, replica_groups=mesh['row'=16,'col'=8,'grp'=2] {'row'}, dimensions={0} | all-to-all | bytes 2883584 | tf_op jit(solution)/shard_map/all_to_all | solution.py:22
  200.5 2.2 %fusion.12 = bf16[1,512,88]{1,2,0:T(8,128)(2,1)} fusion(bf16[1408,512]{1,0:T(8,128)(2,1)S(1)} %bitcast.114, bf16[1408,384]{1,0:T(8,128)(2,1)} %bitcast.124, bf16[88,512]{1,0:T(8,128)(2,1)S(1)} %get-tuple-element.53), kind=kOutput, calls=%fused_computation.13 | convolution fusion | flops 127012864 | bytes 1982464 | tf_op jit(solution)/shard_map/dot_general | solution.py:32
  (113 shorter events, 17.8 us)
Async XLA Ops:
  6.5 21.6 %copy-start.2 = (bf16[1,512,88]{1,2,0:T(8,128)(2,1)S(1)}, bf16[1,512,88]{1,2,0:T(8,128)(2,1)}, u32[]{:S(2)}) copy-start(bf16[1,512,88]{1,2,0:T(8,128)(2,1)} %param.25) | copy-start | bytes 270340
  6.5 53.9 %all-gather.5.cloned.1.call-start = ((), (), s32[]{:S(2)}) async-start(), calls=%async_computation.9 | async-start | bytes 3649536 | tf_op jit(solution)/shard_map/all_gather | solution.py:370
  8.7 19.3 %all-to-all-start.1 = ((bf16[8,16,176]{2,1,0:T(8,128)(2,1)}), bf16[8,16,176]{2,1,0:T(8,128)(2,1)S(1)}, u32[]{:S(2)}, u32[]{:S(2)}) async-start(bf16[8,16,176]{2,1,0:T(8,128)(2,1)} %get-tuple-element.32), calls=%async_computation.1 | async-start | bytes 131072 | tf_op jit(solution)/shard_map/all_to_all | solution.py:28
  29.6 7.1 %copy-start.8 = (bf16[264]{0:T(512)(128)(2,1)S(1)}, bf16[264]{0:T(512)(128)(2,1)}, u32[]{:S(2)}) copy-start(bf16[264]{0:T(512)(128)(2,1)} %param.20) | copy-start | bytes 1588
  29.6 30.5 %all-to-all-start.2 = ((bf16[16,112,512]{2,1,0:T(8,128)(2,1)}), bf16[16,112,512]{2,1,0:T(8,128)(2,1)S(1)}, u32[]{:S(2)}, u32[]{:S(2)}) async-start(bf16[16,112,512]{2,1,0:T(8,128)(2,1)} %broadcast_in_dim.132), calls=%async_computation.2 | async-start | bytes 3670016 | tf_op jit(solution)/shard_map/all_to_all | solution.py:22
  62.8 21.2 %all-to-all-start = ((bf16[16,88,384]{2,1,0:T(8,128)(2,1)}), bf16[16,88,384]{2,1,0:T(8,128)(2,1)S(1)}, u32[]{:S(2)}, u32[]{:S(2)}) async-start(bf16[16,88,384]{2,1,0:T(8,128)(2,1)} %bitcast.116), calls=%async_computation | async-start | bytes 2162688 | tf_op jit(solution)/shard_map/all_to_all | solution.py:28
  68.2 2.9 %copy-start.6 = (bf16[16,88,512]{2,1,0:T(8,128)(2,1)}, bf16[16,88,512]{2,1,0:T(8,128)(2,1)S(1)}, u32[]{:S(2)}) copy-start(bf16[16,88,512]{2,1,0:T(8,128)(2,1)S(1)} %slice.134) | copy-start | bytes 4325380
  70.5 1.0 copy-start.7
  84.8 19.4 %all-to-all-start.3 = ((bf16[8,128,176]{1,2,0:T(8,128)(2,1)}), bf16[8,128,176]{1,2,0:T(8,128)(2,1)}, u32[]{:S(2)}, u32[]{:S(2)}) async-start(bf16[8,128,176]{1,2,0:T(8,128)(2,1)} %broadcast_in_dim.236), calls=%async_computation.3 | async-start | bytes 720896 | tf_op jit(solution)/shard_map/all_to_all | solution.py:22
  91.7 57.0 %all-gather.7.cloned.1.call-start = ((), (), s32[]{:S(2)}) async-start(), calls=%async_computation.10 | async-start | bytes 3391488 | tf_op jit(solution)/shard_map/all_gather | solution.py:479
  94.1 6.8 %collective-permute-start = (bf16[184,512]{1,0:T(8,128)(2,1)S(1)}, bf16[184,512]{1,0:T(8,128)(2,1)S(1)}, u32[]{:S(2)}, u32[]{:S(2)}) collective-permute-start(bf16[184,512]{1,0:T(8,128)(2,1)S(1)} %fusion.34), channel_id=1, source_target_pairs={{0,1},{1,0},{2,3},{3,2},{4,5},{5,4},{6,7},{7,6},{8,9},{9,8},{10,11... | collective-permute-start | bytes 565256 | tf_op jit(solution)/shard_map/ppermute | solution.py:476
  108.4 14.8 %all-to-all-start.4 = ((bf16[16,88,128]{2,1,0:T(8,128)(2,1)}), bf16[16,88,128]{2,1,0:T(8,128)(2,1)S(1)}, u32[]{:S(2)}, u32[]{:S(2)}) async-start(bf16[16,88,128]{2,1,0:T(8,128)(2,1)} %vision_attention.1), calls=%async_computation.4 | async-start | bytes 720896 | tf_op jit(solution)/shard_map/all_to_all | solution.py:28
  114.9 13.5 %copy-start.9 = (bf16[88]{0:T(256)(128)(2,1)S(1)}, bf16[88]{0:T(256)(128)(2,1)}, u32[]{:S(2)}) copy-start(bf16[88]{0:T(256)(128)(2,1)} %param.24) | copy-start | bytes 532
  124.5 12.3 %all-to-all-start.5 = ((bf16[16,88,128]{2,1,0:T(8,128)(2,1)}), bf16[16,88,128]{2,1,0:T(8,128)(2,1)S(1)}, u32[]{:S(2)}, u32[]{:S(2)}) async-start(bf16[16,88,128]{2,1,0:T(8,128)(2,1)} %broadcast_in_dim.237), calls=%async_computation.5 | async-start | bytes 720896 | tf_op jit(solution)/shard_map/all_to_all | solution.py:22
  138.0 10.2 %all-to-all-start.6 = ((bf16[16,32,88]{2,1,0:T(8,128)(2,1)}), bf16[16,32,88]{2,1,0:T(8,128)(2,1)S(1)}, u32[]{:S(2)}, u32[]{:S(2)}) async-start(bf16[16,32,88]{2,1,0:T(8,128)(2,1)} %broadcast_in_dim.238), calls=%async_computation.6 | async-start | bytes 262144 | tf_op jit(solution)/shard_map/all_to_all | solution.py:22
  150.0 20.5 %all-to-all-start.7 = ((bf16[16,32,362]{2,1,0:T(8,128)(2,1)}), bf16[16,32,362]{2,1,0:T(8,128)(2,1)S(1)}, u32[]{:S(2)}, u32[]{:S(2)}) async-start(bf16[16,32,362]{2,1,0:T(8,128)(2,1)} %broadcast_in_dim.240), calls=%async_computation.7 | async-start | bytes 786432 | tf_op jit(solution)/shard_map/all_to_all | solution.py:22
  156.2 1.9 copy-start
  158.1 12.5 %copy-start.1 = (bf16[16,184,512]{2,1,0:T(8,128)(2,1)S(1)}, bf16[16,184,512]{2,1,0:T(8,128)(2,1)}, u32[]{:S(2)}) copy-start(bf16[16,184,512]{2,1,0:T(8,128)(2,1)} %all-gather.7.cloned.1.call-done) | copy-start | bytes 9043972
  160.2 0.7 copy-start.4
  170.5 0.9 copy-start.3
  171.4 0.9 copy-start.5
Sparse Core Ops, SparseCore 0:
  9.1 49.6 all-gather.4
  105.5 41.7 all-gather.6
